TPU v7x, 256 devices: a whole 4x4x8 slice. The times are simulated.
256 devices in a mesh: dp: 64 (over z, y, core), mp: 4 (over x).
Axes of the slice: x: 4, y: 4, z: 8, core: 2. Of those that a mesh axis runs over, the one named last changes fastest.
Arguments:
- noise_blocks: bfloat16 [512, 12800], P('dp'), may hold values from -6 to 6
- data_blocks: bfloat16 [512, 12800], P('dp'), may hold values from -6 to 6
- destination: int32 [512], replicated, may hold values from 0 to 511, as said below
- utt_blocks: int32 [64, 4], P('dp'), may hold values from 1 to 4, 8 in all within a row
- span_start: int32 [64, 4], P('dp'), may hold values from 0 to 19
- span_size: int32 [64, 4], P('dp'), may hold values from 44 to 64
- timestep: int32 [64, 4], P('dp'), may hold values from 1 to 63
- in_weight: bfloat16 [200, 1024], replicated, may hold values from -0.4375 to 0.4375
- norm_gain: bfloat16 [1024], replicated, may hold values from 0.5 to 1.5
- qkv_weight: bfloat16 [1024, 3, 512], P(None, None, 'mp'), may hold values from -4 to 4
- out_proj: bfloat16 [512, 1024], P('mp'), may hold values from -0.25 to 0.25
- final_gain: bfloat16 [1024], replicated, may hold values from 0.25 to 1.75
- vel_weight: bfloat16 [1024, 100], replicated, may hold values from -0.1875 to 0.1875
Outputs:
- grad_qkv: float32 [1024, 3, 512], P('dp', None, 'mp')
- grad_out: float32 [512, 1024], P('mp', 'dp')
Inputs may be any that keep to these rules, and one draw needn't show every extreme that they name: `destination`: A permutation of the 512 bin positions; a device sends to each bin either none or exactly 1 of its blocks.
All inputs are finite; a program needn't handle non-finite values.
Results may differ from a plain program's by a relative error of at most 0.004.
Values may be sent and summed in bfloat16 or wider, within the bound.
No kernel may reach another device: no remote copies, remote signals or barrier semaphores. Data moves between devices by JAX's collectives and lax.ppermute only.
A program may use at most 64 MiB of HBM per device.

v0:
```python
import jax
import jax.numpy as jnp
from jax import lax
from jax.sharding import PartitionSpec as P

HEAD_DIM = 64
BLOCK = 128


def sent_together(arrays, axis, split_dim, concat_dim, along):
    widths = [a.shape[along] for a in arrays]
    both = jnp.concatenate(arrays, axis=along)
    out = lax.all_to_all(both, axis, split_axis=split_dim, concat_axis=concat_dim, tiled=True)
    return tuple(jnp.split(out, [sum(widths[:k]) for k in range(1, len(widths))], axis=along))


def sent_together_2(arrays, axis, dim, along):
    both = jnp.concatenate(arrays, axis=along)
    out, at, finished = (lax.all_gather(both, axis, axis=dim, tiled=True), 0, [])
    for a in arrays:
        finished.append(lax.slice_in_dim(out, at, at + a.shape[along], axis=along))
        at += a.shape[along]
    return tuple(finished)


def sent_to_all(shard, axis):
    length = lax.axis_size(axis)
    return lax.all_to_all(
        jnp.broadcast_to(shard[None], (length, *shard.shape)), axis, 0, 0, tiled=True
    )


def of_everyone(shard, axis):
    return sent_to_all(shard, axis).sum(axis=0)


def split_up(shard, dim, length):
    dims = shard.shape
    tiles = shard.reshape(*dims[:dim], length, dims[dim] // length, *dims[dim + 1 :])
    return jnp.moveaxis(tiles, dim, 0)


def sent_and_summed(shard, axis, dim):
    length = lax.axis_size(axis)
    tiles = lax.all_to_all(split_up(shard, dim, length), axis, 0, 0, tiled=True)
    return jnp.sum(tiles, axis=0)


def frame_table(lengths, starts, sizes, steps, rows):
    ends = jnp.cumsum(lengths)
    frame = jnp.arange(rows, dtype=jnp.int32)
    block_index = frame // BLOCK
    segment = jnp.sum((block_index[:, None] >= ends[None, :]).astype(jnp.int32), axis=1)
    member = segment[:, None] == jnp.arange(lengths.shape[0], dtype=jnp.int32)[None, :]
    first = jnp.sum(jnp.where(member, (ends - lengths)[None, :], 0), axis=1) * BLOCK
    span = jnp.sum(jnp.where(member, lengths[None, :], 0), axis=1) * BLOCK
    lower = jnp.sum(jnp.where(member, starts[None, :], 0), axis=1)
    upper = lower + jnp.sum(jnp.where(member, sizes[None, :], 0), axis=1)
    inside = 64 * (frame - first)
    masked = ((inside >= lower * span) & (inside < upper * span)).astype(jnp.float32)
    level = jnp.sum(jnp.where(member, steps[None, :], 0), axis=1).astype(jnp.float32) / 64.0
    return (segment, masked, level)


def attend(query, keys, values, segment):
    rows, width = query.shape
    heads = width // HEAD_DIM
    block = min(512, rows)
    reach = min(4, rows // BLOCK // 2) * BLOCK
    window = min(rows, block + 2 * reach)
    blocks = rows // block
    query_blocks = query.reshape(blocks, block, heads, HEAD_DIM)
    segment_blocks = segment.reshape(blocks, block)
    firsts = jnp.clip(jnp.arange(blocks, dtype=jnp.int32) * block - reach, 0, rows - window)
    keyed = keys.reshape(rows, heads, HEAD_DIM)
    valued = values.reshape(rows, heads, HEAD_DIM)

    def one_block(item):
        query_block, segment_block, first = item
        scores = jnp.einsum(
            "qhd,khd->hqk", query_block, keyed, preferred_element_type=jnp.float32
        ) * HEAD_DIM ** (-0.5)
        scores = jnp.where((segment_block[:, None] == segment[None, :])[None], scores, -1e30)
        top = jnp.max(scores, axis=-1, keepdims=True)
        weights = jnp.exp(scores - top)
        probs = (weights / jnp.sum(weights, axis=-1, keepdims=True)).astype(jnp.bfloat16)
        return jnp.einsum(
            "hqk,khd->qhd", probs, valued, preferred_element_type=jnp.float32
        ).reshape(block, width)

    return lax.map(jax.checkpoint(one_block), (query_blocks, segment_blocks, firsts)).reshape(
        rows, width
    )


def shards(
    noise_blocks,
    data_blocks,
    destination,
    utt_blocks,
    span_start,
    span_size,
    timestep,
    in_weight,
    norm_gain,
    qkv_weight,
    out_proj,
    final_gain,
    vel_weight,
):
    sources = lax.axis_size("dp")
    here = lax.axis_index("dp")
    per_dev = noise_blocks.shape[0]
    depth = max(1, per_dev // sources)
    lanes_total = sources * depth
    table = destination.reshape(sources, per_dev)
    owner = table // per_dev
    order = jnp.arange(per_dev, dtype=jnp.int32)
    earlier = (owner[:, :, None] == owner[:, None, :]) & (
        order[None, None, :] < order[None, :, None]
    )
    rank = jnp.sum(earlier.astype(jnp.int32), axis=2)
    code = jnp.arange(sources, dtype=jnp.int32)[:, None] * depth + rank
    mine_owner = lax.dynamic_index_in_dim(owner, here, 0, keepdims=False)
    mine_rank = lax.dynamic_index_in_dim(rank, here, 0, keepdims=False)
    lanes = jnp.arange(lanes_total, dtype=jnp.int32)
    packing = (lanes[:, None] == (mine_owner * depth + mine_rank)[None, :]).astype(jnp.bfloat16)
    wanted = here * per_dev + order
    hit = table[None, :, :] == wanted[:, None, None]
    source_code = jnp.sum(jnp.where(hit, code[None, :, :], 0), axis=(1, 2))
    unpacking = (source_code[:, None] == lanes[None, :]).astype(jnp.bfloat16)

    def outgoing(blocks):
        sent = jnp.dot(packing, blocks, preferred_element_type=jnp.float32).astype(jnp.bfloat16)
        return sent.reshape(sources, depth, blocks.shape[1])

    def incoming(arrived):
        flat = arrived.reshape(lanes_total, arrived.shape[2])
        return jnp.dot(unpacking, flat, preferred_element_type=jnp.float32).astype(jnp.bfloat16)

    share = noise_blocks.shape[1] // lax.axis_size("mp")
    offset = lax.axis_index("mp") * share
    noise_share = lax.dynamic_slice_in_dim(noise_blocks, offset, share, 1)
    data_share = lax.dynamic_slice_in_dim(data_blocks, offset, share, 1)
    got_noise, got_data = sent_together(
        (outgoing(noise_share), outgoing(data_share)), "dp", 0, 0, 1
    )
    bin_noise, bin_data = sent_together_2((incoming(got_noise), incoming(got_data)), "mp", 1, 0)
    rows = per_dev * BLOCK
    mel = noise_blocks.shape[1] // BLOCK
    noise = bin_noise.reshape(rows, mel).astype(jnp.float32)
    data = bin_data.reshape(rows, mel).astype(jnp.float32)
    segment, masked, level = frame_table(
        utt_blocks[0], span_start[0], span_size[0], timestep[0], rows
    )
    noisy = (1.0 - level[:, None]) * noise + level[:, None] * data
    cond = data * (1.0 - masked[:, None])
    target = data - noise
    inputs = jnp.concatenate([noisy, cond], axis=1).astype(jnp.bfloat16)
    hidden0 = jnp.dot(inputs, in_weight, preferred_element_type=jnp.float32)
    scale = lax.rsqrt(jnp.mean(hidden0 * hidden0, axis=1, keepdims=True) + 1e-06)
    normed = (hidden0 * scale * norm_gain.astype(jnp.float32)[None, :]).astype(jnp.bfloat16)
    query = jnp.dot(normed, qkv_weight[:, 0, :], preferred_element_type=jnp.float32).astype(
        jnp.bfloat16
    )
    keys = jnp.dot(normed, qkv_weight[:, 1, :], preferred_element_type=jnp.float32).astype(
        jnp.bfloat16
    )
    values = jnp.dot(normed, qkv_weight[:, 2, :], preferred_element_type=jnp.float32).astype(
        jnp.bfloat16
    )
    heads_out, pullback = jax.vjp(lambda a, b, c: attend(a, b, c, segment), query, keys, values)
    attended = heads_out.astype(jnp.bfloat16)
    partial_mix = jnp.dot(attended, out_proj, preferred_element_type=jnp.float32)
    mixed = lax.psum(partial_mix.astype(jnp.bfloat16), "mp").astype(jnp.float32)
    hidden1 = (hidden0 + mixed).astype(jnp.bfloat16)
    wide1 = lax.optimization_barrier(hidden1).astype(jnp.float32)
    rscale = lax.rsqrt(jnp.mean(wide1 * wide1, axis=1, keepdims=True) + 1e-06)
    normalized = wide1 * rscale
    gain_out = final_gain.astype(jnp.float32)[None, :]
    final = (normalized * gain_out).astype(jnp.bfloat16)
    velocity = jnp.dot(final, vel_weight, preferred_element_type=jnp.float32)
    count = of_everyone(jnp.sum(masked), "dp")
    error = (2.0 * masked[:, None] * (velocity - target)).astype(jnp.bfloat16)
    grad_final = jnp.dot(error, vel_weight.T, preferred_element_type=jnp.float32)
    scaled = grad_final * gain_out
    back1 = (
        rscale * (scaled - normalized * jnp.mean(scaled * normalized, axis=1, keepdims=True))
    ).astype(jnp.bfloat16)
    back_att = jnp.dot(back1, out_proj.T, preferred_element_type=jnp.float32).astype(jnp.bfloat16)
    dquery, dkeys, dvalues = pullback(back_att.astype(jnp.float32))
    out_terms = jnp.dot(attended.T, back1, preferred_element_type=jnp.float32)
    qkv_terms = jnp.stack(
        [
            jnp.dot(normed.T, dquery, preferred_element_type=jnp.float32),
            jnp.dot(normed.T, dkeys, preferred_element_type=jnp.float32),
            jnp.dot(normed.T, dvalues, preferred_element_type=jnp.float32),
        ],
        axis=1,
    )
    summed_qkv, summed_out = (
        sent_and_summed(qkv_terms, "dp", 0),
        sent_and_summed(out_terms, "dp", 1),
    )
    return (summed_qkv / count, summed_out / count)


def solution(mesh):
    in_specs = (
        P("dp", None),
        P("dp", None),
        P(),
        P("dp", None),
        P("dp", None),
        P("dp", None),
        P("dp", None),
        P(),
        P(),
        P(None, None, "mp"),
        P("mp", None),
        P(),
        P(),
    )
    out_specs = (P("dp", None, "mp"), P("mp", "dp"))
    return jax.shard_map(shards, mesh=mesh, in_specs=in_specs, out_specs=out_specs, check_vma=False)
```

profile of v0, /device:TPU:8, one launch (start us, length us, event | category | flops | bytes accessed | tf_op | source)
XLA Modules:
  0.0 277.2 jit_solution(8119586240358613834)
XLA Ops:
  12.4 12.1 %all-to-all-start = ((bf16[64,2,3200]{2,1,0:T(2,128)(2,1)}), bf16[64,2,3200]{2,1,0:T(2,128)(2,1)S(1)}, u32[]{:S(2)}, u32[]{:S(2)}) async-start(bf16[64,2,3200]{2,1,0:T(2,128)(2,1)} %copy.118), calls=%async_computation | async-start | bytes 1638400 | tf_op jit(solution)/shard_map/all_to_all | solution.py:13
  26.6 21.7 %all-to-all-done = bf16[64,2,3200]{2,1,0:T(2,128)(2,1)S(1)} async-done(((bf16[64,2,3200]{2,1,0:T(2,128)(2,1)}), bf16[64,2,3200]{2,1,0:T(2,128)(2,1)S(1)}, u32[]{:S(2)}, u32[]{:S(2)}) %all-to-all-start) | async-done | bytes 819232 | tf_op jit(solution)/shard_map/all_to_all | solution.py:13
  50.0 13.1 %all_gather.3 = bf16[16,12800]{1,0:T(8,128)(2,1)S(1)} all-gather(bf16[16,3200]{1,0:T(8,128)(2,1)S(1)} %pad_maximum_fusion.2), channel_id=1, replica_groups=mesh['dp'=64,'mp'=4] {'mp'}, dimensions={1}, use_global_device_ids=true | all-gather | bytes 512000 | tf_op jit(solution)/shard_map/all_gather | solution.py:19
  71.6 16.2 %while.30 = (s32[]{:T(128)}, bf16[2,512,128]{2,1,0:T(8,128)(2,1)S(1)}, s32[2,512]{1,0:T(2,128)S(1)}, s32[1,1024]{1,0:T(1,128)S(1)}, bf16[2,512,2,64]{1,3,2,0:T(8...) while((s32[]{:T(128)}, ...), condition=%wide.region_13.14_spmd, body=%wide.region_10.13_spmd.sunk | while | flops 275252224 | bytes 10766441 | solution.py:91
  72.0 4.5 %fusion.178 = (f32[2,512]{1,0:T(2,128)S(1)}, f32[2,512,1024]{2,1,0:T(8,128)}) fusion(pred[512,1024]{1,0:T(8,128)(4,1)S(1)} %broadcast_compare_fusion.4, bf16[1024,2,64]{0,2,1:T(8,128)(2,1)S(1)} %get-tuple-element.655, bf16[2,512,2,64]{1,3,2,0:T(8,128)(2,1)} %get-tuple-element.654, s32[]{:T(128)S(6)} %copy.175), kind=kOutput, calls=%fused_computation.183.clone.1 | convolution fusion | flops 138413056 | bytes 5115908 | tf_op jit(solution)/shard_map/jvp()/while/body/eval_jaxpr/sub | solution.py:85
  76.5 3.0 %fusion.179 = bf16[2,512,64]{1,2,0:T(8,128)(2,1)S(1)} fusion(bf16[1024,2,64]{0,2,1:T(8,128)(2,1)S(1)} %get-tuple-element.656, f32[2,512,1024]{2,1,0:T(8,128)} %get-tuple-element.608, f32[2,512]{1,0:T(2,128)S(1)} %get-tuple-element.609), kind=kOutput, calls=%fused_computation.8.clone.1 | convolution fusion | flops 136314880 | bytes 4591616 | tf_op jit(solution)/shard_map/jvp()/while/body/eval_jaxpr/hqk,khd->qhd/dot_general | solution.py:87
  80.1 4.5 %fusion.178 = (f32[2,512]{1,0:T(2,128)S(1)}, f32[2,512,1024]{2,1,0:T(8,128)}) fusion(pred[512,1024]{1,0:T(8,128)(4,1)S(1)} %broadcast_compare_fusion.4, bf16[1024,2,64]{0,2,1:T(8,128)(2,1)S(1)} %get-tuple-element.655, bf16[2,512,2,64]{1,3,2,0:T(8,128)(2,1)} %get-tuple-element.654, s32[]{:T(128)S(6)} %copy.175), kind=kOutput, calls=%fused_computation.183.clone.1 | convolution fusion | flops 138413056 | bytes 5115908 | tf_op jit(solution)/shard_map/jvp()/while/body/eval_jaxpr/sub | solution.py:85
  84.6 3.0 %fusion.179 = bf16[2,512,64]{1,2,0:T(8,128)(2,1)S(1)} fusion(bf16[1024,2,64]{0,2,1:T(8,128)(2,1)S(1)} %get-tuple-element.656, f32[2,512,1024]{2,1,0:T(8,128)} %get-tuple-element.608, f32[2,512]{1,0:T(2,128)S(1)} %get-tuple-element.609), kind=kOutput, calls=%fused_computation.8.clone.1 | convolution fusion | flops 136314880 | bytes 4591616 | tf_op jit(solution)/shard_map/jvp()/while/body/eval_jaxpr/hqk,khd->qhd/dot_general | solution.py:87
  87.8 2.1 convolution_convert_fusion.5
  91.3 6.4 %all-to-all-start.2 = ((f32[64,1,1]{2,1,0:T(1,128)}), f32[64,1,1]{2,1,0:T(1,128)}, u32[]{:S(2)}, u32[]{:S(2)}) async-start(f32[64,1,1]{2,1,0:T(1,128)} %broadcast_in_dim.203), calls=%async_computation.2 | async-start | bytes 65536 | tf_op jit(solution)/shard_map/all_to_all | solution.py:28
  100.3 49.7 %all-reduce.2.cloned.1.call-done = bf16[1024,1024]{0,1:T(8,128)(2,1)} async-done(((bf16[1024,1024]{0,1:T(8,128)(2,1)}), bf16[1024,1024]{0,1:T(8,128)(2,1)}) %all-reduce.2.cloned.1.call-update) | async-done | bytes 2097168 | tf_op jit(solution)/shard_map/psum | solution.py:175
  150.0 3.6 %add_convert_fusion = bf16[1024,1024]{0,1:T(8,128)(2,1)S(1)} fusion(f32[1024,1024]{0,1:T(8,128)} %copy-done.1, bf16[1024,1024]{0,1:T(8,128)(2,1)} %all-reduce.2.cloned.1.call-done), kind=kLoop, calls=%fused_computation.86 | loop fusion | flops 3145728 | bytes 8388608 | tf_op jit(solution)/shard_map/convert_element_type | solution.py:176
  154.2 4.4 %fusion.64 = (f32[1024]{0:T(1024)S(1)}, f32[1024,1024]{0,1:T(8,128)}) fusion(bf16[1024,1024]{0,1:T(8,128)(2,1)S(1)} %add_convert_fusion, f32[1024]{0:T(1024)S(1)} %copy-done.19, f32[1024]{0:T(1024)S(1)} %add_rsqrt_fusion, bf16[1024,100]{0,1:T(8,128)(2,1)} %param.29, f32[1024,100]{0,1:T(8,128)S(1)} %copy-done.10, f32[1024,100]{0,1:T(8,128)S(1)} %copy-done.9, ...), kind=kOutput, calls=%fused_computation.81 | convolution fusion | flops 429276160 | bytes 7331840 | tf_op jit(solution)/shard_map/dot_general | solution.py:185
  158.6 3.2 %fusion.67 = bf16[1024,1024]{0,1:T(8,128)(2,1)S(1)} fusion(bf16[1024,1024]{0,1:T(8,128)(2,1)S(1)} %add_convert_fusion, f32[1024,1024]{0,1:T(8,128)} %get-tuple-element.497, f32[1024]{0:T(1024)S(1)} %broadcast_multiply_fusion, f32[1024]{0:T(1024)S(1)} %copy-done.19, f32[1024]{0:T(1024)S(1)} %add_rsqrt_fusion), kind=kLoop, calls=%fused_computation.84 | loop fusion | flops 7340032 | bytes 8400896 | tf_op jit(solution)/shard_map/convert_element_type | solution.py:189
  161.8 2.3 fusion.75
  166.0 10.8 %all-to-all-start.3 = ((f32[64,128,16]{1,2,0:T(8,128)}), f32[64,128,16]{1,2,0:T(8,128)}, u32[]{:S(2)}, u32[]{:S(2)}) async-start(f32[64,128,16]{1,2,0:T(8,128)} %copy.136), calls=%async_computation.3 | async-start | bytes 1048576 | tf_op jit(solution)/shard_map/all_to_all | solution.py:45
  177.5 33.6 %while.31 = (s32[]{:T(128)}, bf16[1024,2,64]{0,2,1:T(8,128)(2,1)}, bf16[1024,2,64]{0,2,1:T(8,128)(2,1)}, bf16[2,512,2,64]{1,3,2,0:T(8,128)(2,1)}, bf16[2,512,2,6...) while((s32[]{:T(128)}, bf16[1024,2,64]{0,2,1:T(8,128)(2,1)}, ...), condition=%wide.region_23.24_spmd.clone, body=%wide.region_17.23_spmd.clone.sunk | while | flops 712179712 | bytes 56854912 | solution.py:91
  181.0 2.1 fusion.187
  185.8 2.8 convert_reduce_fusion.5
  188.6 1.9 fusion.189
  197.8 2.1 fusion.187
  202.5 2.8 convert_reduce_fusion.5
  218.7 10.3 %all-to-all-start.1 = ((f32[64,16,3,128]{3,1,2,0:T(8,128)}), f32[64,16,3,128]{3,1,2,0:T(8,128)S(1)}, u32[]{:S(2)}, u32[]{:S(2)}) async-start(f32[64,16,3,128]{3,1,2,0:T(8,128)} %copy.133), calls=%async_computation.1 | async-start | bytes 3145728 | tf_op jit(solution)/shard_map/all_to_all | solution.py:45
  232.7 36.3 %all-to-all-done.1 = f32[64,16,3,128]{3,1,2,0:T(8,128)S(1)} async-done(((f32[64,16,3,128]{3,1,2,0:T(8,128)}), f32[64,16,3,128]{3,1,2,0:T(8,128)S(1)}, u32[]{:S(2)}, u32[]{:S(2)}) %all-to-all-start.1) | async-done | bytes 1572896 | tf_op jit(solution)/shard_map/all_to_all | solution.py:45
  (181 shorter events, 59.5 us)
Async XLA Ops:
  7.2 58.4 %copy-start = (bf16[200,1024]{1,0:T(8,128)(2,1)S(1)}, bf16[200,1024]{1,0:T(8,128)(2,1)}, u32[]{:S(2)}) copy-start(bf16[200,1024]{1,0:T(8,128)(2,1)} %param.24) | copy-start | bytes 1228804
  7.2 17.4 %copy-start.24 = (s32[1,4]{1,0:T(1,128)S(1)}, s32[1,4]{1,0:T(1,128)}, u32[]{:S(2)}) copy-start(s32[1,4]{1,0:T(1,128)} %param.20) | copy-start | bytes 52
  7.2 17.6 %copy-start.21 = (bf16[1024]{0:T(1024)(128)(2,1)S(1)}, bf16[1024]{0:T(1024)(128)(2,1)}, u32[]{:S(2)}) copy-start(bf16[1024]{0:T(1024)(128)(2,1)} %param.25) | copy-start | bytes 6148
  7.2 18.0 %copy-start.23 = (s32[1,4]{1,0:T(1,128)S(1)}, s32[1,4]{1,0:T(1,128)}, u32[]{:S(2)}) copy-start(s32[1,4]{1,0:T(1,128)} %param.23) | copy-start | bytes 52
  7.2 18.0 %copy-start.25 = (s32[1,4]{1,0:T(1,128)S(1)}, s32[1,4]{1,0:T(1,128)}, u32[]{:S(2)}) copy-start(s32[1,4]{1,0:T(1,128)} %param.22) | copy-start | bytes 52
  7.2 18.0 %copy-start.26 = (s32[1,4]{1,0:T(1,128)S(1)}, s32[1,4]{1,0:T(1,128)}, u32[]{:S(2)}) copy-start(s32[1,4]{1,0:T(1,128)} %param.21) | copy-start | bytes 52
  12.4 36.0 %all-to-all-start = ((bf16[64,2,3200]{2,1,0:T(2,128)(2,1)}), bf16[64,2,3200]{2,1,0:T(2,128)(2,1)S(1)}, u32[]{:S(2)}, u32[]{:S(2)}) async-start(bf16[64,2,3200]{2,1,0:T(2,128)(2,1)} %copy.118), calls=%async_computation | async-start | bytes 1638400 | tf_op jit(solution)/shard_map/all_to_all | solution.py:13
  24.5 125.5 %all-reduce.2.cloned.1.call-start = ((), (), s32[]{:S(2)}) async-start(), calls=%async_computation.4 | async-start | bytes 4194304 | tf_op jit(solution)/shard_map/psum | solution.py:175
  71.6 16.2 %copy-start.4 = (bf16[128,1024]{1,0:T(8,128)(2,1)S(1)}, bf16[128,1024]{1,0:T(8,128)(2,1)}, u32[]{:S(2)}) copy-start(bf16[128,1024]{1,0:T(8,128)(2,1)} %param.27) | copy-start | bytes 786436
  87.8 12.5 %copy-start.8 = (s32[1,1024]{1,0:T(1,128)}, s32[1,1024]{1,0:T(1,128)S(1)}, u32[]{:S(2)}) copy-start(s32[1,1024]{1,0:T(1,128)S(1)} %get-tuple-element.700) | copy-start | bytes 12292
  87.8 12.5 %copy-start.11 = (bf16[2,512,128]{2,1,0:T(8,128)(2,1)}, bf16[2,512,128]{2,1,0:T(8,128)(2,1)S(1)}, u32[]{:S(2)}) copy-start(bf16[2,512,128]{2,1,0:T(8,128)(2,1)S(1)} %get-tuple-element.271) | copy-start | bytes 786436
  87.8 12.5 %copy-start.18 = (s32[2,512]{1,0:T(2,128)}, s32[2,512]{1,0:T(2,128)S(1)}, u32[]{:S(2)}) copy-start(s32[2,512]{1,0:T(2,128)S(1)} %get-tuple-element.701) | copy-start | bytes 12292
  87.8 12.5 %copy-start.28 = (bf16[1024,2,64]{0,2,1:T(8,128)(2,1)}, bf16[1024,2,64]{0,2,1:T(8,128)(2,1)S(1)}, u32[]{:S(2)}) copy-start(bf16[1024,2,64]{0,2,1:T(8,128)(2,1)S(1)} %get-tuple-element.702) | copy-start | bytes 786436
  87.8 12.4 %copy-start.30 = (bf16[1024,2,64]{0,2,1:T(8,128)(2,1)}, bf16[1024,2,64]{0,2,1:T(8,128)(2,1)S(1)}, u32[]{:S(2)}) copy-start(bf16[1024,2,64]{0,2,1:T(8,128)(2,1)S(1)} %get-tuple-element.703) | copy-start | bytes 786436
  87.8 9.9 %copy-start.22 = (bf16[1024]{0:T(1024)(128)(2,1)S(1)}, bf16[1024]{0:T(1024)(128)(2,1)}, u32[]{:S(2)}) copy-start(bf16[1024]{0:T(1024)(128)(2,1)} %param.28) | copy-start | bytes 6148
  91.3 74.7 %all-to-all-start.2 = ((f32[64,1,1]{2,1,0:T(1,128)}), f32[64,1,1]{2,1,0:T(1,128)}, u32[]{:S(2)}, u32[]{:S(2)}) async-start(f32[64,1,1]{2,1,0:T(1,128)} %broadcast_in_dim.203), calls=%async_computation.2 | async-start | bytes 65536 | tf_op jit(solution)/shard_map/all_to_all | solution.py:28
  100.3 53.9 %copy-start.9 = (f32[1024,100]{0,1:T(8,128)S(1)}, f32[1024,100]{0,1:T(8,128)}, u32[]{:S(2)}) copy-start(f32[1024,100]{0,1:T(8,128)} %copy.126) | copy-start | bytes 1228804
  100.3 53.9 %copy-start.10 = (f32[1024,100]{0,1:T(8,128)S(1)}, f32[1024,100]{0,1:T(8,128)}, u32[]{:S(2)}) copy-start(f32[1024,100]{0,1:T(8,128)} %copy.125) | copy-start | bytes 1228804
  100.3 53.9 %copy-start.19 = (f32[1024]{0:T(1024)S(1)}, f32[1024]{0:T(1024)}, u32[]{:S(2)}) copy-start(f32[1024]{0:T(1024)} %convert_element_type.206) | copy-start | bytes 12292
  100.3 53.9 %copy-start.20 = (f32[1024]{0:T(1024)S(1)}, f32[1024]{0:T(1024)}, u32[]{:S(2)}) copy-start(f32[1024]{0:T(1024)} %get-tuple-element.492) | copy-start | bytes 12292
  158.6 5.5 %copy-start.5 = (bf16[128,1024]{1,0:T(8,128)(2,1)S(1)}, bf16[128,1024]{1,0:T(8,128)(2,1)}, u32[]{:S(2)}) copy-start(bf16[128,1024]{1,0:T(8,128)(2,1)} %param.27) | copy-start | bytes 786436
  166.0 52.7 %all-to-all-start.3 = ((f32[64,128,16]{1,2,0:T(8,128)}), f32[64,128,16]{1,2,0:T(8,128)}, u32[]{:S(2)}, u32[]{:S(2)}) async-start(f32[64,128,16]{1,2,0:T(8,128)} %copy.136), calls=%async_computation.3 | async-start | bytes 1048576 | tf_op jit(solution)/shard_map/all_to_all | solution.py:45
  177.5 35.7 %copy-start.3 = (bf16[1024,1024]{0,1:T(8,128)(2,1)S(1)}, bf16[1024,1024]{0,1:T(8,128)(2,1)}, u32[]{:S(2)}) copy-start(bf16[1024,1024]{0,1:T(8,128)(2,1)} %copy-done.2) | copy-start | bytes 6291460
  218.7 50.3 %all-to-all-start.1 = ((f32[64,16,3,128]{3,1,2,0:T(8,128)}), f32[64,16,3,128]{3,1,2,0:T(8,128)S(1)}, u32[]{:S(2)}, u32[]{:S(2)}) async-start(f32[64,16,3,128]{3,1,2,0:T(8,128)} %copy.133), calls=%async_computation.1 | async-start | bytes 3145728 | tf_op jit(solution)/shard_map/all_to_all | solution.py:45
  (21 other events, 41.5 us)
Sparse Core Ops, SparseCore 0:
  90.1 59.8 all-reduce.1
where the time goes:
time: 278 us; the launch traced here: 277 us
  waiting for transfers between devices  108 us (39%)
  matrix products  52.6 us (19%)
  starting transfers between devices  39.6 us (14%)
  other arithmetic  25.4 us (9%)
  local copies, waits for them, and re-layouts  23.7 us (9%)
  between operations  14.6 us (5%)
  blocking collectives  13.1 us (5%)
    psum x1, waiting for transfers between devices, shards(): mixed = lax.psum(partial_mix.astype(jnp.bfloat16), 'mp').astype(jnp.float32)  49.7 us
    all_to_all x2, waiting for transfers between devices, sent_and_summed(): tiles = lax.all_to_all(split_up(shard, dim, length), axis, 0, 0, tiled=True)  36.3 us
    all_to_all x1, waiting for transfers between devices, sent_together(): lax.all_to_all(both, axis, split_axis=split_dim, concat_axis=concat_dim,...  21.7 us
    all_to_all x2, starting transfers between devices, sent_and_summed(): tiles = lax.all_to_all(split_up(shard, dim, length), axis, 0, 0, tiled=True)  21.1 us
    dot_general x6, matrix products, one_block(): jnp.einsum('hqk,khd->qhd', probs, valued, preferred_element_type=jnp.floa...  14.5 us
    all_gather x1, blocking collectives, sent_together_2(): lax.all_gather(both, axis, axis=dim, tiled=True)  13.1 us
    all_to_all x1, starting transfers between devices, sent_together(): lax.all_to_all(both, axis, split_axis=split_dim, concat_axis=concat_dim,...  12.1 us
    dot_general x6, matrix products, one_block(): jnp.einsum('qhd,khd->hqk', query_block, keyed, preferred_element_type=jnp...  10.2 us
  transfers between devices with their start and end apart: 5, of which 3 were waited for; matrix products, arithmetic and copies ran while one was open for 24% of the time, Pallas kernels for 0%

commit v1 on v0

v1 whole, which is shorter than its diff:
```python
import jax
import jax.numpy as jnp
from jax import lax
from jax.experimental import pallas as pl
from jax.experimental.pallas import tpu as pltpu
from jax.sharding import Mesh, PartitionSpec as P

F32, BF16 = jnp.float32, jnp.bfloat16
HEAD = 64
BLOCK = 128
MEL = 100
SLOT = 56
EPS = 1e-06
VMEM, SMEM = pltpu.VMEM, pltpu.SMEM
NT = (((1,), (1,)), ((), ()))


def vm():
    return pl.BlockSpec(memory_space=VMEM)


def sm():
    return pl.BlockSpec(memory_space=SMEM)


def params():
    return pltpu.CompilerParams(vmem_limit_bytes=48 << 20)


def dot(a, b, dims=None):
    if dims is None:
        return jnp.dot(a, b, preferred_element_type=F32)
    return lax.dot_general(a, b, dims, preferred_element_type=F32)


def pack_kernel(core, bins, own, other, out):
    c = core[0]
    for half, ref in ((0, own), (1, other)):
        out[:, half, 48:SLOT, :] = jnp.broadcast_to(ref[0, 48:SLOT, :][None], (out.shape[0], SLOT - 48, 128))
    for half, ref in ((0, own), (1, other)):
        for i in range(8):
            b = bins[half * 8 + i]

            @pl.when((b & 1) == c)
            def _():
                out[b >> 1, half] = ref[i]


def unpack_kernel(source, arrived, out, sems):
    copies = [
        pltpu.make_async_copy(arrived.at[source[j]], out.at[j], sems.at[j]) for j in range(8)
    ]
    for copy in copies:
        copy.start()
    for copy in copies:
        copy.wait()


def utterances(utt, start, size):
    first, rows = jnp.int32(0), []
    for u in range(4):
        blocks = utt[0, u]
        lo = first * BLOCK + 2 * blocks * start[0, u]
        end = (first + blocks) * BLOCK
        hi = jnp.minimum(first * BLOCK + 2 * blocks * (start[0, u] + size[0, u]), end)
        rows.append((first * BLOCK, end, lo, hi))
        first = first + blocks
    return rows


def masked_of(frame, spans):
    hit = None
    for _, _, lo, hi in spans:
        one = (frame >= lo) & (frame < hi)
        hit = one if hit is None else hit | one
    return hit


def each_utterance(utt, body):
    def step(u, first):
        blocks = utt[0, u]
        for length in range(1, 5):

            @pl.when(blocks == length)
            def _():
                body(pl.multiple_of(first * BLOCK, BLOCK), length * BLOCK)

        return first + blocks

    lax.fori_loop(0, 4, step, jnp.int32(0))


def head_mask(rows, h):
    lane = lax.broadcasted_iota(jnp.int32, (rows, 2 * HEAD), 1)
    return (lane < HEAD) if h == 0 else (lane >= HEAD)


def front_kernel(
    place, utt, start, size, level, x0, x1, x2, x3, w, gain, wqkv,
    att, inp, tgt, q, k, v, stat, vt, attt,
):
    spans = utterances(utt, start, size)
    for step, x in enumerate((x0, x1, x2, x3)):
        part = lax.rem(place[0] + step, 4)
        row = lax.broadcasted_iota(jnp.int32, (256, 128), 0)
        frame = (row >> 5) * BLOCK + part * 32 + (row & 31)
        lev = jnp.zeros((256, 128), F32)
        for u, (begin, end, _, _) in enumerate(spans):
            inside = (frame >= begin) & (frame < end)
            lev = jnp.where(inside, level[0, u].astype(F32) / 64.0, lev)
        noise, data = x[:, :128].astype(F32), x[:, 128:].astype(F32)
        noisy = (1.0 - lev) * noise + lev * data
        cond = jnp.where(masked_of(frame, spans), 0.0, data)
        both = jnp.concatenate([noisy, cond], axis=1).astype(BF16)
        diff = data - noise
        for b in range(8):
            at = pl.ds(pl.multiple_of(b * BLOCK + part * 32, 32), 32)
            inp[at, :] = both[b * 32 : b * 32 + 32]
            tgt[at, :] = diff[b * 32 : b * 32 + 32]

    def project(i, carry):
        rows = pl.ds(pl.multiple_of(i * 256, 256), 256)
        h = dot(inp[rows, :], w[...])
        scale = lax.rsqrt(jnp.mean(h * h, axis=1, keepdims=True) + EPS)
        normed = (h * scale * gain[...]).astype(BF16)
        out = dot(normed, wqkv[...])
        q[rows, :] = (out[:, :128].astype(BF16).astype(F32) * HEAD ** (-0.5)).astype(BF16)
        k[rows, :] = out[:, 128:256].astype(BF16)
        v[rows, :] = out[:, 256:].astype(BF16)
        return carry

    lax.fori_loop(0, 4, project, 0)
    vt[...] = v[...].T

    def one(first, rows):
        at = pl.ds(first, rows)
        for h in range(2):
            keys = jnp.where(head_mask(rows, h), k[at, :], jnp.zeros((), BF16))
            scores = dot(keys, q[at, :], NT)
            top = jnp.max(scores, axis=0, keepdims=True)
            weights = jnp.exp(scores - top)
            inv = 1.0 / jnp.sum(weights, axis=0, keepdims=True)
            probs = (weights * inv).astype(BF16)
            attt[h * HEAD : (h + 1) * HEAD, at] = dot(vt[h * HEAD : (h + 1) * HEAD, at], probs).astype(BF16)
            stat[h : h + 1, at] = top
            stat[h + 2 : h + 3, at] = inv

    each_utterance(utt, one)
    att[...] = attt[...].T


def back_kernel(
    place, utt, start, size, a0, a1, a2, a3, proj, inp, tgt, w, gain, fgain, vel, q, k, v, stat,
    keep, send, normed, back1, dout, kt, dqt, dk, dv, lhs,
):
    spans = utterances(utt, start, size)

    def project(i, carry):
        rows = pl.ds(pl.multiple_of(i * 256, 256), 256)
        h = dot(inp[rows, :], w[...])
        scale = lax.rsqrt(jnp.mean(h * h, axis=1, keepdims=True) + EPS)
        normed[rows, :] = (h * scale * gain[...]).astype(BF16)
        groups = jnp.concatenate([a0[rows, :], a1[rows, :], a2[rows, :], a3[rows, :]], axis=1)
        wide = (h + dot(groups, proj[...])).astype(BF16).astype(F32)
        rscale = lax.rsqrt(jnp.mean(wide * wide, axis=1, keepdims=True) + EPS)
        normalized = wide * rscale
        final = (normalized * fgain[...]).astype(BF16)
        velocity = dot(final, vel[...])
        frame = i * 256 + lax.broadcasted_iota(jnp.int32, (256, 128), 0)
        error = jnp.where(masked_of(frame, spans), 2.0 * (velocity - tgt[rows, :]), 0.0).astype(BF16)
        scaled = dot(error, vel[...], NT) * fgain[...]
        middle = jnp.mean(scaled * normalized, axis=1, keepdims=True)
        b1 = (rscale * (scaled - normalized * middle)).astype(BF16)
        back1[rows, :] = b1
        dout[rows, :] = dot(b1, proj[0:128, :], NT).astype(BF16)
        return carry

    lax.fori_loop(0, 4, project, 0)
    kt[...] = k[...].T

    def one(first, rows):
        at = pl.ds(first, rows)
        qs, ks, vs, ds = q[at, :], k[at, :], v[at, :], dout[at, :]
        dks, dvs = [], []
        for h in range(2):
            mask = head_mask(rows, h)
            zero = jnp.zeros((), BF16)
            scores = dot(jnp.where(mask, ks, zero), qs, NT)
            p = jnp.exp(scores - stat[h : h + 1, at]) * stat[h + 2 : h + 3, at]
            dp = dot(jnp.where(mask, vs, zero), ds, NT).astype(BF16).astype(F32)
            inner = jnp.sum(p * dp, axis=0, keepdims=True)
            dscore = (p * (dp - inner)).astype(BF16)
            dvs.append(dot(p.astype(BF16), ds))
            dks.append(dot(dscore, qs))
            span = slice(h * HEAD, (h + 1) * HEAD)
            dqt[span, at] = (dot(kt[span, at], dscore) * HEAD ** (-0.5)).astype(BF16)
        mask = head_mask(rows, 0)
        dk[at, :] = jnp.where(mask, dks[0], dks[1]).astype(BF16)
        dv[at, :] = jnp.where(mask, dvs[0], dvs[1]).astype(BF16)

    each_utterance(utt, one)
    lhs[0:128, :] = dqt[...]
    lhs[128:256, :] = dk[...].T
    lhs[256:384, :] = dv[...].T
    lhs[384:512, :] = a0[...].T
    mine = place[1] == 0
    for j in range(4):
        cols = slice(j * 256, (j + 1) * 256)
        top = dot(lhs[0:384, :], normed[:, cols])
        low = dot(lhs[384:512, :], back1[:, cols])
        terms = jnp.concatenate([top.T, low.T], axis=1).reshape(8, 2, 16, 512)
        even, odd = terms[:, 0], terms[:, 1]
        keep[j * 8 : j * 8 + 8] = jnp.where(mine, even, odd)
        send[j * 8 : j * 8 + 8] = jnp.where(mine, odd, even)


def shards(
    noise_blocks, data_blocks, destination, utt_blocks, span_start, span_size, timestep,
    in_weight, norm_gain, qkv_weight, out_proj, final_gain, vel_weight,
):
    z, y, c, x = (lax.axis_index(n) for n in ("z", "y", "c", "mp"))
    here = (z * 4 + y) * 2 + c
    share = noise_blocks.shape[1] // 4
    swap = [(0, 1), (1, 0)]

    def turned(a, by):
        return lax.ppermute(a, "mp", [(i, (i - by) % 4) for i in range(4)])

    bin_count = jnp.sum(2 * utt_blocks * (jnp.minimum(span_start + span_size, 64) - span_start))
    lane = lax.broadcasted_iota(jnp.int32, (8, SLOT - 50, 128), 2)
    tail = jnp.where(lane == 0, bin_count // 32, jnp.where(lane == 1, bin_count % 32, 0)).astype(BF16)
    mine = [
        lax.dynamic_slice_in_dim(a, x * share, share, 1).reshape(8, 25, 128)
        for a in (noise_blocks, data_blocks)
    ]
    own = jnp.concatenate([*mine, tail], axis=1)
    other = lax.ppermute(own, "c", swap)
    bins = destination // 8
    nearby = jnp.concatenate(
        [lax.dynamic_slice_in_dim(bins, here * 8, 8), lax.dynamic_slice_in_dim(bins, (here ^ 1) * 8, 8)]
    )
    packed = pl.pallas_call(
        pack_kernel,
        out_shape=jax.ShapeDtypeStruct((32, 2, SLOT, 128), BF16),
        in_specs=[sm(), sm(), vm(), vm()],
        out_specs=vm(),
        compiler_params=params(),
        name="pack",
    )(c[None], nearby, own, other)
    arrived = lax.all_to_all(packed, ("z", "y"), 0, 0, tiled=True).reshape(64, SLOT, 128)
    wanted = here * 8 + jnp.arange(8, dtype=jnp.int32)
    row = jnp.sum(
        jnp.where(destination[None, :] == wanted[:, None], jnp.arange(512, dtype=jnp.int32)[None, :], 0), axis=1
    )
    source = (row >> 4) * 2 + (((row >> 3) & 1) ^ c)
    blocks = pl.pallas_call(
        unpack_kernel,
        out_shape=jax.ShapeDtypeStruct((8, SLOT, 128), BF16),
        in_specs=[sm(), pl.BlockSpec(memory_space=pl.ANY)],
        out_specs=vm(),
        scratch_shapes=[pltpu.SemaphoreType.DMA((8,))],
        compiler_params=params(),
        name="unpack",
    )(source, arrived)
    counts = jnp.sum(arrived[:, 50, 0:2].astype(F32), axis=0)
    count = counts[0] * 32.0 + counts[1]
    frames = blocks[:, 0:50].reshape(8, 2, 32, MEL).transpose(0, 2, 1, 3)
    frames = jnp.pad(frames, ((0, 0), (0, 0), (0, 0), (0, 128 - MEL))).reshape(256, 256)
    pieces = [frames] + [turned(frames, by) for by in (1, 2, 3)]

    w = jnp.concatenate(
        [jnp.pad(in_weight[:MEL], ((0, 28), (0, 0))), jnp.pad(in_weight[MEL:], ((0, 28), (0, 0)))], axis=0
    )
    gain = norm_gain.astype(F32)[None, :]
    fgain = final_gain.astype(F32)[None, :]
    wqkv = qkv_weight.reshape(1024, 384)
    vel = jnp.pad(vel_weight, ((0, 0), (0, 28)))
    proj = jnp.concatenate([out_proj] + [turned(out_proj, by) for by in (1, 2, 3)], axis=0)
    place = jnp.stack([x, c])
    tables = (place, utt_blocks, span_start, span_size)

    half = jax.ShapeDtypeStruct((1024, 128), BF16)
    att, inp, tgt, q, k, v, stat = pl.pallas_call(
        front_kernel,
        out_shape=(
            half, jax.ShapeDtypeStruct((1024, 256), BF16), jax.ShapeDtypeStruct((1024, 128), F32),
            half, half, half, jax.ShapeDtypeStruct((8, 1024), F32),
        ),
        in_specs=[sm()] * 5 + [vm()] * 7,
        out_specs=(vm(),) * 7,
        scratch_shapes=[VMEM((128, 1024), BF16), VMEM((128, 1024), BF16)],
        compiler_params=params(),
        name="front",
    )(*tables, timestep, *pieces, w, gain, wqkv)
    heads = [att] + [turned(att, by) for by in (1, 2, 3)]
    terms = jax.ShapeDtypeStruct((32, 16, 512), F32)
    keep, send = pl.pallas_call(
        back_kernel,
        out_shape=(terms, terms),
        in_specs=[sm()] * 4 + [vm()] * 15,
        out_specs=(vm(), vm()),
        scratch_shapes=[
            VMEM((1024, 1024), BF16), VMEM((1024, 1024), BF16), VMEM((1024, 128), BF16),
            VMEM((128, 1024), BF16), VMEM((128, 1024), BF16), VMEM((1024, 128), BF16),
            VMEM((1024, 128), BF16), VMEM((512, 1024), BF16),
        ],
        compiler_params=params(),
        name="back",
    )(*tables, *heads, proj, inp, tgt, w, gain, fgain, vel, q, k, v, stat)
    pair = (keep + lax.ppermute(send, "c", swap)).astype(BF16)
    parts = lax.all_to_all(pair, ("z", "y"), 0, 0, tiled=True)
    total = jnp.sum(parts.astype(F32), axis=0) / count
    return (total[:, :384].reshape(16, 3, 128), total[:, 384:].T)


def solution(mesh):
    dp = ("z", "y", "c")
    fine = Mesh(mesh.devices.reshape(8, 4, 2, 4), dp + ("mp",))
    row = P(dp, None)
    in_specs = (
        row, row, P(), row, row, row, row, P(), P(), P(None, None, "mp"), P("mp", None), P(), P(),
    )
    out_specs = (P(dp, None, "mp"), P("mp", dp))
    return jax.shard_map(shards, mesh=fine, in_specs=in_specs, out_specs=out_specs, check_vma=False)
```

time: 278 us -> 131 us (0.47)
  waiting for transfers between devices: 108 us -> 45.9 us
  matrix products: 52.6 us -> 0 us
  Pallas kernels: 0 us -> 24.6 us
  other arithmetic: 25.4 us -> 8.24 us
  blocking collectives: 13.1 us -> 0 us
  local copies, waits for them, and re-layouts: 23.7 us -> 13.3 us
  between operations: 14.6 us -> 4.97 us
  starting transfers between devices: 39.6 us -> 32.5 us
    psum x1 -> x0, waiting for transfers between devices: 49.7 us -> none  [shards(): mixed = lax.psum(partial_mix.astype(jnp.bfloat16), 'mp').astype(jnp.float32)]
    dot_general x27 -> x0, matrix products: 43.5 us -> none  [the longest x6 14.5 us: one_block(): jnp.einsum('hqk,khd->qhd', probs, valued, preferred_element_type=jnp.floa...]
    pallas_call x0 -> x4, Pallas kernels: none -> 24.6 us  [the longest x1 13.8 us: shards(): pl.pallas_call(back_kernel, out_shape=(terms, terms), in_specs=[sm()] * 4...]
    all_to_all x4 -> x2, waiting for transfers between devices: 58 us -> 35.4 us  [the longest x1 20.2 us: shards(): lax.all_to_all(packed, ('z', 'y'), 0, 0, tiled=True).reshape(64, SLOT, 128)]
    all_to_all x4 -> x2, starting transfers between devices: 39.5 us -> 17.7 us  [the longest x1 11.8 us: shards(): lax.all_to_all(packed, ('z', 'y'), 0, 0, tiled=True).reshape(64, SLOT, 128)]
    ppermute x0 -> x11, starting transfers between devices: none -> 14.8 us  [the longest x9 14.6 us: turned(): return lax.ppermute(a, 'mp', [(i, (i - by) % 4) for i in range(4)])]
    all_gather x1 -> x0, blocking collectives: 13.1 us -> none  [sent_together_2(): lax.all_gather(both, axis, axis=dim, tiled=True)]
    ppermute x0 -> x11, waiting for transfers between devices: none -> 10.5 us  [the longest x9 7.44 us: turned(): return lax.ppermute(a, 'mp', [(i, (i - by) % 4) for i in range(4)])]
  transfers between devices with their start and end apart: 5 -> 13, of which waited for: 3 -> 8; matrix products, arithmetic and copies ran while one was open for 24% -> 8% of each run, Pallas kernels for 0% -> 7%
where the time goes in v1:
time: 131 us; the launch traced here: 130 us
  waiting for transfers between devices  45.9 us (35%)
  starting transfers between devices  32.5 us (25%)
  Pallas kernels  24.6 us (19%)
  local copies, waits for them, and re-layouts  13.3 us (10%)
  other arithmetic  8.24 us (6%)
  between operations  4.97 us (4%)
    all_to_all x1, waiting for transfers between devices, shards(): lax.all_to_all(packed, ('z', 'y'), 0, 0, tiled=True).reshape(64, SLOT, 128)  20.2 us
    all_to_all x1, waiting for transfers between devices, shards(): parts = lax.all_to_all(pair, ('z', 'y'), 0, 0, tiled=True)  15.2 us
    ppermute x9, starting transfers between devices, turned(): return lax.ppermute(a, 'mp', [(i, (i - by) % 4) for i in range(4)])  14.6 us
    pallas_call x1, Pallas kernels, shards(): pl.pallas_call(back_kernel, out_shape=(terms, terms), in_specs=[sm()] * 4...  13.8 us
    all_to_all x1, starting transfers between devices, shards(): lax.all_to_all(packed, ('z', 'y'), 0, 0, tiled=True).reshape(64, SLOT, 128)  11.8 us
    unnamed x55, local copies, waits for them, and re-layouts  9.31 us
    pallas_call x1, Pallas kernels, shards(): pl.pallas_call(front_kernel, out_shape=(half, jax.ShapeDtypeStruct((1024,...  8.47 us
    ppermute x9, waiting for transfers between devices, turned(): return lax.ppermute(a, 'mp', [(i, (i - by) % 4) for i in range(4)])  7.44 us
  transfers between devices with their start and end apart: 13, of which 8 were waited for; matrix products, arithmetic and copies ran while one was open for 8% of the time, Pallas kernels for 7%

profile of v1, /device:TPU:8, one launch (start us, length us, event | category | flops | bytes accessed | tf_op | source)
XLA Modules:
  0.0 129.5 jit_solution(12214552164791610077)
XLA Ops:
  0.6 1.3 %multiply_reduce_fusion = s32[]{:T(128)} fusion(s32[1,4]{1,0:T(1,128)} %start.3, s32[1,4]{1,0:T(1,128)} %size.3, s32[1,4]{1,0:T(1,128)} %utt.3), kind=kLoop, calls=%fused_computation.29 | loop fusion | flops 23 | bytes 52 | tf_op jit(solution)/shard_map/reduce_sum | solution.py:229
  7.0 1.6 %pack.1 = bf16[32,2,56,128]{3,2,1,0:T(8,128)(2,1)} custom-call(s32[1]{0:T(128)} %bitcast.1.core, s32[16]{0:T(128)S(1)} %pad_add_fusion.1.bins, bf16[8,56,128]{2,1,0:T(8,128)(2,1)S(1)} %pad_maximum_fusion.1.own, bf16[8,56,128]{2,1,0:T(8,128)(2,1)S(1)} %collective-permute-done.other), custom_call_target="tpu_custom_call" | custom-call | tf_op jit(solution)/shard_map/pack/pallas_call | solution.py:242
  8.6 11.8 %all-to-all-start = ((bf16[32,2,56,128]{3,2,1,0:T(8,128)(2,1)}), bf16[32,2,56,128]{3,2,1,0:T(8,128)(2,1)S(1)}, u32[]{:S(2)}, u32[]{:S(2)}) async-start(bf16[32,2,56,128]{3,2,1,0:T(8,128)(2,1)} %pack.1), calls=%async_computation | async-start | bytes 1835008 | tf_op jit(solution)/shard_map/all_to_all | solution.py:250
  20.5 3.1 %collective-permute-start.8 = (bf16[128,1024]{1,0:T(8,128)(2,1)}, bf16[128,1024]{1,0:T(8,128)(2,1)}, u32[]{:S(2)}, u32[]{:S(2)}) collective-permute-start(bf16[128,1024]{1,0:T(8,128)(2,1)} %param.23), channel_id=1, source_target_pairs={{0,2},{1,3},{2,0},{3,1},{4,6},{5,7},{6,4},{7,5},{8,10},{9,11},{10,... | collective-permute-start | bytes 786440 | tf_op jit(solution)/shard_map/ppermute | solution.py:227
  23.6 1.1 collective-permute-start.7
  25.8 20.2 %all-to-all-done = bf16[32,2,56,128]{3,2,1,0:T(8,128)(2,1)S(1)} async-done(((bf16[32,2,56,128]{3,2,1,0:T(8,128)(2,1)}), bf16[32,2,56,128]{3,2,1,0:T(8,128)(2,1)S(1)}, u32[]{:S(2)}, u32[]{:S(2)}) %all-to-all-start) | async-done | bytes 917536 | tf_op jit(solution)/shard_map/all_to_all | solution.py:250
  47.6 1.6 %collective-permute-start.3 = (bf16[256,256]{1,0:T(8,128)(2,1)S(1)}, bf16[256,256]{1,0:T(8,128)(2,1)S(1)}, u32[]{:S(2)}, u32[]{:S(2)}) collective-permute-start(bf16[256,256]{1,0:T(8,128)(2,1)S(1)} %bitcast.27), channel_id=1, source_target_pairs={{0,1},{1,2},{2,3},{3,0},{4,5},{5,6},{6,7},{7,4},{8,9},{9,10},{10,1... | collective-permute-start | bytes 393224 | tf_op jit(solution)/shard_map/ppermute | solution.py:227
  50.0 2.7 %collective-permute-start.2 = (bf16[256,256]{1,0:T(8,128)(2,1)S(1)}, bf16[256,256]{1,0:T(8,128)(2,1)S(1)}, u32[]{:S(2)}, u32[]{:S(2)}) collective-permute-start(bf16[256,256]{1,0:T(8,128)(2,1)S(1)} %bitcast.28), channel_id=1, source_target_pairs={{0,2},{1,3},{2,0},{3,1},{4,6},{5,7},{6,4},{7,5},{8,10},{9,11},{10,... | collective-permute-start | bytes 393224 | tf_op jit(solution)/shard_map/ppermute | solution.py:227
  52.7 2.2 %collective-permute-done.3.x3 = bf16[256,256]{1,0:T(8,128)(2,1)S(1)} collective-permute-done((bf16[256,256]{1,0:T(8,128)(2,1)S(1)}, bf16[256,256]{1,0:T(8,128)(2,1)S(1)}, u32[]{:S(2)}, u32[]{:S(2)}) %collective-permute-start.3) | collective-permute-done | bytes 131104 | tf_op jit(solution)/shard_map/ppermute | solution.py:227
  57.6 1.1 fusion.1.w
  60.6 0.9 copy-done.7
  61.5 0.9 copy-done.9
  63.7 8.5 %front.1 = (bf16[1024,128]{1,0:T(8,128)(2,1)}, bf16[1024,256]{1,0:T(8,128)(2,1)S(1)}, f32[1024,128]{1,0:T(8,128)S(1)}, bf16[1024,128]{1,0:T(8,128)(2,1)S(1)}, bf...) custom-call(s32[2]{0:T(128)S(1)} %copy-done.16, s32[1,4]{1,0:T(1,128)S(1)} %copy-done.12, ...), custom_call_target="tpu_custom_call" | custom-call | tf_op jit(solution)/shard_map/front/pallas_call | solution.py:283
  75.8 2.3 %collective-permute-start.5 = (bf16[1024,128]{1,0:T(8,128)(2,1)}, bf16[1024,128]{1,0:T(8,128)(2,1)S(1)}, u32[]{:S(2)}, u32[]{:S(2)}) collective-permute-start(bf16[1024,128]{1,0:T(8,128)(2,1)} %get-tuple-element.11.a0), channel_id=1, source_target_pairs={{0,2},{1,3},{2,0},{3,1},{4,6},{5,7},{6,4},{7,5},{8,10},{9,11},{10,... | collective-permute-start | bytes 786440 | tf_op jit(solution)/shard_map/ppermute | solution.py:227
  78.1 1.3 %collective-permute-start.4 = (bf16[1024,128]{1,0:T(8,128)(2,1)}, bf16[1024,128]{1,0:T(8,128)(2,1)S(1)}, u32[]{:S(2)}, u32[]{:S(2)}) collective-permute-start(bf16[1024,128]{1,0:T(8,128)(2,1)} %get-tuple-element.11.a0), channel_id=1, source_target_pairs={{0,3},{1,0},{2,1},{3,2},{4,7},{5,4},{6,5},{7,6},{8,11},{9,8},{10,9... | collective-permute-start | bytes 786440 | tf_op jit(solution)/shard_map/ppermute | solution.py:227
  79.5 1.1 copy.30
  80.7 2.3 %pad_maximum_fusion.proj = bf16[512,1024]{1,0:T(8,128)(2,1)} fusion(bf16[128,1024]{1,0:T(8,128)(2,1)} %collective-permute-done.9, bf16[128,1024]{1,0:T(8,128)(2,1)} %collective-permute-done.8, bf16[128,1024]{1,0:T(8,128)(2,1)} %collective-permute-done.7, bf16[128,1024]{1,0:T(8,128)(2,1)} %param.23), kind=kLoop, calls=%fused_computation.1 | loop fusion | flops 4194304 | bytes 2097152 | tf_op jit(solution)/shard_map/concatenate | solution.py:278
  83.0 1.8 %collective-permute-done.6.a3 = bf16[1024,128]{1,0:T(8,128)(2,1)S(1)} collective-permute-done((bf16[1024,128]{1,0:T(8,128)(2,1)}, bf16[1024,128]{1,0:T(8,128)(2,1)S(1)}, u32[]{:S(2)}, u32[]{:S(2)}) %collective-permute-start.6) | collective-permute-done | bytes 262176 | tf_op jit(solution)/shard_map/ppermute | solution.py:227
  84.8 2.8 %collective-permute-done.5.a2 = bf16[1024,128]{1,0:T(8,128)(2,1)S(1)} collective-permute-done((bf16[1024,128]{1,0:T(8,128)(2,1)}, bf16[1024,128]{1,0:T(8,128)(2,1)S(1)}, u32[]{:S(2)}, u32[]{:S(2)}) %collective-permute-start.5) | collective-permute-done | bytes 262176 | tf_op jit(solution)/shard_map/ppermute | solution.py:227
  87.7 13.8 %back.1 = (f32[32,16,512]{2,1,0:T(8,128)S(1)}, f32[32,16,512]{2,1,0:T(8,128)S(1)}) custom-call(s32[2]{0:T(128)S(1)} %copy-done.17, s32[1,4]{1,0:T(1,128)S(1)} %copy-done.12, s32[1,4]{1,0:T(1,128)S(1)} %copy-done.13, s32[1,4]{1,0:T(1,128)S(1)} %copy-done.15, bf16[1024,128]{1,0:T(8,128)(2,1)} %get-tuple-element.11.a0, ...), custom_call_target="tpu_custom_call" | custom-call | tf_op jit(solution)/shard_map/back/pallas_call | solution.py:297
  101.6 2.6 %collective-permute-done.10 = f32[32,16,512]{2,1,0:T(8,128)S(1)} collective-permute-done((f32[32,16,512]{2,1,0:T(8,128)S(1)}, f32[32,16,512]{2,1,0:T(8,128)S(1)}, u32[]{:S(2)}, u32[]{:S(2)}) %collective-permute-start.10) | collective-permute-done | bytes 1048608 | tf_op jit(solution)/shard_map/ppermute | solution.py:310
  104.2 1.0 add_convert_fusion
  105.2 5.9 %all-to-all-start.1 = ((bf16[32,16,512]{2,1,0:T(8,128)(2,1)}), bf16[32,16,512]{2,1,0:T(8,128)(2,1)S(1)}, u32[]{:S(2)}, u32[]{:S(2)}) async-start(bf16[32,16,512]{2,1,0:T(8,128)(2,1)} %add_convert_fusion), calls=%async_computation.1 | async-start | bytes 1048576 | tf_op jit(solution)/shard_map/all_to_all | solution.py:311
  113.0 15.2 %all-to-all-done.1 = bf16[32,16,512]{2,1,0:T(8,128)(2,1)S(1)} async-done(((bf16[32,16,512]{2,1,0:T(8,128)(2,1)}), bf16[32,16,512]{2,1,0:T(8,128)(2,1)S(1)}, u32[]{:S(2)}, u32[]{:S(2)}) %all-to-all-start.1) | async-done | bytes 524320 | tf_op jit(solution)/shard_map/all_to_all | solution.py:311
  (92 shorter events, 17.3 us)
Async XLA Ops:
  5.6 1.4 %collective-permute-start = (bf16[8,56,128]{2,1,0:T(8,128)(2,1)S(1)}, bf16[8,56,128]{2,1,0:T(8,128)(2,1)S(1)}, u32[]{:S(2)}, u32[]{:S(2)}) collective-permute-start(bf16[8,56,128]{2,1,0:T(8,128)(2,1)S(1)} %pad_maximum_fusion.1.own), channel_id=1, source_target_pairs={{0,4},{4,0},{1,5},{5,1},{2,6},{6,2},{3,7},{7,3},{8,12},{12,8},{9,1... | collective-permute-start | bytes 344072 | tf_op jit(solution)/shard_map/ppermute | solution.py:237
  8.6 17.0 %copy-start.21 = (s32[512]{0:T(512)S(1)}, s32[512]{0:T(512)}, u32[]{:S(2)}) copy-start(s32[512]{0:T(512)} %param.15) | copy-start | bytes 6148
  8.6 37.4 %all-to-all-start = ((bf16[32,2,56,128]{3,2,1,0:T(8,128)(2,1)}), bf16[32,2,56,128]{3,2,1,0:T(8,128)(2,1)S(1)}, u32[]{:S(2)}, u32[]{:S(2)}) async-start(bf16[32,2,56,128]{3,2,1,0:T(8,128)(2,1)} %pack.1), calls=%async_computation | async-start | bytes 1835008 | tf_op jit(solution)/shard_map/all_to_all | solution.py:250
  20.5 28.7 %copy-start.20 = (bf16[200,1024]{1,0:T(8,128)(2,1)S(1)}, bf16[200,1024]{1,0:T(8,128)(2,1)}, u32[]{:S(2)}) copy-start(bf16[200,1024]{1,0:T(8,128)(2,1)} %param.20) | copy-start | bytes 1228804
  20.5 28.7 %copy-start.24 = (pred[128]{0:T(512)(128)(4,1)S(1)}, pred[128]{0:T(512)(128)(4,1)}, u32[]{:S(2)}) copy-start(pred[128]{0:T(512)(128)(4,1)} %constant.84.clone.1) | copy-start | bytes 388
  20.5 57.6 %collective-permute-start.8 = (bf16[128,1024]{1,0:T(8,128)(2,1)}, bf16[128,1024]{1,0:T(8,128)(2,1)}, u32[]{:S(2)}, u32[]{:S(2)}) collective-permute-start(bf16[128,1024]{1,0:T(8,128)(2,1)} %param.23), channel_id=1, source_target_pairs={{0,2},{1,3},{2,0},{3,1},{4,6},{5,7},{6,4},{7,5},{8,10},{9,11},{10,... | collective-permute-start | bytes 786440 | tf_op jit(solution)/shard_map/ppermute | solution.py:227
  23.6 57.1 %collective-permute-start.7 = (bf16[128,1024]{1,0:T(8,128)(2,1)}, bf16[128,1024]{1,0:T(8,128)(2,1)}, u32[]{:S(2)}, u32[]{:S(2)}) collective-permute-start(bf16[128,1024]{1,0:T(8,128)(2,1)} %param.23), channel_id=1, source_target_pairs={{0,3},{1,0},{2,1},{3,2},{4,7},{5,4},{6,5},{7,6},{8,11},{9,8},{10,9... | collective-permute-start | bytes 786440 | tf_op jit(solution)/shard_map/ppermute | solution.py:227
  24.7 56.0 %collective-permute-start.9 = (bf16[128,1024]{1,0:T(8,128)(2,1)}, bf16[128,1024]{1,0:T(8,128)(2,1)}, u32[]{:S(2)}, u32[]{:S(2)}) collective-permute-start(bf16[128,1024]{1,0:T(8,128)(2,1)} %param.23), channel_id=1, source_target_pairs={{0,1},{1,2},{2,3},{3,0},{4,5},{5,6},{6,7},{7,4},{8,9},{9,10},{10,1... | collective-permute-start | bytes 786440 | tf_op jit(solution)/shard_map/ppermute | solution.py:227
  46.8 10.1 %copy-start.22 = (bf16[1024]{0:T(1024)(128)(2,1)S(1)}, bf16[1024]{0:T(1024)(128)(2,1)}, u32[]{:S(2)}) copy-start(bf16[1024]{0:T(1024)(128)(2,1)} %param.21) | copy-start | bytes 6148
  46.8 10.1 %copy-start.19 = (bf16[1024,3,128]{2,0,1:T(8,128)(2,1)S(1)}, bf16[1024,3,128]{2,0,1:T(8,128)(2,1)}, u32[]{:S(2)}) copy-start(bf16[1024,3,128]{2,0,1:T(8,128)(2,1)} %param.22) | copy-start | bytes 2359300
  47.6 7.3 %collective-permute-start.3 = (bf16[256,256]{1,0:T(8,128)(2,1)S(1)}, bf16[256,256]{1,0:T(8,128)(2,1)S(1)}, u32[]{:S(2)}, u32[]{:S(2)}) collective-permute-start(bf16[256,256]{1,0:T(8,128)(2,1)S(1)} %bitcast.27), channel_id=1, source_target_pairs={{0,1},{1,2},{2,3},{3,0},{4,5},{5,6},{6,7},{7,4},{8,9},{9,10},{10,1... | collective-permute-start | bytes 393224 | tf_op jit(solution)/shard_map/ppermute | solution.py:227
  50.0 8.7 %collective-permute-start.2 = (bf16[256,256]{1,0:T(8,128)(2,1)S(1)}, bf16[256,256]{1,0:T(8,128)(2,1)S(1)}, u32[]{:S(2)}, u32[]{:S(2)}) collective-permute-start(bf16[256,256]{1,0:T(8,128)(2,1)S(1)} %bitcast.28), channel_id=1, source_target_pairs={{0,2},{1,3},{2,0},{3,1},{4,6},{5,7},{6,4},{7,5},{8,10},{9,11},{10,... | collective-permute-start | bytes 393224 | tf_op jit(solution)/shard_map/ppermute | solution.py:227
  55.0 5.0 %collective-permute-start.1 = (bf16[256,256]{1,0:T(8,128)(2,1)S(1)}, bf16[256,256]{1,0:T(8,128)(2,1)S(1)}, u32[]{:S(2)}, u32[]{:S(2)}) collective-permute-start(bf16[256,256]{1,0:T(8,128)(2,1)S(1)} %bitcast.29), channel_id=1, source_target_pairs={{0,3},{1,0},{2,1},{3,2},{4,7},{5,4},{6,5},{7,6},{8,11},{9,8},{10,9... | collective-permute-start | bytes 393224 | tf_op jit(solution)/shard_map/ppermute | solution.py:227
  57.6 21.9 %copy-start.23 = (bf16[1024]{0:T(1024)(128)(2,1)S(1)}, bf16[1024]{0:T(1024)(128)(2,1)}, u32[]{:S(2)}) copy-start(bf16[1024]{0:T(1024)(128)(2,1)} %param.24) | copy-start | bytes 6148
  74.9 9.9 %collective-permute-start.6 = (bf16[1024,128]{1,0:T(8,128)(2,1)}, bf16[1024,128]{1,0:T(8,128)(2,1)S(1)}, u32[]{:S(2)}, u32[]{:S(2)}) collective-permute-start(bf16[1024,128]{1,0:T(8,128)(2,1)} %get-tuple-element.11.a0), channel_id=1, source_target_pairs={{0,1},{1,2},{2,3},{3,0},{4,5},{5,6},{6,7},{7,4},{8,9},{9,10},{10,1... | collective-permute-start | bytes 786440 | tf_op jit(solution)/shard_map/ppermute | solution.py:227
  75.8 11.9 %collective-permute-start.5 = (bf16[1024,128]{1,0:T(8,128)(2,1)}, bf16[1024,128]{1,0:T(8,128)(2,1)S(1)}, u32[]{:S(2)}, u32[]{:S(2)}) collective-permute-start(bf16[1024,128]{1,0:T(8,128)(2,1)} %get-tuple-element.11.a0), channel_id=1, source_target_pairs={{0,2},{1,3},{2,0},{3,1},{4,6},{5,7},{6,4},{7,5},{8,10},{9,11},{10,... | collective-permute-start | bytes 786440 | tf_op jit(solution)/shard_map/ppermute | solution.py:227
  78.1 9.5 %collective-permute-start.4 = (bf16[1024,128]{1,0:T(8,128)(2,1)}, bf16[1024,128]{1,0:T(8,128)(2,1)S(1)}, u32[]{:S(2)}, u32[]{:S(2)}) collective-permute-start(bf16[1024,128]{1,0:T(8,128)(2,1)} %get-tuple-element.11.a0), channel_id=1, source_target_pairs={{0,3},{1,0},{2,1},{3,2},{4,7},{5,4},{6,5},{7,6},{8,11},{9,8},{10,9... | collective-permute-start | bytes 786440 | tf_op jit(solution)/shard_map/ppermute | solution.py:227
  80.6 7.0 %copy-start.1 = (bf16[1024,128]{1,0:T(8,128)(2,1)S(1)}, bf16[1024,128]{1,0:T(8,128)(2,1)}, u32[]{:S(2)}) copy-start(bf16[1024,128]{1,0:T(8,128)(2,1)} %copy-done) | copy-start | bytes 786436
  80.7 7.0 %copy-start.3 = (bf16[1024,128]{1,0:T(8,128)(2,1)S(1)}, bf16[1024,128]{1,0:T(8,128)(2,1)}, u32[]{:S(2)}) copy-start(bf16[1024,128]{1,0:T(8,128)(2,1)} %copy-done.2) | copy-start | bytes 786436
  80.7 7.0 %copy-start.5 = (bf16[1024,128]{1,0:T(8,128)(2,1)S(1)}, bf16[1024,128]{1,0:T(8,128)(2,1)}, u32[]{:S(2)}) copy-start(bf16[1024,128]{1,0:T(8,128)(2,1)} %copy-done.4) | copy-start | bytes 786436
  80.7 7.0 %copy-start.11 = (f32[8,1024]{1,0:T(8,128)S(1)}, f32[8,1024]{1,0:T(8,128)}, u32[]{:S(2)}) copy-start(f32[8,1024]{1,0:T(8,128)} %copy-done.10) | copy-start | bytes 98308
  80.7 7.0 %copy-start.15 = (s32[1,4]{1,0:T(1,128)S(1)}, s32[1,4]{1,0:T(1,128)}, u32[]{:S(2)}) copy-start(s32[1,4]{1,0:T(1,128)} %size.3) | copy-start | bytes 52
  101.5 2.7 %collective-permute-start.10 = (f32[32,16,512]{2,1,0:T(8,128)S(1)}, f32[32,16,512]{2,1,0:T(8,128)S(1)}, u32[]{:S(2)}, u32[]{:S(2)}) collective-permute-start(f32[32,16,512]{2,1,0:T(8,128)S(1)} %get-tuple-element.19), channel_id=1, source_target_pairs={{0,4},{4,0},{1,5},{5,1},{2,6},{6,2},{3,7},{7,3},{8,12},{12,8},{9,1... | collective-permute-start | bytes 3145736 | tf_op jit(solution)/shard_map/ppermute | solution.py:310
  105.2 23.0 %all-to-all-start.1 = ((bf16[32,16,512]{2,1,0:T(8,128)(2,1)}), bf16[32,16,512]{2,1,0:T(8,128)(2,1)S(1)}, u32[]{:S(2)}, u32[]{:S(2)}) async-start(bf16[32,16,512]{2,1,0:T(8,128)(2,1)} %add_convert_fusion), calls=%async_computation.1 | async-start | bytes 1048576 | tf_op jit(solution)/shard_map/all_to_all | solution.py:311
  (14 other events, 24.3 us)

commit v2 on v1

--- a/solution.py
+++ b/solution.py
@@ -10,6 +10,7 @@
 BLOCK = 128
 MEL = 100
 SLOT = 56
+ALL = 60
 EPS = 1e-06
 VMEM, SMEM = pltpu.VMEM, pltpu.SMEM
 NT = (((1,), (1,)), ((), ()))
@@ -23,8 +24,28 @@
     return pl.BlockSpec(memory_space=SMEM)
 
 
-def params():
-    return pltpu.CompilerParams(vmem_limit_bytes=48 << 20)
+def hb():
+    return pl.BlockSpec(memory_space=pltpu.HBM)
+
+
+def fetch(pairs, sems):
+    copies = [pltpu.make_async_copy(a, b, sems.at[i]) for i, (a, b) in enumerate(pairs)]
+    for copy in copies:
+        copy.start()
+
+    def wait():
+        for copy in copies:
+            copy.wait()
+
+    return wait
+
+
+def params(mib):
+    return pltpu.CompilerParams(vmem_limit_bytes=mib << 20)
+
+
+def device():
+    return (lax.axis_index("z") * 4 + lax.axis_index("y")) * 2 + lax.axis_index("c")
 
 
 def dot(a, b, dims=None):
@@ -33,36 +54,78 @@
     return lax.dot_general(a, b, dims, preferred_element_type=F32)
 
 
-def pack_kernel(core, bins, own, other, out):
-    c = core[0]
-    for half, ref in ((0, own), (1, other)):
-        out[:, half, 48:SLOT, :] = jnp.broadcast_to(ref[0, 48:SLOT, :][None], (out.shape[0], SLOT - 48, 128))
+def share_kernel(utt_hbm, start_hbm, size_hbm, noise, data, out, utt, start, size, ins, buf, sems):
+    part = pl.multiple_of(lax.axis_index("mp") * 3200, 128)
+    wait = fetch(
+        [(utt_hbm, utt), (start_hbm, start), (size_hbm, size)]
+        + [(ref.at[:, pl.ds(part, 3200)], ins.at[a]) for a, ref in enumerate((noise, data))],
+        sems,
+    )
+    wait()
+    for a in range(2):
+        for r in range(25):
+            buf[pl.ds(a * 25 + r, 8, stride=SLOT), :] = ins[a, :, r * 128 : (r + 1) * 128].astype(F32)
+    count = jnp.int32(0)
+    for u in range(4):
+        count += 2 * utt[0, u] * (jnp.minimum(start[0, u] + size[0, u], 64) - start[0, u])
+    lane = lax.broadcasted_iota(jnp.int32, (SLOT - 50, 128), 1)
+    tail = jnp.where(lane == 0, count >> 5, jnp.where(lane == 1, count & 31, 0)).astype(F32)
+    for b in range(8):
+        buf[b * SLOT + 50 : (b + 1) * SLOT, :] = tail
+        out[b] = buf[b * SLOT : (b + 1) * SLOT, :].astype(BF16)
+
+
+def pack_kernel(bins, own, other, out, ends, tails, sem, sems):
+    here = device()
+    fetch([(ref.at[:, 48:SLOT, :], ends.at[half]) for half, ref in ((0, own), (1, other))], sem)()
+    for half in range(2):
+        tails[:, half] = jnp.broadcast_to(ends[half, 0][None], (out.shape[0], SLOT - 48, 128))
+    sends = []
     for half, ref in ((0, own), (1, other)):
         for i in range(8):
-            b = bins[half * 8 + i]
-
-            @pl.when((b & 1) == c)
+            b = bins[(here ^ half) * 8 + i]
+            copy = pltpu.make_async_copy(
+                ref.at[i, 0:48, :], out.at[b >> 1, half, 0:48, :], sems.at[half * 8 + i]
+            )
+            sends.append(((b & 1) == (here & 1), copy))
+
+            @pl.when(sends[-1][0])
             def _():
-                out[b >> 1, half] = ref[i]
-
-
-def unpack_kernel(source, arrived, out, sems):
-    copies = [
-        pltpu.make_async_copy(arrived.at[source[j]], out.at[j], sems.at[j]) for j in range(8)
-    ]
-    for copy in copies:
-        copy.start()
-    for copy in copies:
-        copy.wait()
-
-
-def utterances(utt, start, size):
+                copy.start()
+                tails[b >> 1, half] = ends[half, i]
+
+    last = pltpu.make_async_copy(tails, out.at[:, :, 48:SLOT, :], sems.at[16])
+    last.start()
+    for chosen, copy in sends:
+        pl.when(chosen)(copy.wait)
+    last.wait()
+
+
+def unpack_kernel(source, arrived, out, slots, wide, rows, sems):
+    fetch([(arrived.at[source[j]], slots.at[j]) for j in range(8)], sems)()
+    for j in range(8):
+        wide[j * SLOT : (j + 1) * SLOT, :] = slots[j].astype(F32)
+    lane = lax.broadcasted_iota(jnp.int32, (8, 128), 1)
+    for a in range(2):
+        lines = [wide[pl.ds(a * 25 + r, 8, stride=SLOT), :] for r in range(25)]
+        for f in range(32):
+            r, off = divmod(f * MEL, 128)
+            line = lines[r]
+            if off:
+                line = pltpu.roll(line, 128 - off, 1)
+                if off + MEL > 128:
+                    line = jnp.where(lane < 128 - off, line, pltpu.roll(lines[r + 1], 128 - off, 1))
+            rows[pl.ds(f, 8, stride=32), :] = jnp.where(lane < MEL, line, 0.0)
+        out[:, a * 128 : (a + 1) * 128] = rows[...].astype(BF16)
+
+
+def utterances(table):
     first, rows = jnp.int32(0), []
     for u in range(4):
-        blocks = utt[0, u]
-        lo = first * BLOCK + 2 * blocks * start[0, u]
+        blocks, start, size = (table[0, 4 * k + u] for k in range(3))
+        lo = first * BLOCK + 2 * blocks * start
         end = (first + blocks) * BLOCK
-        hi = jnp.minimum(first * BLOCK + 2 * blocks * (start[0, u] + size[0, u]), end)
+        hi = jnp.minimum(first * BLOCK + 2 * blocks * (start + size), end)
         rows.append((first * BLOCK, end, lo, hi))
         first = first + blocks
     return rows
@@ -76,9 +139,9 @@
     return hit
 
 
-def each_utterance(utt, body):
+def each_utterance(table, body):
     def step(u, first):
-        blocks = utt[0, u]
+        blocks = table[0, u]
         for length in range(1, 5):
 
             @pl.when(blocks == length)
@@ -96,18 +159,18 @@
 
 
 def front_kernel(
-    place, utt, start, size, level, x0, x1, x2, x3, w, gain, wqkv,
+    table, x0, x1, x2, x3, w, gain, wqkv,
     att, inp, tgt, q, k, v, stat, vt, attt,
 ):
-    spans = utterances(utt, start, size)
+    spans = utterances(table)
     for step, x in enumerate((x0, x1, x2, x3)):
-        part = lax.rem(place[0] + step, 4)
+        part = lax.rem(lax.axis_index("mp") + step, 4)
         row = lax.broadcasted_iota(jnp.int32, (256, 128), 0)
         frame = (row >> 5) * BLOCK + part * 32 + (row & 31)
         lev = jnp.zeros((256, 128), F32)
         for u, (begin, end, _, _) in enumerate(spans):
             inside = (frame >= begin) & (frame < end)
-            lev = jnp.where(inside, level[0, u].astype(F32) / 64.0, lev)
+            lev = jnp.where(inside, table[0, 12 + u].astype(F32) / 64.0, lev)
         noise, data = x[:, :128].astype(F32), x[:, 128:].astype(F32)
         noisy = (1.0 - lev) * noise + lev * data
         cond = jnp.where(masked_of(frame, spans), 0.0, data)
@@ -123,7 +186,7 @@
         h = dot(inp[rows, :], w[...])
         scale = lax.rsqrt(jnp.mean(h * h, axis=1, keepdims=True) + EPS)
         normed = (h * scale * gain[...]).astype(BF16)
-        out = dot(normed, wqkv[...])
+        out = dot(normed, jnp.concatenate([wqkv[0], wqkv[1], wqkv[2]], axis=1))
         q[rows, :] = (out[:, :128].astype(BF16).astype(F32) * HEAD ** (-0.5)).astype(BF16)
         k[rows, :] = out[:, 128:256].astype(BF16)
         v[rows, :] = out[:, 256:].astype(BF16)
@@ -145,15 +208,15 @@
             stat[h : h + 1, at] = top
             stat[h + 2 : h + 3, at] = inv
 
-    each_utterance(utt, one)
+    each_utterance(table, one)
     att[...] = attt[...].T
 
 
 def back_kernel(
-    place, utt, start, size, a0, a1, a2, a3, proj, inp, tgt, w, gain, fgain, vel, q, k, v, stat,
+    table, a0, a1, a2, a3, proj, inp, tgt, w, gain, fgain, vel, q, k, v, stat,
     keep, send, normed, back1, dout, kt, dqt, dk, dv, lhs,
 ):
-    spans = utterances(utt, start, size)
+    spans = utterances(table)
 
     def project(i, carry):
         rows = pl.ds(pl.multiple_of(i * 256, 256), 256)
@@ -198,12 +261,12 @@
         dk[at, :] = jnp.where(mask, dks[0], dks[1]).astype(BF16)
         dv[at, :] = jnp.where(mask, dvs[0], dvs[1]).astype(BF16)
 
-    each_utterance(utt, one)
+    each_utterance(table, one)
     lhs[0:128, :] = dqt[...]
     lhs[128:256, :] = dk[...].T
     lhs[256:384, :] = dv[...].T
     lhs[384:512, :] = a0[...].T
-    mine = place[1] == 0
+    mine = lax.axis_index("c") == 0
     for j in range(4):
         cols = slice(j * 256, (j + 1) * 256)
         top = dot(lhs[0:384, :], normed[:, cols])
@@ -214,70 +277,84 @@
         send[j * 8 : j * 8 + 8] = jnp.where(mine, odd, even)
 
 
+def finish_kernel(count, parts, qkv, out):
+    total = jnp.sum(parts[...].astype(F32), axis=0) / count[...]
+    for j in range(3):
+        qkv[j] = total[:, j * 128 : (j + 1) * 128]
+    out[...] = total[:, 384:]
+
+
 def shards(
     noise_blocks, data_blocks, destination, utt_blocks, span_start, span_size, timestep,
     in_weight, norm_gain, qkv_weight, out_proj, final_gain, vel_weight,
 ):
-    z, y, c, x = (lax.axis_index(n) for n in ("z", "y", "c", "mp"))
-    here = (z * 4 + y) * 2 + c
-    share = noise_blocks.shape[1] // 4
+    here, c = device(), lax.axis_index("c")
     swap = [(0, 1), (1, 0)]
 
     def turned(a, by):
         return lax.ppermute(a, "mp", [(i, (i - by) % 4) for i in range(4)])
 
-    bin_count = jnp.sum(2 * utt_blocks * (jnp.minimum(span_start + span_size, 64) - span_start))
-    lane = lax.broadcasted_iota(jnp.int32, (8, SLOT - 50, 128), 2)
-    tail = jnp.where(lane == 0, bin_count // 32, jnp.where(lane == 1, bin_count % 32, 0)).astype(BF16)
-    mine = [
-        lax.dynamic_slice_in_dim(a, x * share, share, 1).reshape(8, 25, 128)
-        for a in (noise_blocks, data_blocks)
-    ]
-    own = jnp.concatenate([*mine, tail], axis=1)
+    spans = (utt_blocks, span_start, span_size)
+    own = pl.pallas_call(
+        share_kernel,
+        out_shape=jax.ShapeDtypeStruct((8, SLOT, 128), BF16),
+        in_specs=[hb()] * 5,
+        out_specs=vm(),
+        scratch_shapes=[SMEM((1, 4), jnp.int32)] * 3
+        + [VMEM((2, 8, 3200), BF16), VMEM((8 * SLOT, 128), F32), pltpu.SemaphoreType.DMA((5,))],
+        compiler_params=params(ALL),
+        name="share",
+    )(*spans, noise_blocks, data_blocks)
     other = lax.ppermute(own, "c", swap)
     bins = destination // 8
-    nearby = jnp.concatenate(
-        [lax.dynamic_slice_in_dim(bins, here * 8, 8), lax.dynamic_slice_in_dim(bins, (here ^ 1) * 8, 8)]
-    )
     packed = pl.pallas_call(
         pack_kernel,
         out_shape=jax.ShapeDtypeStruct((32, 2, SLOT, 128), BF16),
-        in_specs=[sm(), sm(), vm(), vm()],
-        out_specs=vm(),
-        compiler_params=params(),
+        in_specs=[sm(), hb(), hb()],
+        out_specs=hb(),
+        scratch_shapes=[
+            VMEM((2, 8, SLOT - 48, 128), BF16), VMEM((32, 2, SLOT - 48, 128), BF16),
+            pltpu.SemaphoreType.DMA((2,)), pltpu.SemaphoreType.DMA((17,)),
+        ],
+        compiler_params=params(8),
         name="pack",
-    )(c[None], nearby, own, other)
+    )(bins, own, other)
+    packed, in_weight, qkv_weight, out_proj, vel_weight, norm_gain, final_gain, table = lax.optimization_barrier(
+        (packed, in_weight, qkv_weight, out_proj, vel_weight, norm_gain, final_gain, spans + (timestep,))
+    )
+    table = jnp.concatenate(table, axis=1)
+    w = jnp.concatenate(
+        [jnp.pad(in_weight[:MEL], ((0, 28), (0, 0))), jnp.pad(in_weight[MEL:], ((0, 28), (0, 0)))], axis=0
+    )
+    gain = norm_gain.astype(F32)[None, :]
+    fgain = final_gain.astype(F32)[None, :]
+    wqkv = qkv_weight.transpose(1, 0, 2)
+    vel = jnp.pad(vel_weight, ((0, 0), (0, 28)))
+    proj = jnp.concatenate([out_proj] + [turned(out_proj, by) for by in (1, 2, 3)], axis=0)
     arrived = lax.all_to_all(packed, ("z", "y"), 0, 0, tiled=True).reshape(64, SLOT, 128)
     wanted = here * 8 + jnp.arange(8, dtype=jnp.int32)
     row = jnp.sum(
         jnp.where(destination[None, :] == wanted[:, None], jnp.arange(512, dtype=jnp.int32)[None, :], 0), axis=1
     )
     source = (row >> 4) * 2 + (((row >> 3) & 1) ^ c)
-    blocks = pl.pallas_call(
+    arrived, source, w, gain, fgain, wqkv, vel, proj, table = lax.optimization_barrier(
+        (arrived, source, w, gain, fgain, wqkv, vel, proj, table)
+    )
+    frames = pl.pallas_call(
         unpack_kernel,
-        out_shape=jax.ShapeDtypeStruct((8, SLOT, 128), BF16),
-        in_specs=[sm(), pl.BlockSpec(memory_space=pl.ANY)],
+        out_shape=jax.ShapeDtypeStruct((256, 256), BF16),
+        in_specs=[sm(), hb()],
         out_specs=vm(),
-        scratch_shapes=[pltpu.SemaphoreType.DMA((8,))],
-        compiler_params=params(),
+        scratch_shapes=[
+            VMEM((8, SLOT, 128), BF16), VMEM((8 * SLOT, 128), F32), VMEM((256, 128), F32),
+            pltpu.SemaphoreType.DMA((8,)),
+        ],
+        compiler_params=params(8),
         name="unpack",
     )(source, arrived)
     counts = jnp.sum(arrived[:, 50, 0:2].astype(F32), axis=0)
     count = counts[0] * 32.0 + counts[1]
-    frames = blocks[:, 0:50].reshape(8, 2, 32, MEL).transpose(0, 2, 1, 3)
-    frames = jnp.pad(frames, ((0, 0), (0, 0), (0, 0), (0, 128 - MEL))).reshape(256, 256)
     pieces = [frames] + [turned(frames, by) for by in (1, 2, 3)]
-
-    w = jnp.concatenate(
-        [jnp.pad(in_weight[:MEL], ((0, 28), (0, 0))), jnp.pad(in_weight[MEL:], ((0, 28), (0, 0)))], axis=0
-    )
-    gain = norm_gain.astype(F32)[None, :]
-    fgain = final_gain.astype(F32)[None, :]
-    wqkv = qkv_weight.reshape(1024, 384)
-    vel = jnp.pad(vel_weight, ((0, 0), (0, 28)))
-    proj = jnp.concatenate([out_proj] + [turned(out_proj, by) for by in (1, 2, 3)], axis=0)
-    place = jnp.stack([x, c])
-    tables = (place, utt_blocks, span_start, span_size)
 
     half = jax.ShapeDtypeStruct((1024, 128), BF16)
     att, inp, tgt, q, k, v, stat = pl.pallas_call(
@@ -286,31 +363,38 @@
             half, jax.ShapeDtypeStruct((1024, 256), BF16), jax.ShapeDtypeStruct((1024, 128), F32),
             half, half, half, jax.ShapeDtypeStruct((8, 1024), F32),
         ),
-        in_specs=[sm()] * 5 + [vm()] * 7,
+        in_specs=[sm()] + [vm()] * 7,
         out_specs=(vm(),) * 7,
         scratch_shapes=[VMEM((128, 1024), BF16), VMEM((128, 1024), BF16)],
-        compiler_params=params(),
+        compiler_params=params(20),
         name="front",
-    )(*tables, timestep, *pieces, w, gain, wqkv)
+    )(table, *pieces, w, gain, wqkv)
     heads = [att] + [turned(att, by) for by in (1, 2, 3)]
     terms = jax.ShapeDtypeStruct((32, 16, 512), F32)
     keep, send = pl.pallas_call(
         back_kernel,
         out_shape=(terms, terms),
-        in_specs=[sm()] * 4 + [vm()] * 15,
+        in_specs=[sm()] + [vm()] * 15,
         out_specs=(vm(), vm()),
         scratch_shapes=[
             VMEM((1024, 1024), BF16), VMEM((1024, 1024), BF16), VMEM((1024, 128), BF16),
             VMEM((128, 1024), BF16), VMEM((128, 1024), BF16), VMEM((1024, 128), BF16),
             VMEM((1024, 128), BF16), VMEM((512, 1024), BF16),
         ],
-        compiler_params=params(),
+        compiler_params=params(28),
         name="back",
-    )(*tables, *heads, proj, inp, tgt, w, gain, fgain, vel, q, k, v, stat)
+    )(table, *heads, proj, inp, tgt, w, gain, fgain, vel, q, k, v, stat)
     pair = (keep + lax.ppermute(send, "c", swap)).astype(BF16)
     parts = lax.all_to_all(pair, ("z", "y"), 0, 0, tiled=True)
-    total = jnp.sum(parts.astype(F32), axis=0) / count
-    return (total[:, :384].reshape(16, 3, 128), total[:, 384:].T)
+    grad_qkv, grad_out = pl.pallas_call(
+        finish_kernel,
+        out_shape=(jax.ShapeDtypeStruct((3, 16, 128), F32), jax.ShapeDtypeStruct((16, 128), F32)),
+        in_specs=[vm()] * 2,
+        out_specs=(vm(), vm()),
+        compiler_params=params(8),
+        name="finish",
+    )(count.reshape(1, 1), parts)
+    return (grad_qkv.transpose(1, 0, 2), grad_out.T)
 
 
 def solution(mesh):

time: 131 us -> 118 us (0.901)
  local copies, waits for them, and re-layouts: 13.3 us -> 1.84 us
  other arithmetic: 8.24 us -> 3.16 us
  starting transfers between devices: 32.5 us -> 36.1 us
  between operations: 4.97 us -> 2.25 us
  waiting for transfers between devices: 45.9 us -> 48.1 us
    ppermute x9, waiting for transfers between devices: 7.44 us -> 20.9 us  [turned(): return lax.ppermute(a, 'mp', [(i, (i - by) % 4) for i in range(4)])]
    all_to_all x1, waiting for transfers between devices: 20.2 us -> 8.56 us  [shards(): lax.all_to_all(packed, ('z', 'y'), 0, 0, tiled=True).reshape(64, SLOT, 128)]
    unnamed x55 -> x26, local copies, waits for them, and re-layouts: 9.31 us -> 0.97 us
    ppermute x9, starting transfers between devices: 14.6 us -> 16.5 us  [turned(): return lax.ppermute(a, 'mp', [(i, (i - by) % 4) for i in range(4)])]
    reshape x5 -> x0, local copies, waits for them, and re-layouts: 1.74 us -> none  [the longest x3 0.87 us: shards(): lax.dynamic_slice_in_dim(a, x * share, share, 1).reshape(8, 25, 128)]
    all_to_all x1, starting transfers between devices: 5.89 us -> 7.61 us  [shards(): parts = lax.all_to_all(pair, ('z', 'y'), 0, 0, tiled=True)]
    pallas_call x2 -> x4, Pallas kernels: 14.5 us -> 16.2 us  [the longest x1 12.8 us: shards(): pl.pallas_call(back_kernel, out_shape=(terms, terms), in_specs=[sm()] + [...]
    reduce_sum x2 -> x0, other arithmetic: 1.41 us -> none  [the longest x1 1.33 us: shards(): jnp.sum(2 * utt_blocks * (jnp.minimum(span_start + span_size, 64) - span_...]
  transfers between devices with their start and end apart: 13 -> 13, of which waited for: 8 -> 11; matrix products, arithmetic and copies ran while one was open for 8% -> 3% of each run, Pallas kernels for 7% -> 0%
where the time goes in v2:
time: 118 us; the launch traced here: 117 us
  waiting for transfers between devices  48.1 us (41%)
  starting transfers between devices  36.1 us (31%)
  Pallas kernels  25.4 us (22%)
  other arithmetic  3.16 us (3%)
  between operations  2.25 us (2%)
  local copies, waits for them, and re-layouts  1.84 us (2%)
    ppermute x9, waiting for transfers between devices, turned(): return lax.ppermute(a, 'mp', [(i, (i - by) % 4) for i in range(4)])  20.9 us
    ppermute x9, starting transfers between devices, turned(): return lax.ppermute(a, 'mp', [(i, (i - by) % 4) for i in range(4)])  16.5 us
    all_to_all x1, waiting for transfers between devices, shards(): parts = lax.all_to_all(pair, ('z', 'y'), 0, 0, tiled=True)  15.2 us
    pallas_call x1, Pallas kernels, shards(): pl.pallas_call(back_kernel, out_shape=(terms, terms), in_specs=[sm()] + [...  12.8 us
    all_to_all x1, starting transfers between devices, shards(): lax.all_to_all(packed, ('z', 'y'), 0, 0, tiled=True).reshape(64, SLOT, 128)  11.8 us
    all_to_all x1, waiting for transfers between devices, shards(): lax.all_to_all(packed, ('z', 'y'), 0, 0, tiled=True).reshape(64, SLOT, 128)  8.56 us
    pallas_call x1, Pallas kernels, shards(): pl.pallas_call(front_kernel, out_shape=(half, jax.ShapeDtypeStruct((1024,...  7.69 us
    all_to_all x1, starting transfers between devices, shards(): parts = lax.all_to_all(pair, ('z', 'y'), 0, 0, tiled=True)  7.61 us
  transfers between devices with their start and end apart: 13, of which 11 were waited for; matrix products, arithmetic and copies ran while one was open for 3% of the time, Pallas kernels for 0%

profile of v2, /device:TPU:8, one launch (start us, length us, event | category | flops | bytes accessed | tf_op | source)
XLA Modules:
  0.0 116.9 jit_solution(6046503531921860594)
XLA Ops:
  0.6 1.6 %share.1.own = bf16[8,56,128]{2,1,0:T(8,128)(2,1)} custom-call(s32[1,4]{1,0:T(1,128)} %utt_hbm.1, s32[1,4]{1,0:T(1,128)} %start_hbm.1, s32[1,4]{1,0:T(1,128)} %size_hbm.1, bf16[8,12800]{1,0:T(8,128)(2,1)} %noise.1, bf16[8,12800]{1,0:T(8,128)(2,1)} %data.1), custom_call_target="tpu_custom_call" | custom-call | tf_op jit(solution)/shard_map/share/pallas_call | solution.py:298
  4.7 1.6 %pack.1 = bf16[32,2,56,128]{3,2,1,0:T(8,128)(2,1)} custom-call(s32[512]{0:T(512)S(1)} %add_select_fusion.bins, bf16[8,56,128]{2,1,0:T(8,128)(2,1)S(1)} %copy-done.1, bf16[8,56,128]{2,1,0:T(8,128)(2,1)S(1)} %collective-permute-done.other), custom_call_target="tpu_custom_call" | custom-call | tf_op jit(solution)/shard_map/pack/pallas_call | solution.py:310
  6.4 11.8 %all-to-all-start = ((bf16[32,2,56,128]{3,2,1,0:T(8,128)(2,1)}), bf16[32,2,56,128]{3,2,1,0:T(8,128)(2,1)S(1)}, u32[]{:S(2)}, u32[]{:S(2)}) async-start(bf16[32,2,56,128]{3,2,1,0:T(8,128)(2,1)} %pack.1), calls=%async_computation | async-start | bytes 1835008 | tf_op jit(solution)/shard_map/all_to_all | solution.py:334
  18.5 1.6 %collective-permute-start.3 = (bf16[128,1024]{1,0:T(8,128)(2,1)S(1)}, bf16[128,1024]{1,0:T(8,128)(2,1)S(1)}, u32[]{:S(2)}, u32[]{:S(2)}) collective-permute-start(bf16[128,1024]{1,0:T(8,128)(2,1)S(1)} %copy-done.3), channel_id=1, source_target_pairs={{0,1},{1,2},{2,3},{3,0},{4,5},{5,6},{6,7},{7,4},{8,9},{9,10},{10,1... | collective-permute-start | bytes 786440 | tf_op jit(solution)/shard_map/ppermute | solution.py:295
  20.1 2.7 %collective-permute-start.2 = (bf16[128,1024]{1,0:T(8,128)(2,1)S(1)}, bf16[128,1024]{1,0:T(8,128)(2,1)S(1)}, u32[]{:S(2)}, u32[]{:S(2)}) collective-permute-start(bf16[128,1024]{1,0:T(8,128)(2,1)S(1)} %copy-done.3), channel_id=1, source_target_pairs={{0,2},{1,3},{2,0},{3,1},{4,6},{5,7},{6,4},{7,5},{8,10},{9,11},{10,... | collective-permute-start | bytes 786440 | tf_op jit(solution)/shard_map/ppermute | solution.py:295
  22.8 1.4 %collective-permute-start.1 = (bf16[128,1024]{1,0:T(8,128)(2,1)S(1)}, bf16[128,1024]{1,0:T(8,128)(2,1)}, u32[]{:S(2)}, u32[]{:S(2)}) collective-permute-start(bf16[128,1024]{1,0:T(8,128)(2,1)S(1)} %copy-done.3), channel_id=1, source_target_pairs={{0,3},{1,0},{2,1},{3,2},{4,7},{5,4},{6,5},{7,6},{8,11},{9,8},{10,9... | collective-permute-start | bytes 786440 | tf_op jit(solution)/shard_map/ppermute | solution.py:295
  24.9 3.2 %collective-permute-done.3 = bf16[128,1024]{1,0:T(8,128)(2,1)S(1)} collective-permute-done((bf16[128,1024]{1,0:T(8,128)(2,1)S(1)}, bf16[128,1024]{1,0:T(8,128)(2,1)S(1)}, u32[]{:S(2)}, u32[]{:S(2)}) %collective-permute-start.3) | collective-permute-done | bytes 262176 | tf_op jit(solution)/shard_map/ppermute | solution.py:295
  28.0 6.2 %collective-permute-done.2 = bf16[128,1024]{1,0:T(8,128)(2,1)S(1)} collective-permute-done((bf16[128,1024]{1,0:T(8,128)(2,1)S(1)}, bf16[128,1024]{1,0:T(8,128)(2,1)S(1)}, u32[]{:S(2)}, u32[]{:S(2)}) %collective-permute-start.2) | collective-permute-done | bytes 262176 | tf_op jit(solution)/shard_map/ppermute | solution.py:295
  35.2 8.6 %all-to-all-done = bf16[32,2,56,128]{3,2,1,0:T(8,128)(2,1)S(1)} async-done(((bf16[32,2,56,128]{3,2,1,0:T(8,128)(2,1)}), bf16[32,2,56,128]{3,2,1,0:T(8,128)(2,1)S(1)}, u32[]{:S(2)}, u32[]{:S(2)}) %all-to-all-start) | async-done | bytes 917536 | tf_op jit(solution)/shard_map/all_to_all | solution.py:334
  43.8 1.0 unpack.1.x0
  44.8 1.6 %collective-permute-start.6 = (bf16[256,256]{1,0:T(8,128)(2,1)S(1)}, bf16[256,256]{1,0:T(8,128)(2,1)S(1)}, u32[]{:S(2)}, u32[]{:S(2)}) collective-permute-start(bf16[256,256]{1,0:T(8,128)(2,1)S(1)} %unpack.1.x0), channel_id=1, source_target_pairs={{0,1},{1,2},{2,3},{3,0},{4,5},{5,6},{6,7},{7,4},{8,9},{9,10},{10,1... | collective-permute-start | bytes 393224 | tf_op jit(solution)/shard_map/ppermute | solution.py:295
  46.4 2.7 %collective-permute-start.5 = (bf16[256,256]{1,0:T(8,128)(2,1)S(1)}, bf16[256,256]{1,0:T(8,128)(2,1)S(1)}, u32[]{:S(2)}, u32[]{:S(2)}) collective-permute-start(bf16[256,256]{1,0:T(8,128)(2,1)S(1)} %unpack.1.x0), channel_id=1, source_target_pairs={{0,2},{1,3},{2,0},{3,1},{4,6},{5,7},{6,4},{7,5},{8,10},{9,11},{10,... | collective-permute-start | bytes 393224 | tf_op jit(solution)/shard_map/ppermute | solution.py:295
  49.1 1.4 %collective-permute-start.4 = (bf16[256,256]{1,0:T(8,128)(2,1)S(1)}, bf16[256,256]{1,0:T(8,128)(2,1)S(1)}, u32[]{:S(2)}, u32[]{:S(2)}) collective-permute-start(bf16[256,256]{1,0:T(8,128)(2,1)S(1)} %unpack.1.x0), channel_id=1, source_target_pairs={{0,3},{1,0},{2,1},{3,2},{4,7},{5,4},{6,5},{7,6},{8,11},{9,8},{10,9... | collective-permute-start | bytes 393224 | tf_op jit(solution)/shard_map/ppermute | solution.py:295
  50.6 1.6 %collective-permute-done.6.x3 = bf16[256,256]{1,0:T(8,128)(2,1)S(1)} collective-permute-done((bf16[256,256]{1,0:T(8,128)(2,1)S(1)}, bf16[256,256]{1,0:T(8,128)(2,1)S(1)}, u32[]{:S(2)}, u32[]{:S(2)}) %collective-permute-start.6) | collective-permute-done | bytes 131104 | tf_op jit(solution)/shard_map/ppermute | solution.py:295
  52.2 1.4 %collective-permute-done.5.x2 = bf16[256,256]{1,0:T(8,128)(2,1)S(1)} collective-permute-done((bf16[256,256]{1,0:T(8,128)(2,1)S(1)}, bf16[256,256]{1,0:T(8,128)(2,1)S(1)}, u32[]{:S(2)}, u32[]{:S(2)}) %collective-permute-start.5) | collective-permute-done | bytes 131104 | tf_op jit(solution)/shard_map/ppermute | solution.py:295
  54.1 7.7 %front.1 = (bf16[1024,128]{1,0:T(8,128)(2,1)S(1)}, bf16[1024,256]{1,0:T(8,128)(2,1)S(1)}, f32[1024,128]{1,0:T(8,128)S(1)}, bf16[1024,128]{1,0:T(8,128)(2,1)S(1)}...) custom-call(s32[1,16]{1,0:T(1,128)S(1)} %pad_add_fusion.table, ...), custom_call_target="tpu_custom_call" | custom-call | tf_op jit(solution)/shard_map/front/pallas_call | solution.py:360
  61.8 1.4 %collective-permute-start.9 = (bf16[1024,128]{1,0:T(8,128)(2,1)S(1)}, bf16[1024,128]{1,0:T(8,128)(2,1)S(1)}, u32[]{:S(2)}, u32[]{:S(2)}) collective-permute-start(bf16[1024,128]{1,0:T(8,128)(2,1)S(1)} %get-tuple-element.50.a0), channel_id=1, source_target_pairs={{0,1},{1,2},{2,3},{3,0},{4,5},{5,6},{6,7},{7,4},{8,9},{9,10},{10,1... | collective-permute-start | bytes 786440 | tf_op jit(solution)/shard_map/ppermute | solution.py:295
  63.2 2.8 %collective-permute-start.8 = (bf16[1024,128]{1,0:T(8,128)(2,1)S(1)}, bf16[1024,128]{1,0:T(8,128)(2,1)S(1)}, u32[]{:S(2)}, u32[]{:S(2)}) collective-permute-start(bf16[1024,128]{1,0:T(8,128)(2,1)S(1)} %get-tuple-element.50.a0), channel_id=1, source_target_pairs={{0,2},{1,3},{2,0},{3,1},{4,6},{5,7},{6,4},{7,5},{8,10},{9,11},{10,... | collective-permute-start | bytes 786440 | tf_op jit(solution)/shard_map/ppermute | solution.py:295
  66.8 5.2 %collective-permute-done.9.a3 = bf16[1024,128]{1,0:T(8,128)(2,1)S(1)} collective-permute-done((bf16[1024,128]{1,0:T(8,128)(2,1)S(1)}, bf16[1024,128]{1,0:T(8,128)(2,1)S(1)}, u32[]{:S(2)}, u32[]{:S(2)}) %collective-permute-start.9) | collective-permute-done | bytes 262176 | tf_op jit(solution)/shard_map/ppermute | solution.py:295
  72.0 2.8 %collective-permute-done.8.a2 = bf16[1024,128]{1,0:T(8,128)(2,1)S(1)} collective-permute-done((bf16[1024,128]{1,0:T(8,128)(2,1)S(1)}, bf16[1024,128]{1,0:T(8,128)(2,1)S(1)}, u32[]{:S(2)}, u32[]{:S(2)}) %collective-permute-start.8) | collective-permute-done | bytes 262176 | tf_op jit(solution)/shard_map/ppermute | solution.py:295
  74.8 12.8 %back.1 = (f32[32,16,512]{2,1,0:T(8,128)S(1)}, f32[32,16,512]{2,1,0:T(8,128)S(1)}) custom-call(s32[1,16]{1,0:T(1,128)S(1)} %pad_add_fusion.table, bf16[1024,128]{1,0:T(8,128)(2,1)S(1)} %get-tuple-element.50.a0, bf16[1024,128]{1,0:T(8,128)(2,1)S(1)} %collective-permute-done.7.a1, bf16[1024,128]{1,0:T(8,128)(2,1)S(1)} %collective-permute-done.8.a2, ...), custom_call_target="tpu_custom_call" | custom-call | tf_op jit(solution)/shard_map/back/pallas_call | solution.py:374
  87.8 2.6 %collective-permute-done.10 = f32[32,16,512]{2,1,0:T(8,128)S(1)} collective-permute-done((f32[32,16,512]{2,1,0:T(8,128)S(1)}, f32[32,16,512]{2,1,0:T(8,128)S(1)}, u32[]{:S(2)}, u32[]{:S(2)}) %collective-permute-start.10) | collective-permute-done | bytes 1048608 | tf_op jit(solution)/shard_map/ppermute | solution.py:387
  91.4 7.6 %all-to-all-start.1 = ((bf16[32,16,512]{2,1,0:T(8,128)(2,1)}), bf16[32,16,512]{2,1,0:T(8,128)(2,1)S(1)}, u32[]{:S(2)}, u32[]{:S(2)}) async-start(bf16[32,16,512]{2,1,0:T(8,128)(2,1)} %add_convert_fusion), calls=%async_computation.1 | async-start | bytes 1048576 | tf_op jit(solution)/shard_map/all_to_all | solution.py:388
  101.0 15.2 %all-to-all-done.1.parts = bf16[32,16,512]{2,1,0:T(8,128)(2,1)S(1)} async-done(((bf16[32,16,512]{2,1,0:T(8,128)(2,1)}), bf16[32,16,512]{2,1,0:T(8,128)(2,1)S(1)}, u32[]{:S(2)}, u32[]{:S(2)}) %all-to-all-start.1) | async-done | bytes 524320 | tf_op jit(solution)/shard_map/all_to_all | solution.py:388
  (50 shorter events, 8.1 us)
Async XLA Ops:
  2.2 1.6 %collective-permute-start = (bf16[8,56,128]{2,1,0:T(8,128)(2,1)}, bf16[8,56,128]{2,1,0:T(8,128)(2,1)S(1)}, u32[]{:S(2)}, u32[]{:S(2)}) collective-permute-start(bf16[8,56,128]{2,1,0:T(8,128)(2,1)} %share.1.own), channel_id=1, source_target_pairs={{0,4},{4,0},{1,5},{5,1},{2,6},{6,2},{3,7},{7,3},{8,12},{12,8},{9,1... | collective-permute-start | bytes 344072 | tf_op jit(solution)/shard_map/ppermute | solution.py:308
  6.3 12.0 %copy-start.5 = (s32[512]{0:T(512)S(1)}, s32[512]{0:T(512)}, u32[]{:S(2)}) copy-start(s32[512]{0:T(512)} %param.15) | copy-start | bytes 6148
  6.3 12.2 %copy-start.3 = (bf16[128,1024]{1,0:T(8,128)(2,1)S(1)}, bf16[128,1024]{1,0:T(8,128)(2,1)}, u32[]{:S(2)}) copy-start(bf16[128,1024]{1,0:T(8,128)(2,1)} %param.23) | copy-start | bytes 786436
  6.3 17.9 %copy-start.2 = (bf16[200,1024]{1,0:T(8,128)(2,1)S(1)}, bf16[200,1024]{1,0:T(8,128)(2,1)}, u32[]{:S(2)}) copy-start(bf16[200,1024]{1,0:T(8,128)(2,1)} %param.20) | copy-start | bytes 1228804
  6.3 17.9 %copy-start.11 = (pred[128]{0:T(512)(128)(4,1)S(1)}, pred[128]{0:T(512)(128)(4,1)}, u32[]{:S(2)}) copy-start(pred[128]{0:T(512)(128)(4,1)} %constant.46.clone.1) | copy-start | bytes 388
  6.4 18.1 %copy-start.9 = (bf16[1024]{0:T(1024)(128)(2,1)S(1)}, bf16[1024]{0:T(1024)(128)(2,1)}, u32[]{:S(2)}) copy-start(bf16[1024]{0:T(1024)(128)(2,1)} %param.21) | copy-start | bytes 6148
  6.4 18.1 %copy-start.10 = (bf16[1024]{0:T(1024)(128)(2,1)S(1)}, bf16[1024]{0:T(1024)(128)(2,1)}, u32[]{:S(2)}) copy-start(bf16[1024]{0:T(1024)(128)(2,1)} %param.24) | copy-start | bytes 6148
  6.4 18.1 %copy-start.4 = (bf16[1024,100]{0,1:T(8,128)(2,1)S(1)}, bf16[1024,100]{0,1:T(8,128)(2,1)}, u32[]{:S(2)}) copy-start(bf16[1024,100]{0,1:T(8,128)(2,1)} %param.25) | copy-start | bytes 614404
  6.4 37.4 %all-to-all-start = ((bf16[32,2,56,128]{3,2,1,0:T(8,128)(2,1)}), bf16[32,2,56,128]{3,2,1,0:T(8,128)(2,1)S(1)}, u32[]{:S(2)}, u32[]{:S(2)}) async-start(bf16[32,2,56,128]{3,2,1,0:T(8,128)(2,1)} %pack.1), calls=%async_computation | async-start | bytes 1835008 | tf_op jit(solution)/shard_map/all_to_all | solution.py:334
  18.2 6.5 %copy-start.6 = (s32[1,4]{1,0:T(1,128)S(1)}, s32[1,4]{1,0:T(1,128)}, u32[]{:S(2)}) copy-start(s32[1,4]{1,0:T(1,128)} %utt_hbm.1) | copy-start | bytes 52
  18.2 6.5 %copy-start.7 = (s32[1,4]{1,0:T(1,128)S(1)}, s32[1,4]{1,0:T(1,128)}, u32[]{:S(2)}) copy-start(s32[1,4]{1,0:T(1,128)} %start_hbm.1) | copy-start | bytes 52
  18.3 6.5 %copy-start.8 = (s32[1,4]{1,0:T(1,128)S(1)}, s32[1,4]{1,0:T(1,128)}, u32[]{:S(2)}) copy-start(s32[1,4]{1,0:T(1,128)} %size_hbm.1) | copy-start | bytes 52
  18.5 9.5 %collective-permute-start.3 = (bf16[128,1024]{1,0:T(8,128)(2,1)S(1)}, bf16[128,1024]{1,0:T(8,128)(2,1)S(1)}, u32[]{:S(2)}, u32[]{:S(2)}) collective-permute-start(bf16[128,1024]{1,0:T(8,128)(2,1)S(1)} %copy-done.3), channel_id=1, source_target_pairs={{0,1},{1,2},{2,3},{3,0},{4,5},{5,6},{6,7},{7,4},{8,9},{9,10},{10,1... | collective-permute-start | bytes 786440 | tf_op jit(solution)/shard_map/ppermute | solution.py:295
  20.1 14.1 %collective-permute-start.2 = (bf16[128,1024]{1,0:T(8,128)(2,1)S(1)}, bf16[128,1024]{1,0:T(8,128)(2,1)S(1)}, u32[]{:S(2)}, u32[]{:S(2)}) collective-permute-start(bf16[128,1024]{1,0:T(8,128)(2,1)S(1)} %copy-done.3), channel_id=1, source_target_pairs={{0,2},{1,3},{2,0},{3,1},{4,6},{5,7},{6,4},{7,5},{8,10},{9,11},{10,... | collective-permute-start | bytes 786440 | tf_op jit(solution)/shard_map/ppermute | solution.py:295
  22.8 11.4 %collective-permute-start.1 = (bf16[128,1024]{1,0:T(8,128)(2,1)S(1)}, bf16[128,1024]{1,0:T(8,128)(2,1)}, u32[]{:S(2)}, u32[]{:S(2)}) collective-permute-start(bf16[128,1024]{1,0:T(8,128)(2,1)S(1)} %copy-done.3), channel_id=1, source_target_pairs={{0,3},{1,0},{2,1},{3,2},{4,7},{5,4},{6,5},{7,6},{8,11},{9,8},{10,9... | collective-permute-start | bytes 786440 | tf_op jit(solution)/shard_map/ppermute | solution.py:295
  35.2 18.9 %copy-start = (bf16[1024,3,128]{2,0,1:T(8,128)(2,1)S(1)}, bf16[1024,3,128]{2,0,1:T(8,128)(2,1)}, u32[]{:S(2)}) copy-start(bf16[1024,3,128]{2,0,1:T(8,128)(2,1)} %param.22) | copy-start | bytes 2359300
  44.8 7.3 %collective-permute-start.6 = (bf16[256,256]{1,0:T(8,128)(2,1)S(1)}, bf16[256,256]{1,0:T(8,128)(2,1)S(1)}, u32[]{:S(2)}, u32[]{:S(2)}) collective-permute-start(bf16[256,256]{1,0:T(8,128)(2,1)S(1)} %unpack.1.x0), channel_id=1, source_target_pairs={{0,1},{1,2},{2,3},{3,0},{4,5},{5,6},{6,7},{7,4},{8,9},{9,10},{10,1... | collective-permute-start | bytes 393224 | tf_op jit(solution)/shard_map/ppermute | solution.py:295
  46.4 7.2 %collective-permute-start.5 = (bf16[256,256]{1,0:T(8,128)(2,1)S(1)}, bf16[256,256]{1,0:T(8,128)(2,1)S(1)}, u32[]{:S(2)}, u32[]{:S(2)}) collective-permute-start(bf16[256,256]{1,0:T(8,128)(2,1)S(1)} %unpack.1.x0), channel_id=1, source_target_pairs={{0,2},{1,3},{2,0},{3,1},{4,6},{5,7},{6,4},{7,5},{8,10},{9,11},{10,... | collective-permute-start | bytes 393224 | tf_op jit(solution)/shard_map/ppermute | solution.py:295
  49.1 5.0 %collective-permute-start.4 = (bf16[256,256]{1,0:T(8,128)(2,1)S(1)}, bf16[256,256]{1,0:T(8,128)(2,1)S(1)}, u32[]{:S(2)}, u32[]{:S(2)}) collective-permute-start(bf16[256,256]{1,0:T(8,128)(2,1)S(1)} %unpack.1.x0), channel_id=1, source_target_pairs={{0,3},{1,0},{2,1},{3,2},{4,7},{5,4},{6,5},{7,6},{8,11},{9,8},{10,9... | collective-permute-start | bytes 393224 | tf_op jit(solution)/shard_map/ppermute | solution.py:295
  61.8 10.2 %collective-permute-start.9 = (bf16[1024,128]{1,0:T(8,128)(2,1)S(1)}, bf16[1024,128]{1,0:T(8,128)(2,1)S(1)}, u32[]{:S(2)}, u32[]{:S(2)}) collective-permute-start(bf16[1024,128]{1,0:T(8,128)(2,1)S(1)} %get-tuple-element.50.a0), channel_id=1, source_target_pairs={{0,1},{1,2},{2,3},{3,0},{4,5},{5,6},{6,7},{7,4},{8,9},{9,10},{10,1... | collective-permute-start | bytes 786440 | tf_op jit(solution)/shard_map/ppermute | solution.py:295
  63.2 11.7 %collective-permute-start.8 = (bf16[1024,128]{1,0:T(8,128)(2,1)S(1)}, bf16[1024,128]{1,0:T(8,128)(2,1)S(1)}, u32[]{:S(2)}, u32[]{:S(2)}) collective-permute-start(bf16[1024,128]{1,0:T(8,128)(2,1)S(1)} %get-tuple-element.50.a0), channel_id=1, source_target_pairs={{0,2},{1,3},{2,0},{3,1},{4,6},{5,7},{6,4},{7,5},{8,10},{9,11},{10,... | collective-permute-start | bytes 786440 | tf_op jit(solution)/shard_map/ppermute | solution.py:295
  66.0 8.8 %collective-permute-start.7 = (bf16[1024,128]{1,0:T(8,128)(2,1)S(1)}, bf16[1024,128]{1,0:T(8,128)(2,1)S(1)}, u32[]{:S(2)}, u32[]{:S(2)}) collective-permute-start(bf16[1024,128]{1,0:T(8,128)(2,1)S(1)} %get-tuple-element.50.a0), channel_id=1, source_target_pairs={{0,3},{1,0},{2,1},{3,2},{4,7},{5,4},{6,5},{7,6},{8,11},{9,8},{10,9... | collective-permute-start | bytes 786440 | tf_op jit(solution)/shard_map/ppermute | solution.py:295
  87.7 2.7 %collective-permute-start.10 = (f32[32,16,512]{2,1,0:T(8,128)S(1)}, f32[32,16,512]{2,1,0:T(8,128)S(1)}, u32[]{:S(2)}, u32[]{:S(2)}) collective-permute-start(f32[32,16,512]{2,1,0:T(8,128)S(1)} %get-tuple-element.61), channel_id=1, source_target_pairs={{0,4},{4,0},{1,5},{5,1},{2,6},{6,2},{3,7},{7,3},{8,12},{12,8},{9,1... | collective-permute-start | bytes 3145736 | tf_op jit(solution)/shard_map/ppermute | solution.py:387
  91.4 24.8 %all-to-all-start.1 = ((bf16[32,16,512]{2,1,0:T(8,128)(2,1)}), bf16[32,16,512]{2,1,0:T(8,128)(2,1)S(1)}, u32[]{:S(2)}, u32[]{:S(2)}) async-start(bf16[32,16,512]{2,1,0:T(8,128)(2,1)} %add_convert_fusion), calls=%async_computation.1 | async-start | bytes 1048576 | tf_op jit(solution)/shard_map/all_to_all | solution.py:388
  (2 other events, 7.4 us)

commit v3 on v2

--- a/solution.py
+++ b/solution.py
@@ -160,7 +160,7 @@
 
 def front_kernel(
     table, x0, x1, x2, x3, w, gain, wqkv,
-    att, inp, tgt, q, k, v, stat, vt, attt,
+    att, inp, tgt, q, k, v, probs_out, vt, attt,
 ):
     spans = utterances(table)
     for step, x in enumerate((x0, x1, x2, x3)):
@@ -181,18 +181,16 @@
             inp[at, :] = both[b * 32 : b * 32 + 32]
             tgt[at, :] = diff[b * 32 : b * 32 + 32]
 
-    def project(i, carry):
-        rows = pl.ds(pl.multiple_of(i * 256, 256), 256)
+    qkv = jnp.concatenate([wqkv[0], wqkv[1], wqkv[2]], axis=1)
+    for i in range(4):
+        rows = pl.ds(i * 256, 256)
         h = dot(inp[rows, :], w[...])
         scale = lax.rsqrt(jnp.mean(h * h, axis=1, keepdims=True) + EPS)
-        normed = (h * scale * gain[...]).astype(BF16)
-        out = dot(normed, jnp.concatenate([wqkv[0], wqkv[1], wqkv[2]], axis=1))
+        out = dot((h * scale * gain[...]).astype(BF16), qkv)
         q[rows, :] = (out[:, :128].astype(BF16).astype(F32) * HEAD ** (-0.5)).astype(BF16)
         k[rows, :] = out[:, 128:256].astype(BF16)
         v[rows, :] = out[:, 256:].astype(BF16)
-        return carry
-
-    lax.fori_loop(0, 4, project, 0)
+
     vt[...] = v[...].T
 
     def one(first, rows):
@@ -203,28 +201,33 @@
             top = jnp.max(scores, axis=0, keepdims=True)
             weights = jnp.exp(scores - top)
             inv = 1.0 / jnp.sum(weights, axis=0, keepdims=True)
-            probs = (weights * inv).astype(BF16)
-            attt[h * HEAD : (h + 1) * HEAD, at] = dot(vt[h * HEAD : (h + 1) * HEAD, at], probs).astype(BF16)
-            stat[h : h + 1, at] = top
-            stat[h + 2 : h + 3, at] = inv
+            probs = weights * inv
+            probs_out[h, at, 0:rows] = probs
+            part = dot(vt[h * HEAD : (h + 1) * HEAD, at], probs.astype(BF16))
+            attt[h * HEAD : (h + 1) * HEAD, at] = part.astype(BF16)
 
     each_utterance(table, one)
     att[...] = attt[...].T
 
 
+def mid_kernel(inp, w, gain, hidden, normed):
+    for i in range(4):
+        rows = pl.ds(i * 256, 256)
+        h = dot(inp[rows, :], w[...])
+        hidden[rows, :] = h
+        scale = lax.rsqrt(jnp.mean(h * h, axis=1, keepdims=True) + EPS)
+        normed[rows, :] = (h * scale * gain[...]).astype(BF16)
+
+
 def back_kernel(
-    table, a0, a1, a2, a3, proj, inp, tgt, w, gain, fgain, vel, q, k, v, stat,
-    keep, send, normed, back1, dout, kt, dqt, dk, dv, lhs,
+    table, a0, a1, a2, a3, proj, hidden, normed, tgt, fgain, vel, q, k, v, probs,
+    keep, send, back1, dout, kt, dqt, dk, dv, lhs,
 ):
     spans = utterances(table)
-
-    def project(i, carry):
-        rows = pl.ds(pl.multiple_of(i * 256, 256), 256)
-        h = dot(inp[rows, :], w[...])
-        scale = lax.rsqrt(jnp.mean(h * h, axis=1, keepdims=True) + EPS)
-        normed[rows, :] = (h * scale * gain[...]).astype(BF16)
+    for i in range(4):
+        rows = pl.ds(i * 256, 256)
         groups = jnp.concatenate([a0[rows, :], a1[rows, :], a2[rows, :], a3[rows, :]], axis=1)
-        wide = (h + dot(groups, proj[...])).astype(BF16).astype(F32)
+        wide = (hidden[rows, :] + dot(groups, proj[...])).astype(BF16).astype(F32)
         rscale = lax.rsqrt(jnp.mean(wide * wide, axis=1, keepdims=True) + EPS)
         normalized = wide * rscale
         final = (normalized * fgain[...]).astype(BF16)
@@ -236,20 +239,17 @@
         b1 = (rscale * (scaled - normalized * middle)).astype(BF16)
         back1[rows, :] = b1
         dout[rows, :] = dot(b1, proj[0:128, :], NT).astype(BF16)
-        return carry
-
-    lax.fori_loop(0, 4, project, 0)
+
     kt[...] = k[...].T
 
     def one(first, rows):
         at = pl.ds(first, rows)
-        qs, ks, vs, ds = q[at, :], k[at, :], v[at, :], dout[at, :]
+        qs, vs, ds = q[at, :], v[at, :], dout[at, :]
         dks, dvs = [], []
         for h in range(2):
             mask = head_mask(rows, h)
             zero = jnp.zeros((), BF16)
-            scores = dot(jnp.where(mask, ks, zero), qs, NT)
-            p = jnp.exp(scores - stat[h : h + 1, at]) * stat[h + 2 : h + 3, at]
+            p = probs[h, at, 0:rows]
             dp = dot(jnp.where(mask, vs, zero), ds, NT).astype(BF16).astype(F32)
             inner = jnp.sum(p * dp, axis=0, keepdims=True)
             dscore = (p * (dp - inner)).astype(BF16)
@@ -273,8 +273,21 @@
         low = dot(lhs[384:512, :], back1[:, cols])
         terms = jnp.concatenate([top.T, low.T], axis=1).reshape(8, 2, 16, 512)
         even, odd = terms[:, 0], terms[:, 1]
-        keep[j * 8 : j * 8 + 8] = jnp.where(mine, even, odd)
-        send[j * 8 : j * 8 + 8] = jnp.where(mine, odd, even)
+        keep[2 * j : 2 * j + 2] = jnp.where(mine, even, odd).reshape(2, 4, 16, 512)
+        send[2 * j : 2 * j + 2] = jnp.where(mine, odd, even).reshape(2, 4, 16, 512)
+
+
+def pair_kernel(keep, got, own, s1, s2, s3):
+    y = lax.axis_index("y")
+    own[...] = keep[:, y] + got[:, y]
+    for by, ref in ((1, s1), (2, s2), (3, s3)):
+        to = lax.rem(y + by, 4)
+        ref[...] = (keep[:, to] + got[:, to]).astype(BF16)
+
+
+def line_kernel(own, r1, r2, r3, out):
+    total = own[...] + r1[...].astype(F32) + r2[...].astype(F32) + r3[...].astype(F32)
+    out[...] = total.astype(BF16)
 
 
 def finish_kernel(count, parts, qkv, out):
@@ -357,11 +370,11 @@
     pieces = [frames] + [turned(frames, by) for by in (1, 2, 3)]
 
     half = jax.ShapeDtypeStruct((1024, 128), BF16)
-    att, inp, tgt, q, k, v, stat = pl.pallas_call(
+    att, inp, tgt, q, k, v, probs = pl.pallas_call(
         front_kernel,
         out_shape=(
             half, jax.ShapeDtypeStruct((1024, 256), BF16), jax.ShapeDtypeStruct((1024, 128), F32),
-            half, half, half, jax.ShapeDtypeStruct((8, 1024), F32),
+            half, half, half, jax.ShapeDtypeStruct((2, 1024, 512), F32),
         ),
         in_specs=[sm()] + [vm()] * 7,
         out_specs=(vm(),) * 7,
@@ -369,23 +382,52 @@
         compiler_params=params(20),
         name="front",
     )(table, *pieces, w, gain, wqkv)
+    hidden, normed = pl.pallas_call(
+        mid_kernel,
+        out_shape=(jax.ShapeDtypeStruct((1024, 1024), F32), jax.ShapeDtypeStruct((1024, 1024), BF16)),
+        in_specs=[vm()] * 3,
+        out_specs=(vm(),) * 2,
+        compiler_params=params(14),
+        cost_estimate=pl.CostEstimate(flops=1 << 29, bytes_accessed=7 << 20, transcendentals=0),
+        name="mid",
+    )(inp, w, gain)
     heads = [att] + [turned(att, by) for by in (1, 2, 3)]
-    terms = jax.ShapeDtypeStruct((32, 16, 512), F32)
+    terms = jax.ShapeDtypeStruct((8, 4, 16, 512), F32)
     keep, send = pl.pallas_call(
         back_kernel,
         out_shape=(terms, terms),
-        in_specs=[sm()] + [vm()] * 15,
+        in_specs=[sm()] + [vm()] * 14,
         out_specs=(vm(), vm()),
         scratch_shapes=[
-            VMEM((1024, 1024), BF16), VMEM((1024, 1024), BF16), VMEM((1024, 128), BF16),
+            VMEM((1024, 1024), BF16), VMEM((1024, 128), BF16),
             VMEM((128, 1024), BF16), VMEM((128, 1024), BF16), VMEM((1024, 128), BF16),
             VMEM((1024, 128), BF16), VMEM((512, 1024), BF16),
         ],
         compiler_params=params(28),
         name="back",
-    )(table, *heads, proj, inp, tgt, w, gain, fgain, vel, q, k, v, stat)
-    pair = (keep + lax.ppermute(send, "c", swap)).astype(BF16)
-    parts = lax.all_to_all(pair, ("z", "y"), 0, 0, tiled=True)
+    )(table, *heads, proj, hidden, normed, tgt, fgain, vel, q, k, v, probs)
+    got = lax.ppermute(send, "c", swap)
+    piece = jax.ShapeDtypeStruct((8, 16, 512), BF16)
+    total, *sends = pl.pallas_call(
+        pair_kernel,
+        out_shape=(jax.ShapeDtypeStruct((8, 16, 512), F32), piece, piece, piece),
+        in_specs=[vm()] * 2,
+        out_specs=(vm(),) * 4,
+        compiler_params=params(8),
+        name="pair",
+    )(keep, got)
+    others = [
+        lax.ppermute(a, "y", [(i, (i + by) % 4) for i in range(4)]) for by, a in zip((1, 2, 3), sends)
+    ]
+    line = pl.pallas_call(
+        line_kernel,
+        out_shape=piece,
+        in_specs=[vm()] * 4,
+        out_specs=vm(),
+        compiler_params=params(8),
+        name="line",
+    )(total, *others)
+    parts = lax.all_to_all(line, "z", 0, 0, tiled=True)
     grad_qkv, grad_out = pl.pallas_call(
         finish_kernel,
         out_shape=(jax.ShapeDtypeStruct((3, 16, 128), F32), jax.ShapeDtypeStruct((16, 128), F32)),

time: 118 us -> 114 us (0.966)
  waiting for transfers between devices: 48.1 us -> 44.2 us
  starting transfers between devices: 36.1 us -> 38.3 us
    all_to_all x1, waiting for transfers between devices: 15.2 us -> 7.11 us  [shards(): parts = lax.all_to_all(line, 'z', 0, 0, tiled=True)]
    ppermute x1 -> x4, starting transfers between devices: 0.09 us -> 5.66 us  [the longest x3 5.57 us: shards(): lax.ppermute(a, 'y', [(i, (i + by) % 4) for i in range(4)])]
    ppermute x1 -> x4, waiting for transfers between devices: 2.65 us -> 8.18 us  [the longest x3 5.53 us: shards(): lax.ppermute(a, 'y', [(i, (i + by) % 4) for i in range(4)])]
    all_to_all x1, starting transfers between devices: 7.61 us -> 4.04 us  [shards(): parts = lax.all_to_all(line, 'z', 0, 0, tiled=True)]
    pallas_call x1, Pallas kernels: 12.8 us -> 10.3 us  [shards(): pl.pallas_call(back_kernel, out_shape=(terms, terms), in_specs=[sm()] + [...]
    pallas_call x0 -> x3, Pallas kernels: none -> 1.91 us  [the longest x1 1.11 us: shards(): pl.pallas_call(mid_kernel, out_shape=(jax.ShapeDtypeStruct((1024, 1024),...]
  transfers between devices with their start and end apart: 13 -> 16, of which waited for: 11 -> 14; matrix products, arithmetic and copies ran while one was open for 3% -> 3% of each run, Pallas kernels for 0% -> 1%
where the time goes in v3:
time: 114 us; the launch traced here: 113 us
  waiting for transfers between devices  44.2 us (39%)
  starting transfers between devices  38.3 us (34%)
  Pallas kernels  24.4 us (21%)
  other arithmetic  2.44 us (2%)
  between operations  2.24 us (2%)
  local copies, waits for them, and re-layouts  1.83 us (2%)
    ppermute x9, waiting for transfers between devices, turned(): return lax.ppermute(a, 'mp', [(i, (i - by) % 4) for i in range(4)])  20 us
    ppermute x9, starting transfers between devices, turned(): return lax.ppermute(a, 'mp', [(i, (i - by) % 4) for i in range(4)])  16.7 us
    all_to_all x1, starting transfers between devices, shards(): lax.all_to_all(packed, ('z', 'y'), 0, 0, tiled=True).reshape(64, SLOT, 128)  11.9 us
    pallas_call x1, Pallas kernels, shards(): pl.pallas_call(back_kernel, out_shape=(terms, terms), in_specs=[sm()] + [...  10.3 us
    all_to_all x1, waiting for transfers between devices, shards(): lax.all_to_all(packed, ('z', 'y'), 0, 0, tiled=True).reshape(64, SLOT, 128)  8.08 us
    pallas_call x1, Pallas kernels, shards(): pl.pallas_call(front_kernel, out_shape=(half, jax.ShapeDtypeStruct((1024,...  7.27 us
    all_to_all x1, waiting for transfers between devices, shards(): parts = lax.all_to_all(line, 'z', 0, 0, tiled=True)  7.11 us
    ppermute x3, starting transfers between devices, shards(): lax.ppermute(a, 'y', [(i, (i + by) % 4) for i in range(4)])  5.57 us
  transfers between devices with their start and end apart: 16, of which 14 were waited for; matrix products, arithmetic and copies ran while one was open for 3% of the time, Pallas kernels for 1%

profile of v3, /device:TPU:8, one launch (start us, length us, event | category | flops | bytes accessed | tf_op | source)
XLA Modules:
  0.0 113.4 jit_solution(13275791489303863025)
XLA Ops:
  0.7 1.6 %share.1.own = bf16[8,56,128]{2,1,0:T(8,128)(2,1)} custom-call(s32[1,4]{1,0:T(1,128)} %utt_hbm.1, s32[1,4]{1,0:T(1,128)} %start_hbm.1, s32[1,4]{1,0:T(1,128)} %size_hbm.1, bf16[8,12800]{1,0:T(8,128)(2,1)} %noise.1, bf16[8,12800]{1,0:T(8,128)(2,1)} %data.1), custom_call_target="tpu_custom_call" | custom-call | tf_op jit(solution)/shard_map/share/pallas_call | solution.py:311
  4.8 1.6 %pack.1 = bf16[32,2,56,128]{3,2,1,0:T(8,128)(2,1)} custom-call(s32[512]{0:T(512)S(1)} %add_select_fusion.bins, bf16[8,56,128]{2,1,0:T(8,128)(2,1)S(1)} %copy-done.1, bf16[8,56,128]{2,1,0:T(8,128)(2,1)S(1)} %collective-permute-done.other), custom_call_target="tpu_custom_call" | custom-call | tf_op jit(solution)/shard_map/pack/pallas_call | solution.py:323
  6.5 11.9 %all-to-all-start = ((bf16[32,2,56,128]{3,2,1,0:T(8,128)(2,1)}), bf16[32,2,56,128]{3,2,1,0:T(8,128)(2,1)S(1)}, u32[]{:S(2)}, u32[]{:S(2)}) async-start(bf16[32,2,56,128]{3,2,1,0:T(8,128)(2,1)} %pack.1), calls=%async_computation | async-start | bytes 1835008 | tf_op jit(solution)/shard_map/all_to_all | solution.py:347
  18.6 1.6 %collective-permute-start.3 = (bf16[128,1024]{1,0:T(8,128)(2,1)}, bf16[128,1024]{1,0:T(8,128)(2,1)}, u32[]{:S(2)}, u32[]{:S(2)}) collective-permute-start(bf16[128,1024]{1,0:T(8,128)(2,1)} %param.23), channel_id=1, source_target_pairs={{0,1},{1,2},{2,3},{3,0},{4,5},{5,6},{6,7},{7,4},{8,9},{9,10},{10,1... | collective-permute-start | bytes 786440 | tf_op jit(solution)/shard_map/ppermute | solution.py:308
  20.1 2.7 %collective-permute-start.2 = (bf16[128,1024]{1,0:T(8,128)(2,1)}, bf16[128,1024]{1,0:T(8,128)(2,1)}, u32[]{:S(2)}, u32[]{:S(2)}) collective-permute-start(bf16[128,1024]{1,0:T(8,128)(2,1)} %param.23), channel_id=1, source_target_pairs={{0,2},{1,3},{2,0},{3,1},{4,6},{5,7},{6,4},{7,5},{8,10},{9,11},{10,... | collective-permute-start | bytes 786440 | tf_op jit(solution)/shard_map/ppermute | solution.py:308
  24.9 3.5 %collective-permute-done.3 = bf16[128,1024]{1,0:T(8,128)(2,1)} collective-permute-done((bf16[128,1024]{1,0:T(8,128)(2,1)}, bf16[128,1024]{1,0:T(8,128)(2,1)}, u32[]{:S(2)}, u32[]{:S(2)}) %collective-permute-start.3) | collective-permute-done | bytes 262176 | tf_op jit(solution)/shard_map/ppermute | solution.py:308
  28.4 6.1 %collective-permute-done.2 = bf16[128,1024]{1,0:T(8,128)(2,1)} collective-permute-done((bf16[128,1024]{1,0:T(8,128)(2,1)}, bf16[128,1024]{1,0:T(8,128)(2,1)}, u32[]{:S(2)}, u32[]{:S(2)}) %collective-permute-start.2) | collective-permute-done | bytes 262176 | tf_op jit(solution)/shard_map/ppermute | solution.py:308
  35.8 8.1 %all-to-all-done = bf16[32,2,56,128]{3,2,1,0:T(8,128)(2,1)S(1)} async-done(((bf16[32,2,56,128]{3,2,1,0:T(8,128)(2,1)}), bf16[32,2,56,128]{3,2,1,0:T(8,128)(2,1)S(1)}, u32[]{:S(2)}, u32[]{:S(2)}) %all-to-all-start) | async-done | bytes 917536 | tf_op jit(solution)/shard_map/all_to_all | solution.py:347
  44.9 1.6 %collective-permute-start.6 = (bf16[256,256]{1,0:T(8,128)(2,1)S(1)}, bf16[256,256]{1,0:T(8,128)(2,1)S(1)}, u32[]{:S(2)}, u32[]{:S(2)}) collective-permute-start(bf16[256,256]{1,0:T(8,128)(2,1)S(1)} %unpack.1.x0), channel_id=1, source_target_pairs={{0,1},{1,2},{2,3},{3,0},{4,5},{5,6},{6,7},{7,4},{8,9},{9,10},{10,1... | collective-permute-start | bytes 393224 | tf_op jit(solution)/shard_map/ppermute | solution.py:308
  46.5 2.7 %collective-permute-start.5 = (bf16[256,256]{1,0:T(8,128)(2,1)S(1)}, bf16[256,256]{1,0:T(8,128)(2,1)S(1)}, u32[]{:S(2)}, u32[]{:S(2)}) collective-permute-start(bf16[256,256]{1,0:T(8,128)(2,1)S(1)} %unpack.1.x0), channel_id=1, source_target_pairs={{0,2},{1,3},{2,0},{3,1},{4,6},{5,7},{6,4},{7,5},{8,10},{9,11},{10,... | collective-permute-start | bytes 393224 | tf_op jit(solution)/shard_map/ppermute | solution.py:308
  50.7 1.6 %collective-permute-done.6.x3 = bf16[256,256]{1,0:T(8,128)(2,1)S(1)} collective-permute-done((bf16[256,256]{1,0:T(8,128)(2,1)S(1)}, bf16[256,256]{1,0:T(8,128)(2,1)S(1)}, u32[]{:S(2)}, u32[]{:S(2)}) %collective-permute-start.6) | collective-permute-done | bytes 131104 | tf_op jit(solution)/shard_map/ppermute | solution.py:308
  54.2 7.3 %front.1 = (bf16[1024,128]{1,0:T(8,128)(2,1)S(1)}, bf16[1024,256]{1,0:T(8,128)(2,1)S(1)}, f32[1024,128]{1,0:T(8,128)S(1)}, bf16[1024,128]{1,0:T(8,128)(2,1)S(1)}...) custom-call(s32[1,16]{1,0:T(1,128)S(1)} %pad_add_fusion.table, ...), custom_call_target="tpu_custom_call" | custom-call | tf_op jit(solution)/shard_map/front/pallas_call | solution.py:373
  61.5 1.5 %collective-permute-start.9 = (bf16[1024,128]{1,0:T(8,128)(2,1)S(1)}, bf16[1024,128]{1,0:T(8,128)(2,1)S(1)}, u32[]{:S(2)}, u32[]{:S(2)}) collective-permute-start(bf16[1024,128]{1,0:T(8,128)(2,1)S(1)} %get-tuple-element.56.a0), channel_id=1, source_target_pairs={{0,1},{1,2},{2,3},{3,0},{4,5},{5,6},{6,7},{7,4},{8,9},{9,10},{10,1... | collective-permute-start | bytes 786440 | tf_op jit(solution)/shard_map/ppermute | solution.py:308
  63.0 2.8 %collective-permute-start.8 = (bf16[1024,128]{1,0:T(8,128)(2,1)S(1)}, bf16[1024,128]{1,0:T(8,128)(2,1)S(1)}, u32[]{:S(2)}, u32[]{:S(2)}) collective-permute-start(bf16[1024,128]{1,0:T(8,128)(2,1)S(1)} %get-tuple-element.56.a0), channel_id=1, source_target_pairs={{0,2},{1,3},{2,0},{3,1},{4,6},{5,7},{6,4},{7,5},{8,10},{9,11},{10,... | collective-permute-start | bytes 786440 | tf_op jit(solution)/shard_map/ppermute | solution.py:308
  67.8 4.1 %collective-permute-done.9.a3 = bf16[1024,128]{1,0:T(8,128)(2,1)S(1)} collective-permute-done((bf16[1024,128]{1,0:T(8,128)(2,1)S(1)}, bf16[1024,128]{1,0:T(8,128)(2,1)S(1)}, u32[]{:S(2)}, u32[]{:S(2)}) %collective-permute-start.9) | collective-permute-done | bytes 262176 | tf_op jit(solution)/shard_map/ppermute | solution.py:308
  71.9 2.8 %collective-permute-done.8.a2 = bf16[1024,128]{1,0:T(8,128)(2,1)S(1)} collective-permute-done((bf16[1024,128]{1,0:T(8,128)(2,1)S(1)}, bf16[1024,128]{1,0:T(8,128)(2,1)S(1)}, u32[]{:S(2)}, u32[]{:S(2)}) %collective-permute-start.8) | collective-permute-done | bytes 262176 | tf_op jit(solution)/shard_map/ppermute | solution.py:308
  74.7 10.3 %back.1 = (f32[8,4,16,512]{3,2,1,0:T(8,128)S(1)}, f32[8,4,16,512]{3,2,1,0:T(8,128)S(1)}) custom-call(s32[1,16]{1,0:T(1,128)S(1)} %pad_add_fusion.table, bf16[1024,128]{1,0:T(8,128)(2,1)S(1)} %get-tuple-element.56.a0, bf16[1024,128]{1,0:T(8,128)(2,1)S(1)} %collective-permute-done.7.a1, bf16[1024,128]{1,0:T(8,128)(2,1)S(1)} %collective-permute-done.8.a2, ...), custom_call_target="tpu_custom_call" | custom-call | tf_op jit(solution)/shard_map/back/pallas_call | solution.py:396
  85.1 2.6 %collective-permute-done.10.got = f32[8,4,16,512]{3,2,1,0:T(8,128)S(1)} collective-permute-done((f32[8,4,16,512]{3,2,1,0:T(8,128)S(1)}, f32[8,4,16,512]{3,2,1,0:T(8,128)S(1)}, u32[]{:S(2)}, u32[]{:S(2)}) %collective-permute-start.10) | collective-permute-done | bytes 1048608 | tf_op jit(solution)/shard_map/ppermute | solution.py:409
  87.8 2.4 %collective-permute-start.11 = (bf16[8,16,512]{2,1,0:T(8,128)(2,1)S(1)}, bf16[8,16,512]{2,1,0:T(8,128)(2,1)S(1)}, u32[]{:S(2)}, u32[]{:S(2)}) collective-permute-start(bf16[8,16,512]{2,1,0:T(8,128)(2,1)S(1)} %get-tuple-element.71), channel_id=1, source_target_pairs={{0,8},{8,16},{16,24},{24,0},{1,9},{9,17},{17,25},{25,1},{2,10},{10... | collective-permute-start | bytes 393224 | tf_op jit(solution)/shard_map/ppermute | solution.py:420
  90.9 2.5 %collective-permute-start.13 = (bf16[8,16,512]{2,1,0:T(8,128)(2,1)S(1)}, bf16[8,16,512]{2,1,0:T(8,128)(2,1)S(1)}, u32[]{:S(2)}, u32[]{:S(2)}) collective-permute-start(bf16[8,16,512]{2,1,0:T(8,128)(2,1)S(1)} %get-tuple-element.73), channel_id=1, source_target_pairs={{0,24},{8,0},{16,8},{24,16},{1,25},{9,1},{17,9},{25,17},{2,26},{10... | collective-permute-start | bytes 393224 | tf_op jit(solution)/shard_map/ppermute | solution.py:420
  93.4 2.7 %collective-permute-done.11.r1 = bf16[8,16,512]{2,1,0:T(8,128)(2,1)S(1)} collective-permute-done((bf16[8,16,512]{2,1,0:T(8,128)(2,1)S(1)}, bf16[8,16,512]{2,1,0:T(8,128)(2,1)S(1)}, u32[]{:S(2)}, u32[]{:S(2)}) %collective-permute-start.11) | collective-permute-done | bytes 131104 | tf_op jit(solution)/shard_map/ppermute | solution.py:420
  96.1 2.0 %collective-permute-done.12.r2 = bf16[8,16,512]{2,1,0:T(8,128)(2,1)S(1)} collective-permute-done((bf16[8,16,512]{2,1,0:T(8,128)(2,1)S(1)}, bf16[8,16,512]{2,1,0:T(8,128)(2,1)S(1)}, u32[]{:S(2)}, u32[]{:S(2)}) %collective-permute-start.12) | collective-permute-done | bytes 131104 | tf_op jit(solution)/shard_map/ppermute | solution.py:420
  99.6 4.0 %all-to-all-start.1 = ((bf16[8,16,512]{2,1,0:T(8,128)(2,1)}), bf16[8,16,512]{2,1,0:T(8,128)(2,1)S(1)}, u32[]{:S(2)}, u32[]{:S(2)}) async-start(bf16[8,16,512]{2,1,0:T(8,128)(2,1)} %line.1), calls=%async_computation.1 | async-start | bytes 262144 | tf_op jit(solution)/shard_map/all_to_all | solution.py:430
  105.6 7.1 %all-to-all-done.1.parts = bf16[8,16,512]{2,1,0:T(8,128)(2,1)S(1)} async-done(((bf16[8,16,512]{2,1,0:T(8,128)(2,1)}), bf16[8,16,512]{2,1,0:T(8,128)(2,1)S(1)}, u32[]{:S(2)}, u32[]{:S(2)}) %all-to-all-start.1) | async-done | bytes 131104 | tf_op jit(solution)/shard_map/all_to_all | solution.py:430
  (56 shorter events, 16.0 us)
Async XLA Ops:
  0.6 23.7 %copy-start.10 = (pred[128]{0:T(512)(128)(4,1)S(1)}, pred[128]{0:T(512)(128)(4,1)}, u32[]{:S(2)}) copy-start(pred[128]{0:T(512)(128)(4,1)} %constant.46.clone.1) | copy-start | bytes 388
  0.7 23.7 %copy-start.2 = (bf16[200,1024]{1,0:T(8,128)(2,1)S(1)}, bf16[200,1024]{1,0:T(8,128)(2,1)}, u32[]{:S(2)}) copy-start(bf16[200,1024]{1,0:T(8,128)(2,1)} %param.20) | copy-start | bytes 1228804
  2.3 22.2 %copy-start.8 = (bf16[1024]{0:T(1024)(128)(2,1)S(1)}, bf16[1024]{0:T(1024)(128)(2,1)}, u32[]{:S(2)}) copy-start(bf16[1024]{0:T(1024)(128)(2,1)} %param.21) | copy-start | bytes 6148
  2.3 22.2 %copy-start.9 = (bf16[1024]{0:T(1024)(128)(2,1)S(1)}, bf16[1024]{0:T(1024)(128)(2,1)}, u32[]{:S(2)}) copy-start(bf16[1024]{0:T(1024)(128)(2,1)} %param.24) | copy-start | bytes 6148
  2.3 1.6 %collective-permute-start = (bf16[8,56,128]{2,1,0:T(8,128)(2,1)}, bf16[8,56,128]{2,1,0:T(8,128)(2,1)S(1)}, u32[]{:S(2)}, u32[]{:S(2)}) collective-permute-start(bf16[8,56,128]{2,1,0:T(8,128)(2,1)} %share.1.own), channel_id=1, source_target_pairs={{0,4},{4,0},{1,5},{5,1},{2,6},{6,2},{3,7},{7,3},{8,12},{12,8},{9,1... | collective-permute-start | bytes 344072 | tf_op jit(solution)/shard_map/ppermute | solution.py:321
  4.8 19.7 %copy-start.3 = (bf16[1024,100]{0,1:T(8,128)(2,1)S(1)}, bf16[1024,100]{0,1:T(8,128)(2,1)}, u32[]{:S(2)}) copy-start(bf16[1024,100]{0,1:T(8,128)(2,1)} %param.25) | copy-start | bytes 614404
  6.4 18.3 %copy-start.5 = (s32[1,4]{1,0:T(1,128)S(1)}, s32[1,4]{1,0:T(1,128)}, u32[]{:S(2)}) copy-start(s32[1,4]{1,0:T(1,128)} %utt_hbm.1) | copy-start | bytes 52
  6.4 18.3 %copy-start.6 = (s32[1,4]{1,0:T(1,128)S(1)}, s32[1,4]{1,0:T(1,128)}, u32[]{:S(2)}) copy-start(s32[1,4]{1,0:T(1,128)} %start_hbm.1) | copy-start | bytes 52
  6.5 37.4 %all-to-all-start = ((bf16[32,2,56,128]{3,2,1,0:T(8,128)(2,1)}), bf16[32,2,56,128]{3,2,1,0:T(8,128)(2,1)S(1)}, u32[]{:S(2)}, u32[]{:S(2)}) async-start(bf16[32,2,56,128]{3,2,1,0:T(8,128)(2,1)} %pack.1), calls=%async_computation | async-start | bytes 1835008 | tf_op jit(solution)/shard_map/all_to_all | solution.py:347
  18.6 9.8 %collective-permute-start.3 = (bf16[128,1024]{1,0:T(8,128)(2,1)}, bf16[128,1024]{1,0:T(8,128)(2,1)}, u32[]{:S(2)}, u32[]{:S(2)}) collective-permute-start(bf16[128,1024]{1,0:T(8,128)(2,1)} %param.23), channel_id=1, source_target_pairs={{0,1},{1,2},{2,3},{3,0},{4,5},{5,6},{6,7},{7,4},{8,9},{9,10},{10,1... | collective-permute-start | bytes 786440 | tf_op jit(solution)/shard_map/ppermute | solution.py:308
  20.1 14.4 %collective-permute-start.2 = (bf16[128,1024]{1,0:T(8,128)(2,1)}, bf16[128,1024]{1,0:T(8,128)(2,1)}, u32[]{:S(2)}, u32[]{:S(2)}) collective-permute-start(bf16[128,1024]{1,0:T(8,128)(2,1)} %param.23), channel_id=1, source_target_pairs={{0,2},{1,3},{2,0},{3,1},{4,6},{5,7},{6,4},{7,5},{8,10},{9,11},{10,... | collective-permute-start | bytes 786440 | tf_op jit(solution)/shard_map/ppermute | solution.py:308
  22.9 11.7 %collective-permute-start.1 = (bf16[128,1024]{1,0:T(8,128)(2,1)}, bf16[128,1024]{1,0:T(8,128)(2,1)}, u32[]{:S(2)}, u32[]{:S(2)}) collective-permute-start(bf16[128,1024]{1,0:T(8,128)(2,1)} %param.23), channel_id=1, source_target_pairs={{0,3},{1,0},{2,1},{3,2},{4,7},{5,4},{6,5},{7,6},{8,11},{9,8},{10,9... | collective-permute-start | bytes 786440 | tf_op jit(solution)/shard_map/ppermute | solution.py:308
  24.8 29.4 %copy-start = (bf16[1024,3,128]{2,0,1:T(8,128)(2,1)S(1)}, bf16[1024,3,128]{2,0,1:T(8,128)(2,1)}, u32[]{:S(2)}) copy-start(bf16[1024,3,128]{2,0,1:T(8,128)(2,1)} %param.22) | copy-start | bytes 2359300
  44.9 7.3 %collective-permute-start.6 = (bf16[256,256]{1,0:T(8,128)(2,1)S(1)}, bf16[256,256]{1,0:T(8,128)(2,1)S(1)}, u32[]{:S(2)}, u32[]{:S(2)}) collective-permute-start(bf16[256,256]{1,0:T(8,128)(2,1)S(1)} %unpack.1.x0), channel_id=1, source_target_pairs={{0,1},{1,2},{2,3},{3,0},{4,5},{5,6},{6,7},{7,4},{8,9},{9,10},{10,1... | collective-permute-start | bytes 393224 | tf_op jit(solution)/shard_map/ppermute | solution.py:308
  46.5 7.2 %collective-permute-start.5 = (bf16[256,256]{1,0:T(8,128)(2,1)S(1)}, bf16[256,256]{1,0:T(8,128)(2,1)S(1)}, u32[]{:S(2)}, u32[]{:S(2)}) collective-permute-start(bf16[256,256]{1,0:T(8,128)(2,1)S(1)} %unpack.1.x0), channel_id=1, source_target_pairs={{0,2},{1,3},{2,0},{3,1},{4,6},{5,7},{6,4},{7,5},{8,10},{9,11},{10,... | collective-permute-start | bytes 393224 | tf_op jit(solution)/shard_map/ppermute | solution.py:308
  49.2 5.0 %collective-permute-start.4 = (bf16[256,256]{1,0:T(8,128)(2,1)S(1)}, bf16[256,256]{1,0:T(8,128)(2,1)S(1)}, u32[]{:S(2)}, u32[]{:S(2)}) collective-permute-start(bf16[256,256]{1,0:T(8,128)(2,1)S(1)} %unpack.1.x0), channel_id=1, source_target_pairs={{0,3},{1,0},{2,1},{3,2},{4,7},{5,4},{6,5},{7,6},{8,11},{9,8},{10,9... | collective-permute-start | bytes 393224 | tf_op jit(solution)/shard_map/ppermute | solution.py:308
  61.5 10.4 %collective-permute-start.9 = (bf16[1024,128]{1,0:T(8,128)(2,1)S(1)}, bf16[1024,128]{1,0:T(8,128)(2,1)S(1)}, u32[]{:S(2)}, u32[]{:S(2)}) collective-permute-start(bf16[1024,128]{1,0:T(8,128)(2,1)S(1)} %get-tuple-element.56.a0), channel_id=1, source_target_pairs={{0,1},{1,2},{2,3},{3,0},{4,5},{5,6},{6,7},{7,4},{8,9},{9,10},{10,1... | collective-permute-start | bytes 786440 | tf_op jit(solution)/shard_map/ppermute | solution.py:308
  63.0 11.7 %collective-permute-start.8 = (bf16[1024,128]{1,0:T(8,128)(2,1)S(1)}, bf16[1024,128]{1,0:T(8,128)(2,1)S(1)}, u32[]{:S(2)}, u32[]{:S(2)}) collective-permute-start(bf16[1024,128]{1,0:T(8,128)(2,1)S(1)} %get-tuple-element.56.a0), channel_id=1, source_target_pairs={{0,2},{1,3},{2,0},{3,1},{4,6},{5,7},{6,4},{7,5},{8,10},{9,11},{10,... | collective-permute-start | bytes 786440 | tf_op jit(solution)/shard_map/ppermute | solution.py:308
  65.8 8.8 %collective-permute-start.7 = (bf16[1024,128]{1,0:T(8,128)(2,1)S(1)}, bf16[1024,128]{1,0:T(8,128)(2,1)S(1)}, u32[]{:S(2)}, u32[]{:S(2)}) collective-permute-start(bf16[1024,128]{1,0:T(8,128)(2,1)S(1)} %get-tuple-element.56.a0), channel_id=1, source_target_pairs={{0,3},{1,0},{2,1},{3,2},{4,7},{5,4},{6,5},{7,6},{8,11},{9,8},{10,9... | collective-permute-start | bytes 786440 | tf_op jit(solution)/shard_map/ppermute | solution.py:308
  85.0 2.7 %collective-permute-start.10 = (f32[8,4,16,512]{3,2,1,0:T(8,128)S(1)}, f32[8,4,16,512]{3,2,1,0:T(8,128)S(1)}, u32[]{:S(2)}, u32[]{:S(2)}) collective-permute-start(f32[8,4,16,512]{3,2,1,0:T(8,128)S(1)} %get-tuple-element.69), channel_id=1, source_target_pairs={{0,4},{4,0},{1,5},{5,1},{2,6},{6,2},{3,7},{7,3},{8,12},{12,8},{9,1... | collective-permute-start | bytes 3145736 | tf_op jit(solution)/shard_map/ppermute | solution.py:409
  87.8 8.3 %collective-permute-start.11 = (bf16[8,16,512]{2,1,0:T(8,128)(2,1)S(1)}, bf16[8,16,512]{2,1,0:T(8,128)(2,1)S(1)}, u32[]{:S(2)}, u32[]{:S(2)}) collective-permute-start(bf16[8,16,512]{2,1,0:T(8,128)(2,1)S(1)} %get-tuple-element.71), channel_id=1, source_target_pairs={{0,8},{8,16},{16,24},{24,0},{1,9},{9,17},{17,25},{25,1},{2,10},{10... | collective-permute-start | bytes 393224 | tf_op jit(solution)/shard_map/ppermute | solution.py:420
  90.2 7.9 %collective-permute-start.12 = (bf16[8,16,512]{2,1,0:T(8,128)(2,1)S(1)}, bf16[8,16,512]{2,1,0:T(8,128)(2,1)S(1)}, u32[]{:S(2)}, u32[]{:S(2)}) collective-permute-start(bf16[8,16,512]{2,1,0:T(8,128)(2,1)S(1)} %get-tuple-element.72), channel_id=1, source_target_pairs={{0,16},{8,24},{16,0},{24,8},{1,17},{9,25},{17,1},{25,9},{2,18},{10... | collective-permute-start | bytes 393224 | tf_op jit(solution)/shard_map/ppermute | solution.py:420
  90.9 8.1 %collective-permute-start.13 = (bf16[8,16,512]{2,1,0:T(8,128)(2,1)S(1)}, bf16[8,16,512]{2,1,0:T(8,128)(2,1)S(1)}, u32[]{:S(2)}, u32[]{:S(2)}) collective-permute-start(bf16[8,16,512]{2,1,0:T(8,128)(2,1)S(1)} %get-tuple-element.73), channel_id=1, source_target_pairs={{0,24},{8,0},{16,8},{24,16},{1,25},{9,1},{17,9},{25,17},{2,26},{10... | collective-permute-start | bytes 393224 | tf_op jit(solution)/shard_map/ppermute | solution.py:420
  99.6 13.1 %all-to-all-start.1 = ((bf16[8,16,512]{2,1,0:T(8,128)(2,1)}), bf16[8,16,512]{2,1,0:T(8,128)(2,1)S(1)}, u32[]{:S(2)}, u32[]{:S(2)}) async-start(bf16[8,16,512]{2,1,0:T(8,128)(2,1)} %line.1), calls=%async_computation.1 | async-start | bytes 262144 | tf_op jit(solution)/shard_map/all_to_all | solution.py:430
  (4 other events, 55.3 us)

commit v4 on v3

--- a/solution.py
+++ b/solution.py
@@ -1,3 +1,5 @@
+import functools
+
 import jax
 import jax.numpy as jnp
 from jax import lax
@@ -41,7 +43,7 @@
 
 
 def params(mib):
-    return pltpu.CompilerParams(vmem_limit_bytes=mib << 20)
+    return pltpu.CompilerParams(vmem_limit_bytes=int(mib * (1 << 20)))
 
 
 def device():
@@ -158,39 +160,50 @@
     return (lane < HEAD) if h == 0 else (lane >= HEAD)
 
 
+def piece_of(step, table, spans, x, w, gain, wqkv, inp, tgt):
+    part = lax.rem(lax.axis_index("mp") + step, 4)
+    row = lax.broadcasted_iota(jnp.int32, (256, 128), 0)
+    frame = (row >> 5) * BLOCK + part * 32 + (row & 31)
+    lev = jnp.zeros((256, 128), F32)
+    for u, (begin, end, _, _) in enumerate(spans):
+        inside = (frame >= begin) & (frame < end)
+        lev = jnp.where(inside, table[0, 12 + u].astype(F32) / 64.0, lev)
+    noise, data = x[:, :128].astype(F32), x[:, 128:].astype(F32)
+    noisy = (1.0 - lev) * noise + lev * data
+    cond = jnp.where(masked_of(frame, spans), 0.0, data)
+    both = jnp.concatenate([noisy, cond], axis=1).astype(BF16)
+    inp[...] = both
+    tgt[...] = data - noise
+    h = dot(both, w[...])
+    scale = lax.rsqrt(jnp.mean(h * h, axis=1, keepdims=True) + EPS)
+    weights = jnp.concatenate([wqkv[0], wqkv[1], wqkv[2]], axis=1)
+    out = dot((h * scale * gain[...]).astype(BF16), weights)
+    query = (out[:, 0:128].astype(BF16).astype(F32) * HEAD ** (-0.5)).astype(BF16)
+    return query, out[:, 128:256].astype(BF16), out[:, 256:].astype(BF16)
+
+
+def piece_kernel(step, table, x, w, gain, wqkv, inp, tgt, qkv):
+    out = piece_of(step, table, utterances(table), x, w, gain, wqkv, inp, tgt)
+    for j in range(3):
+        qkv[:, j * 128 : (j + 1) * 128] = out[j]
+
+
+def piece_rows(step):
+    part = lax.rem(lax.axis_index("mp") + step, 4)
+    return [(b * 32, pl.ds(pl.multiple_of(b * BLOCK + part * 32, 32), 32)) for b in range(8)]
+
+
 def front_kernel(
-    table, x0, x1, x2, x3, w, gain, wqkv,
-    att, inp, tgt, q, k, v, probs_out, vt, attt,
+    table, p0, p1, x2, x3, w, gain, wqkv, att, q, k, v, probs_out, i2, i3, t2, t3, vt, attt
 ):
     spans = utterances(table)
-    for step, x in enumerate((x0, x1, x2, x3)):
-        part = lax.rem(lax.axis_index("mp") + step, 4)
-        row = lax.broadcasted_iota(jnp.int32, (256, 128), 0)
-        frame = (row >> 5) * BLOCK + part * 32 + (row & 31)
-        lev = jnp.zeros((256, 128), F32)
-        for u, (begin, end, _, _) in enumerate(spans):
-            inside = (frame >= begin) & (frame < end)
-            lev = jnp.where(inside, table[0, 12 + u].astype(F32) / 64.0, lev)
-        noise, data = x[:, :128].astype(F32), x[:, 128:].astype(F32)
-        noisy = (1.0 - lev) * noise + lev * data
-        cond = jnp.where(masked_of(frame, spans), 0.0, data)
-        both = jnp.concatenate([noisy, cond], axis=1).astype(BF16)
-        diff = data - noise
-        for b in range(8):
-            at = pl.ds(pl.multiple_of(b * BLOCK + part * 32, 32), 32)
-            inp[at, :] = both[b * 32 : b * 32 + 32]
-            tgt[at, :] = diff[b * 32 : b * 32 + 32]
-
-    qkv = jnp.concatenate([wqkv[0], wqkv[1], wqkv[2]], axis=1)
-    for i in range(4):
-        rows = pl.ds(i * 256, 256)
-        h = dot(inp[rows, :], w[...])
-        scale = lax.rsqrt(jnp.mean(h * h, axis=1, keepdims=True) + EPS)
-        out = dot((h * scale * gain[...]).astype(BF16), qkv)
-        q[rows, :] = (out[:, :128].astype(BF16).astype(F32) * HEAD ** (-0.5)).astype(BF16)
-        k[rows, :] = out[:, 128:256].astype(BF16)
-        v[rows, :] = out[:, 256:].astype(BF16)
-
+    late = ((2, x2, i2, t2), (3, x3, i3, t3))
+    made = [piece_of(step, table, spans, x, w, gain, wqkv, i, t) for step, x, i, t in late]
+    early = [[p[:, j * 128 : (j + 1) * 128] for j in range(3)] for p in (p0, p1)]
+    for step, piece in enumerate(early + made):
+        for r, at in piece_rows(step):
+            for ref, rows in zip((q, k, v), piece):
+                ref[at, :] = rows[r : r + 32]
     vt[...] = v[...].T
 
     def one(first, rows):
@@ -210,24 +223,33 @@
     att[...] = attt[...].T
 
 
-def mid_kernel(inp, w, gain, hidden, normed):
+def mid_kernel(i0, i1, i2, i3, t0, t1, t2, t3, w, gain, hidden, normed, tgt):
+    for step, (inp, target) in enumerate(((i0, t0), (i1, t1), (i2, t2), (i3, t3))):
+        h = dot(inp[...], w[...])
+        scale = lax.rsqrt(jnp.mean(h * h, axis=1, keepdims=True) + EPS)
+        n = (h * scale * gain[...]).astype(BF16)
+        for r, at in piece_rows(step):
+            hidden[at, :] = h[r : r + 32]
+            normed[at, :] = n[r : r + 32]
+            tgt[at, :] = target[r : r + 32, :]
+
+
+def mix_kernel(hidden, a0, a3, proj, out):
+    weights = jnp.concatenate([proj[0:128, :], proj[384:512, :]], axis=0)
     for i in range(4):
         rows = pl.ds(i * 256, 256)
-        h = dot(inp[rows, :], w[...])
-        hidden[rows, :] = h
-        scale = lax.rsqrt(jnp.mean(h * h, axis=1, keepdims=True) + EPS)
-        normed[rows, :] = (h * scale * gain[...]).astype(BF16)
+        out[rows, :] = hidden[rows, :] + dot(jnp.concatenate([a0[rows, :], a3[rows, :]], axis=1), weights)
 
 
 def back_kernel(
-    table, a0, a1, a2, a3, proj, hidden, normed, tgt, fgain, vel, q, k, v, probs,
+    table, a0, a1, a2, proj, hidden, normed, tgt, fgain, vel, q, k, v, probs,
     keep, send, back1, dout, kt, dqt, dk, dv, lhs,
 ):
     spans = utterances(table)
     for i in range(4):
         rows = pl.ds(i * 256, 256)
-        groups = jnp.concatenate([a0[rows, :], a1[rows, :], a2[rows, :], a3[rows, :]], axis=1)
-        wide = (hidden[rows, :] + dot(groups, proj[...])).astype(BF16).astype(F32)
+        groups = jnp.concatenate([a1[rows, :], a2[rows, :]], axis=1)
+        wide = (hidden[rows, :] + dot(groups, proj[128:384, :])).astype(BF16).astype(F32)
         rscale = lax.rsqrt(jnp.mean(wide * wide, axis=1, keepdims=True) + EPS)
         normalized = wide * rscale
         final = (normalized * fgain[...]).astype(BF16)
@@ -274,15 +296,15 @@
         terms = jnp.concatenate([top.T, low.T], axis=1).reshape(8, 2, 16, 512)
         even, odd = terms[:, 0], terms[:, 1]
         keep[2 * j : 2 * j + 2] = jnp.where(mine, even, odd).reshape(2, 4, 16, 512)
-        send[2 * j : 2 * j + 2] = jnp.where(mine, odd, even).reshape(2, 4, 16, 512)
+        send[2 * j : 2 * j + 2] = jnp.where(mine, odd, even).reshape(2, 4, 16, 512).astype(BF16)
 
 
 def pair_kernel(keep, got, own, s1, s2, s3):
     y = lax.axis_index("y")
-    own[...] = keep[:, y] + got[:, y]
+    own[...] = keep[:, y] + got[:, y].astype(F32)
     for by, ref in ((1, s1), (2, s2), (3, s3)):
         to = lax.rem(y + by, 4)
-        ref[...] = (keep[:, to] + got[:, to]).astype(BF16)
+        ref[...] = (keep[:, to] + got[:, to].astype(F32)).astype(BF16)
 
 
 def line_kernel(own, r1, r2, r3, out):
@@ -370,33 +392,62 @@
     pieces = [frames] + [turned(frames, by) for by in (1, 2, 3)]
 
     half = jax.ShapeDtypeStruct((1024, 128), BF16)
-    att, inp, tgt, q, k, v, probs = pl.pallas_call(
+
+    def cost(flops, size):
+        return pl.CostEstimate(flops=flops, bytes_accessed=size, transcendentals=0)
+
+    def piece(step, frames):
+        return pl.pallas_call(
+            functools.partial(piece_kernel, step),
+            out_shape=(
+                jax.ShapeDtypeStruct((256, 256), BF16), jax.ShapeDtypeStruct((256, 128), F32),
+                jax.ShapeDtypeStruct((256, 384), BF16),
+            ),
+            in_specs=[sm()] + [vm()] * 4,
+            out_specs=(vm(),) * 3,
+            compiler_params=params(12),
+            cost_estimate=cost(1 << 29, 2 << 20),
+            name=f"piece{step}",
+        )(table, frames, w, gain, wqkv)
+
+    first = [piece(step, pieces[step]) for step in (0, 1)]
+    att, q, k, v, probs, *late = pl.pallas_call(
         front_kernel,
-        out_shape=(
-            half, jax.ShapeDtypeStruct((1024, 256), BF16), jax.ShapeDtypeStruct((1024, 128), F32),
-            half, half, half, jax.ShapeDtypeStruct((2, 1024, 512), F32),
-        ),
+        out_shape=(half, half, half, half, jax.ShapeDtypeStruct((2, 1024, 512), F32))
+        + (jax.ShapeDtypeStruct((256, 256), BF16),) * 2 + (jax.ShapeDtypeStruct((256, 128), F32),) * 2,
         in_specs=[sm()] + [vm()] * 7,
-        out_specs=(vm(),) * 7,
+        out_specs=(vm(),) * 9,
         scratch_shapes=[VMEM((128, 1024), BF16), VMEM((128, 1024), BF16)],
         compiler_params=params(20),
         name="front",
-    )(table, *pieces, w, gain, wqkv)
-    hidden, normed = pl.pallas_call(
+    )(table, first[0][2], first[1][2], pieces[2], pieces[3], w, gain, wqkv)
+    inp = (first[0][0], first[1][0], late[0], late[1])
+    tgt = (first[0][1], first[1][1], late[2], late[3])
+    heads = [att] + [turned(att, by) for by in (1, 2, 3)]
+    full = jax.ShapeDtypeStruct((1024, 1024), F32)
+    hidden, normed, target = pl.pallas_call(
         mid_kernel,
-        out_shape=(jax.ShapeDtypeStruct((1024, 1024), F32), jax.ShapeDtypeStruct((1024, 1024), BF16)),
-        in_specs=[vm()] * 3,
-        out_specs=(vm(),) * 2,
+        out_shape=(full, jax.ShapeDtypeStruct((1024, 1024), BF16), jax.ShapeDtypeStruct((1024, 128), F32)),
+        in_specs=[vm()] * 10,
+        out_specs=(vm(),) * 3,
         compiler_params=params(14),
-        cost_estimate=pl.CostEstimate(flops=1 << 29, bytes_accessed=7 << 20, transcendentals=0),
+        cost_estimate=cost(1 << 29, 7 << 20),
         name="mid",
-    )(inp, w, gain)
-    heads = [att] + [turned(att, by) for by in (1, 2, 3)]
-    terms = jax.ShapeDtypeStruct((8, 4, 16, 512), F32)
+    )(*inp, *tgt, w, gain)
+    hidden = pl.pallas_call(
+        mix_kernel,
+        out_shape=full,
+        in_specs=[vm()] * 4,
+        out_specs=vm(),
+        input_output_aliases={0: 0},
+        compiler_params=params(14),
+        cost_estimate=cost(1 << 29, 7 << 20),
+        name="mix",
+    )(hidden, heads[0], heads[3], proj)
     keep, send = pl.pallas_call(
         back_kernel,
-        out_shape=(terms, terms),
-        in_specs=[sm()] + [vm()] * 14,
+        out_shape=tuple(jax.ShapeDtypeStruct((8, 4, 16, 512), t) for t in (F32, BF16)),
+        in_specs=[sm()] + [vm()] * 13,
         out_specs=(vm(), vm()),
         scratch_shapes=[
             VMEM((1024, 1024), BF16), VMEM((1024, 128), BF16),
@@ -405,7 +456,7 @@
         ],
         compiler_params=params(28),
         name="back",
-    )(table, *heads, proj, hidden, normed, tgt, fgain, vel, q, k, v, probs)
+    )(table, *heads[:3], proj, hidden, normed, target, fgain, vel, q, k, v, probs)
     got = lax.ppermute(send, "c", swap)
     piece = jax.ShapeDtypeStruct((8, 16, 512), BF16)
     total, *sends = pl.pallas_call(

time: 114 us -> 111 us (0.974)
  waiting for transfers between devices: 44.2 us -> 42 us
  starting transfers between devices: 38.3 us -> 36.5 us
  Pallas kernels: 24.4 us -> 26 us
    ppermute x9, starting transfers between devices: 16.7 us -> 14.9 us  [turned(): return lax.ppermute(a, 'mp', [(i, (i - by) % 4) for i in range(4)])]
    pallas_call x3 -> x6, Pallas kernels: 18.6 us -> 20.2 us  [the longest x1 9.41 us: shards(): pl.pallas_call(back_kernel, out_shape=tuple((jax.ShapeDtypeStruct((8, 4,...]
    ppermute x9, waiting for transfers between devices: 20 us -> 18.6 us  [turned(): return lax.ppermute(a, 'mp', [(i, (i - by) % 4) for i in range(4)])]
  transfers between devices with their start and end apart: 16 -> 16, of which waited for: 14 -> 14; matrix products, arithmetic and copies ran while one was open for 3% -> 3% of each run, Pallas kernels for 1% -> 5%
where the time goes in v4:
time: 111 us
  waiting for transfers between devices  42 us (38%)
  starting transfers between devices  36.5 us (33%)
  Pallas kernels  26 us (23%)
  other arithmetic  2.44 us (2%)
  between operations  2.26 us (2%)
  local copies, waits for them, and re-layouts  1.83 us (2%)
    ppermute x9, waiting for transfers between devices, turned(): return lax.ppermute(a, 'mp', [(i, (i - by) % 4) for i in range(4)])  18.6 us
    ppermute x9, starting transfers between devices, turned(): return lax.ppermute(a, 'mp', [(i, (i - by) % 4) for i in range(4)])  14.9 us
    all_to_all x1, starting transfers between devices, shards(): lax.all_to_all(packed, ('z', 'y'), 0, 0, tiled=True).reshape(64, SLOT, 128)  11.9 us
    pallas_call x1, Pallas kernels, shards(): pl.pallas_call(back_kernel, out_shape=tuple((jax.ShapeDtypeStruct((8, 4,...  9.41 us
    all_to_all x1, waiting for transfers between devices, shards(): lax.all_to_all(packed, ('z', 'y'), 0, 0, tiled=True).reshape(64, SLOT, 128)  8.08 us
    all_to_all x1, waiting for transfers between devices, shards(): parts = lax.all_to_all(line, 'z', 0, 0, tiled=True)  7.11 us
    ppermute x3, starting transfers between devices, shards(): lax.ppermute(a, 'y', [(i, (i + by) % 4) for i in range(4)])  5.94 us
    pallas_call x1, Pallas kernels, shards(): pl.pallas_call(front_kernel, out_shape=(half, half, half, half, jax.Shape...  5.81 us
  transfers between devices with their start and end apart: 16, of which 14 were waited for; matrix products, arithmetic and copies ran while one was open for 3% of the time, Pallas kernels for 5%

profile of v4, /device:TPU:8, one launch (start us, length us, event | category | flops | bytes accessed | tf_op | source)
XLA Modules:
  0.0 111.1 jit_solution(15714698919721006113)
XLA Ops:
  0.7 1.6 %share.1.own = bf16[8,56,128]{2,1,0:T(8,128)(2,1)} custom-call(s32[1,4]{1,0:T(1,128)} %utt_hbm.1, s32[1,4]{1,0:T(1,128)} %start_hbm.1, s32[1,4]{1,0:T(1,128)} %size_hbm.1, bf16[8,12800]{1,0:T(8,128)(2,1)} %noise.1, bf16[8,12800]{1,0:T(8,128)(2,1)} %data.1), custom_call_target="tpu_custom_call" | custom-call | tf_op jit(solution)/shard_map/share/pallas_call | solution.py:333
  4.8 1.6 %pack.1 = bf16[32,2,56,128]{3,2,1,0:T(8,128)(2,1)} custom-call(s32[512]{0:T(512)S(1)} %add_select_fusion.bins, bf16[8,56,128]{2,1,0:T(8,128)(2,1)S(1)} %copy-done.1, bf16[8,56,128]{2,1,0:T(8,128)(2,1)S(1)} %collective-permute-done.other), custom_call_target="tpu_custom_call" | custom-call | tf_op jit(solution)/shard_map/pack/pallas_call | solution.py:345
  6.5 11.9 %all-to-all-start = ((bf16[32,2,56,128]{3,2,1,0:T(8,128)(2,1)}), bf16[32,2,56,128]{3,2,1,0:T(8,128)(2,1)S(1)}, u32[]{:S(2)}, u32[]{:S(2)}) async-start(bf16[32,2,56,128]{3,2,1,0:T(8,128)(2,1)} %pack.1), calls=%async_computation | async-start | bytes 1835008 | tf_op jit(solution)/shard_map/all_to_all | solution.py:369
  18.6 1.6 %collective-permute-start.3 = (bf16[128,1024]{1,0:T(8,128)(2,1)}, bf16[128,1024]{1,0:T(8,128)(2,1)}, u32[]{:S(2)}, u32[]{:S(2)}) collective-permute-start(bf16[128,1024]{1,0:T(8,128)(2,1)} %param.23), channel_id=1, source_target_pairs={{0,1},{1,2},{2,3},{3,0},{4,5},{5,6},{6,7},{7,4},{8,9},{9,10},{10,1... | collective-permute-start | bytes 786440 | tf_op jit(solution)/shard_map/ppermute | solution.py:330
  20.2 2.7 %collective-permute-start.2 = (bf16[128,1024]{1,0:T(8,128)(2,1)}, bf16[128,1024]{1,0:T(8,128)(2,1)}, u32[]{:S(2)}, u32[]{:S(2)}) collective-permute-start(bf16[128,1024]{1,0:T(8,128)(2,1)} %param.23), channel_id=1, source_target_pairs={{0,2},{1,3},{2,0},{3,1},{4,6},{5,7},{6,4},{7,5},{8,10},{9,11},{10,... | collective-permute-start | bytes 786440 | tf_op jit(solution)/shard_map/ppermute | solution.py:330
  22.9 1.4 %collective-permute-start.1 = (bf16[128,1024]{1,0:T(8,128)(2,1)}, bf16[128,1024]{1,0:T(8,128)(2,1)}, u32[]{:S(2)}, u32[]{:S(2)}) collective-permute-start(bf16[128,1024]{1,0:T(8,128)(2,1)} %param.23), channel_id=1, source_target_pairs={{0,3},{1,0},{2,1},{3,2},{4,7},{5,4},{6,5},{7,6},{8,11},{9,8},{10,9... | collective-permute-start | bytes 786440 | tf_op jit(solution)/shard_map/ppermute | solution.py:330
  25.0 3.5 %collective-permute-done.3 = bf16[128,1024]{1,0:T(8,128)(2,1)} collective-permute-done((bf16[128,1024]{1,0:T(8,128)(2,1)}, bf16[128,1024]{1,0:T(8,128)(2,1)}, u32[]{:S(2)}, u32[]{:S(2)}) %collective-permute-start.3) | collective-permute-done | bytes 262176 | tf_op jit(solution)/shard_map/ppermute | solution.py:330
  28.5 6.2 %collective-permute-done.2 = bf16[128,1024]{1,0:T(8,128)(2,1)} collective-permute-done((bf16[128,1024]{1,0:T(8,128)(2,1)}, bf16[128,1024]{1,0:T(8,128)(2,1)}, u32[]{:S(2)}, u32[]{:S(2)}) %collective-permute-start.2) | collective-permute-done | bytes 262176 | tf_op jit(solution)/shard_map/ppermute | solution.py:330
  35.9 8.1 %all-to-all-done = bf16[32,2,56,128]{3,2,1,0:T(8,128)(2,1)S(1)} async-done(((bf16[32,2,56,128]{3,2,1,0:T(8,128)(2,1)}), bf16[32,2,56,128]{3,2,1,0:T(8,128)(2,1)S(1)}, u32[]{:S(2)}, u32[]{:S(2)}) %all-to-all-start) | async-done | bytes 917536 | tf_op jit(solution)/shard_map/all_to_all | solution.py:369
  45.0 2.8 %collective-permute-start.4 = (bf16[256,256]{1,0:T(8,128)(2,1)S(1)}, bf16[256,256]{1,0:T(8,128)(2,1)S(1)}, u32[]{:S(2)}, u32[]{:S(2)}) collective-permute-start(bf16[256,256]{1,0:T(8,128)(2,1)S(1)} %unpack.1.x), channel_id=1, source_target_pairs={{0,3},{1,0},{2,1},{3,2},{4,7},{5,4},{6,5},{7,6},{8,11},{9,8},{10,9... | collective-permute-start | bytes 393224 | tf_op jit(solution)/shard_map/ppermute | solution.py:330
  47.8 2.3 %collective-permute-start.5 = (bf16[256,256]{1,0:T(8,128)(2,1)S(1)}, bf16[256,256]{1,0:T(8,128)(2,1)S(1)}, u32[]{:S(2)}, u32[]{:S(2)}) collective-permute-start(bf16[256,256]{1,0:T(8,128)(2,1)S(1)} %unpack.1.x), channel_id=1, source_target_pairs={{0,2},{1,3},{2,0},{3,1},{4,6},{5,7},{6,4},{7,5},{8,10},{9,11},{10,... | collective-permute-start | bytes 393224 | tf_op jit(solution)/shard_map/ppermute | solution.py:330
  53.2 2.2 %collective-permute-done.6.x3 = bf16[256,256]{1,0:T(8,128)(2,1)S(1)} collective-permute-done((bf16[256,256]{1,0:T(8,128)(2,1)S(1)}, bf16[256,256]{1,0:T(8,128)(2,1)S(1)}, u32[]{:S(2)}, u32[]{:S(2)}) %collective-permute-start.6) | collective-permute-done | bytes 131104 | tf_op jit(solution)/shard_map/ppermute | solution.py:330
  55.4 5.8 %front.1 = (bf16[1024,128]{1,0:T(8,128)(2,1)S(1)}, bf16[1024,128]{1,0:T(8,128)(2,1)S(1)}, bf16[1024,128]{1,0:T(8,128)(2,1)S(1)}, bf16[1024,128]{1,0:T(8,128)(2,1...) custom-call(s32[1,16]{1,0:T(1,128)S(1)} %pad_add_fusion.table, ...), custom_call_target="tpu_custom_call" | custom-call | tf_op jit(solution)/shard_map/front/pallas_call | solution.py:414
  61.5 3.6 %collective-permute-start.8 = (bf16[1024,128]{1,0:T(8,128)(2,1)S(1)}, bf16[1024,128]{1,0:T(8,128)(2,1)S(1)}, u32[]{:S(2)}, u32[]{:S(2)}) collective-permute-start(bf16[1024,128]{1,0:T(8,128)(2,1)S(1)} %get-tuple-element.67.a0), channel_id=1, source_target_pairs={{0,2},{1,3},{2,0},{3,1},{4,6},{5,7},{6,4},{7,5},{8,10},{9,11},{10,... | collective-permute-start | bytes 786440 | tf_op jit(solution)/shard_map/ppermute | solution.py:330
  66.5 4.2 %collective-permute-done.9.a3 = bf16[1024,128]{1,0:T(8,128)(2,1)S(1)} collective-permute-done((bf16[1024,128]{1,0:T(8,128)(2,1)S(1)}, bf16[1024,128]{1,0:T(8,128)(2,1)S(1)}, u32[]{:S(2)}, u32[]{:S(2)}) %collective-permute-start.9) | collective-permute-done | bytes 262176 | tf_op jit(solution)/shard_map/ppermute | solution.py:330
  71.6 1.9 %collective-permute-done.8.a2 = bf16[1024,128]{1,0:T(8,128)(2,1)S(1)} collective-permute-done((bf16[1024,128]{1,0:T(8,128)(2,1)S(1)}, bf16[1024,128]{1,0:T(8,128)(2,1)S(1)}, u32[]{:S(2)}, u32[]{:S(2)}) %collective-permute-start.8) | collective-permute-done | bytes 262176 | tf_op jit(solution)/shard_map/ppermute | solution.py:330
  74.0 9.4 %back.1 = (f32[8,4,16,512]{3,2,1,0:T(8,128)S(1)}, bf16[8,4,16,512]{3,2,1,0:T(8,128)(2,1)S(1)}) custom-call(s32[1,16]{1,0:T(1,128)S(1)} %pad_add_fusion.table, bf16[1024,128]{1,0:T(8,128)(2,1)S(1)} %get-tuple-element.67.a0, bf16[1024,128]{1,0:T(8,128)(2,1)S(1)} %collective-permute-done.7.a1, bf16[1024,128]{1,0:T(8,128)(2,1)S(1)} %collective-permute-done.8.a2, ...), custom_call_target="tpu_custom_call" | custom-call | tf_op jit(solution)/shard_map/back/pallas_call | solution.py:447
  83.7 1.9 %collective-permute-done.10.got = bf16[8,4,16,512]{3,2,1,0:T(8,128)(2,1)S(1)} collective-permute-done((bf16[8,4,16,512]{3,2,1,0:T(8,128)(2,1)S(1)}, bf16[8,4,16,512]{3,2,1,0:T(8,128)(2,1)S(1)}, u32[]{:S(2)}, u32[]{:S(2)}) %collective-permute-start.10) | collective-permute-done | bytes 524320 | tf_op jit(solution)/shard_map/ppermute | solution.py:460
  85.7 2.7 %collective-permute-start.11 = (bf16[8,16,512]{2,1,0:T(8,128)(2,1)S(1)}, bf16[8,16,512]{2,1,0:T(8,128)(2,1)S(1)}, u32[]{:S(2)}, u32[]{:S(2)}) collective-permute-start(bf16[8,16,512]{2,1,0:T(8,128)(2,1)S(1)} %get-tuple-element.89), channel_id=1, source_target_pairs={{0,8},{8,16},{16,24},{24,0},{1,9},{9,17},{17,25},{25,1},{2,10},{10... | collective-permute-start | bytes 393224 | tf_op jit(solution)/shard_map/ppermute | solution.py:471
  89.1 2.5 %collective-permute-start.13 = (bf16[8,16,512]{2,1,0:T(8,128)(2,1)S(1)}, bf16[8,16,512]{2,1,0:T(8,128)(2,1)S(1)}, u32[]{:S(2)}, u32[]{:S(2)}) collective-permute-start(bf16[8,16,512]{2,1,0:T(8,128)(2,1)S(1)} %get-tuple-element.91), channel_id=1, source_target_pairs={{0,24},{8,0},{16,8},{24,16},{1,25},{9,1},{17,9},{25,17},{2,26},{10... | collective-permute-start | bytes 393224 | tf_op jit(solution)/shard_map/ppermute | solution.py:471
  91.7 2.7 %collective-permute-done.11.r1 = bf16[8,16,512]{2,1,0:T(8,128)(2,1)S(1)} collective-permute-done((bf16[8,16,512]{2,1,0:T(8,128)(2,1)S(1)}, bf16[8,16,512]{2,1,0:T(8,128)(2,1)S(1)}, u32[]{:S(2)}, u32[]{:S(2)}) %collective-permute-start.11) | collective-permute-done | bytes 131104 | tf_op jit(solution)/shard_map/ppermute | solution.py:471
  94.3 2.0 %collective-permute-done.12.r2 = bf16[8,16,512]{2,1,0:T(8,128)(2,1)S(1)} collective-permute-done((bf16[8,16,512]{2,1,0:T(8,128)(2,1)S(1)}, bf16[8,16,512]{2,1,0:T(8,128)(2,1)S(1)}, u32[]{:S(2)}, u32[]{:S(2)}) %collective-permute-start.12) | collective-permute-done | bytes 131104 | tf_op jit(solution)/shard_map/ppermute | solution.py:471
  97.9 3.4 %all-to-all-start.1 = ((bf16[8,16,512]{2,1,0:T(8,128)(2,1)}), bf16[8,16,512]{2,1,0:T(8,128)(2,1)S(1)}, u32[]{:S(2)}, u32[]{:S(2)}) async-start(bf16[8,16,512]{2,1,0:T(8,128)(2,1)} %line.1), calls=%async_computation.1 | async-start | bytes 262144 | tf_op jit(solution)/shard_map/all_to_all | solution.py:481
  103.3 7.1 %all-to-all-done.1.parts = bf16[8,16,512]{2,1,0:T(8,128)(2,1)S(1)} async-done(((bf16[8,16,512]{2,1,0:T(8,128)(2,1)}), bf16[8,16,512]{2,1,0:T(8,128)(2,1)S(1)}, u32[]{:S(2)}, u32[]{:S(2)}) %all-to-all-start.1) | async-done | bytes 131104 | tf_op jit(solution)/shard_map/all_to_all | solution.py:481
  (59 shorter events, 15.7 us)
Async XLA Ops:
  0.6 23.7 %copy-start.10 = (pred[128]{0:T(512)(128)(4,1)S(1)}, pred[128]{0:T(512)(128)(4,1)}, u32[]{:S(2)}) copy-start(pred[128]{0:T(512)(128)(4,1)} %constant.46.clone.1) | copy-start | bytes 388
  0.7 23.7 %copy-start.2 = (bf16[200,1024]{1,0:T(8,128)(2,1)S(1)}, bf16[200,1024]{1,0:T(8,128)(2,1)}, u32[]{:S(2)}) copy-start(bf16[200,1024]{1,0:T(8,128)(2,1)} %param.20) | copy-start | bytes 1228804
  2.3 22.2 %copy-start.8 = (bf16[1024]{0:T(1024)(128)(2,1)S(1)}, bf16[1024]{0:T(1024)(128)(2,1)}, u32[]{:S(2)}) copy-start(bf16[1024]{0:T(1024)(128)(2,1)} %param.21) | copy-start | bytes 6148
  2.3 22.2 %copy-start.9 = (bf16[1024]{0:T(1024)(128)(2,1)S(1)}, bf16[1024]{0:T(1024)(128)(2,1)}, u32[]{:S(2)}) copy-start(bf16[1024]{0:T(1024)(128)(2,1)} %param.24) | copy-start | bytes 6148
  2.3 1.6 %collective-permute-start = (bf16[8,56,128]{2,1,0:T(8,128)(2,1)}, bf16[8,56,128]{2,1,0:T(8,128)(2,1)S(1)}, u32[]{:S(2)}, u32[]{:S(2)}) collective-permute-start(bf16[8,56,128]{2,1,0:T(8,128)(2,1)} %share.1.own), channel_id=1, source_target_pairs={{0,4},{4,0},{1,5},{5,1},{2,6},{6,2},{3,7},{7,3},{8,12},{12,8},{9,1... | collective-permute-start | bytes 344072 | tf_op jit(solution)/shard_map/ppermute | solution.py:343
  4.8 19.7 %copy-start.3 = (bf16[1024,100]{0,1:T(8,128)(2,1)S(1)}, bf16[1024,100]{0,1:T(8,128)(2,1)}, u32[]{:S(2)}) copy-start(bf16[1024,100]{0,1:T(8,128)(2,1)} %param.25) | copy-start | bytes 614404
  6.5 18.3 %copy-start.5 = (s32[1,4]{1,0:T(1,128)S(1)}, s32[1,4]{1,0:T(1,128)}, u32[]{:S(2)}) copy-start(s32[1,4]{1,0:T(1,128)} %utt_hbm.1) | copy-start | bytes 52
  6.5 18.3 %copy-start.6 = (s32[1,4]{1,0:T(1,128)S(1)}, s32[1,4]{1,0:T(1,128)}, u32[]{:S(2)}) copy-start(s32[1,4]{1,0:T(1,128)} %start_hbm.1) | copy-start | bytes 52
  6.5 37.4 %all-to-all-start = ((bf16[32,2,56,128]{3,2,1,0:T(8,128)(2,1)}), bf16[32,2,56,128]{3,2,1,0:T(8,128)(2,1)S(1)}, u32[]{:S(2)}, u32[]{:S(2)}) async-start(bf16[32,2,56,128]{3,2,1,0:T(8,128)(2,1)} %pack.1), calls=%async_computation | async-start | bytes 1835008 | tf_op jit(solution)/shard_map/all_to_all | solution.py:369
  18.6 9.8 %collective-permute-start.3 = (bf16[128,1024]{1,0:T(8,128)(2,1)}, bf16[128,1024]{1,0:T(8,128)(2,1)}, u32[]{:S(2)}, u32[]{:S(2)}) collective-permute-start(bf16[128,1024]{1,0:T(8,128)(2,1)} %param.23), channel_id=1, source_target_pairs={{0,1},{1,2},{2,3},{3,0},{4,5},{5,6},{6,7},{7,4},{8,9},{9,10},{10,1... | collective-permute-start | bytes 786440 | tf_op jit(solution)/shard_map/ppermute | solution.py:330
  20.2 14.4 %collective-permute-start.2 = (bf16[128,1024]{1,0:T(8,128)(2,1)}, bf16[128,1024]{1,0:T(8,128)(2,1)}, u32[]{:S(2)}, u32[]{:S(2)}) collective-permute-start(bf16[128,1024]{1,0:T(8,128)(2,1)} %param.23), channel_id=1, source_target_pairs={{0,2},{1,3},{2,0},{3,1},{4,6},{5,7},{6,4},{7,5},{8,10},{9,11},{10,... | collective-permute-start | bytes 786440 | tf_op jit(solution)/shard_map/ppermute | solution.py:330
  22.9 11.7 %collective-permute-start.1 = (bf16[128,1024]{1,0:T(8,128)(2,1)}, bf16[128,1024]{1,0:T(8,128)(2,1)}, u32[]{:S(2)}, u32[]{:S(2)}) collective-permute-start(bf16[128,1024]{1,0:T(8,128)(2,1)} %param.23), channel_id=1, source_target_pairs={{0,3},{1,0},{2,1},{3,2},{4,7},{5,4},{6,5},{7,6},{8,11},{9,8},{10,9... | collective-permute-start | bytes 786440 | tf_op jit(solution)/shard_map/ppermute | solution.py:330
  24.8 25.3 %copy-start = (bf16[1024,3,128]{2,0,1:T(8,128)(2,1)S(1)}, bf16[1024,3,128]{2,0,1:T(8,128)(2,1)}, u32[]{:S(2)}) copy-start(bf16[1024,3,128]{2,0,1:T(8,128)(2,1)} %param.22) | copy-start | bytes 2359300
  45.0 6.8 %collective-permute-start.4 = (bf16[256,256]{1,0:T(8,128)(2,1)S(1)}, bf16[256,256]{1,0:T(8,128)(2,1)S(1)}, u32[]{:S(2)}, u32[]{:S(2)}) collective-permute-start(bf16[256,256]{1,0:T(8,128)(2,1)S(1)} %unpack.1.x), channel_id=1, source_target_pairs={{0,3},{1,0},{2,1},{3,2},{4,7},{5,4},{6,5},{7,6},{8,11},{9,8},{10,9... | collective-permute-start | bytes 393224 | tf_op jit(solution)/shard_map/ppermute | solution.py:330
  47.8 7.6 %collective-permute-start.6 = (bf16[256,256]{1,0:T(8,128)(2,1)S(1)}, bf16[256,256]{1,0:T(8,128)(2,1)S(1)}, u32[]{:S(2)}, u32[]{:S(2)}) collective-permute-start(bf16[256,256]{1,0:T(8,128)(2,1)S(1)} %unpack.1.x), channel_id=1, source_target_pairs={{0,1},{1,2},{2,3},{3,0},{4,5},{5,6},{6,7},{7,4},{8,9},{9,10},{10,1... | collective-permute-start | bytes 393224 | tf_op jit(solution)/shard_map/ppermute | solution.py:330
  47.8 7.6 %collective-permute-start.5 = (bf16[256,256]{1,0:T(8,128)(2,1)S(1)}, bf16[256,256]{1,0:T(8,128)(2,1)S(1)}, u32[]{:S(2)}, u32[]{:S(2)}) collective-permute-start(bf16[256,256]{1,0:T(8,128)(2,1)S(1)} %unpack.1.x), channel_id=1, source_target_pairs={{0,2},{1,3},{2,0},{3,1},{4,6},{5,7},{6,4},{7,5},{8,10},{9,11},{10,... | collective-permute-start | bytes 393224 | tf_op jit(solution)/shard_map/ppermute | solution.py:330
  61.2 9.5 %collective-permute-start.9 = (bf16[1024,128]{1,0:T(8,128)(2,1)S(1)}, bf16[1024,128]{1,0:T(8,128)(2,1)S(1)}, u32[]{:S(2)}, u32[]{:S(2)}) collective-permute-start(bf16[1024,128]{1,0:T(8,128)(2,1)S(1)} %get-tuple-element.67.a0), channel_id=1, source_target_pairs={{0,1},{1,2},{2,3},{3,0},{4,5},{5,6},{6,7},{7,4},{8,9},{9,10},{10,1... | collective-permute-start | bytes 786440 | tf_op jit(solution)/shard_map/ppermute | solution.py:330
  61.5 12.0 %collective-permute-start.8 = (bf16[1024,128]{1,0:T(8,128)(2,1)S(1)}, bf16[1024,128]{1,0:T(8,128)(2,1)S(1)}, u32[]{:S(2)}, u32[]{:S(2)}) collective-permute-start(bf16[1024,128]{1,0:T(8,128)(2,1)S(1)} %get-tuple-element.67.a0), channel_id=1, source_target_pairs={{0,2},{1,3},{2,0},{3,1},{4,6},{5,7},{6,4},{7,5},{8,10},{9,11},{10,... | collective-permute-start | bytes 786440 | tf_op jit(solution)/shard_map/ppermute | solution.py:330
  65.1 8.9 %collective-permute-start.7 = (bf16[1024,128]{1,0:T(8,128)(2,1)S(1)}, bf16[1024,128]{1,0:T(8,128)(2,1)S(1)}, u32[]{:S(2)}, u32[]{:S(2)}) collective-permute-start(bf16[1024,128]{1,0:T(8,128)(2,1)S(1)} %get-tuple-element.67.a0), channel_id=1, source_target_pairs={{0,3},{1,0},{2,1},{3,2},{4,7},{5,4},{6,5},{7,6},{8,11},{9,8},{10,9... | collective-permute-start | bytes 786440 | tf_op jit(solution)/shard_map/ppermute | solution.py:330
  83.4 2.2 %collective-permute-start.10 = (bf16[8,4,16,512]{3,2,1,0:T(8,128)(2,1)S(1)}, bf16[8,4,16,512]{3,2,1,0:T(8,128)(2,1)S(1)}, u32[]{:S(2)}, u32[]{:S(2)}) collective-permute-start(bf16[8,4,16,512]{3,2,1,0:T(8,128)(2,1)S(1)} %get-tuple-element.87), channel_id=1, source_target_pairs={{0,4},{4,0},{1,5},{5,1},{2,6},{6,2},{3,7},{7,3},{8,12},{12,8},{9,1... | collective-permute-start | bytes 1572872 | tf_op jit(solution)/shard_map/ppermute | solution.py:460
  85.7 8.6 %collective-permute-start.11 = (bf16[8,16,512]{2,1,0:T(8,128)(2,1)S(1)}, bf16[8,16,512]{2,1,0:T(8,128)(2,1)S(1)}, u32[]{:S(2)}, u32[]{:S(2)}) collective-permute-start(bf16[8,16,512]{2,1,0:T(8,128)(2,1)S(1)} %get-tuple-element.89), channel_id=1, source_target_pairs={{0,8},{8,16},{16,24},{24,0},{1,9},{9,17},{17,25},{25,1},{2,10},{10... | collective-permute-start | bytes 393224 | tf_op jit(solution)/shard_map/ppermute | solution.py:471
  88.4 7.9 %collective-permute-start.12 = (bf16[8,16,512]{2,1,0:T(8,128)(2,1)S(1)}, bf16[8,16,512]{2,1,0:T(8,128)(2,1)S(1)}, u32[]{:S(2)}, u32[]{:S(2)}) collective-permute-start(bf16[8,16,512]{2,1,0:T(8,128)(2,1)S(1)} %get-tuple-element.90), channel_id=1, source_target_pairs={{0,16},{8,24},{16,0},{24,8},{1,17},{9,25},{17,1},{25,9},{2,18},{10... | collective-permute-start | bytes 393224 | tf_op jit(solution)/shard_map/ppermute | solution.py:471
  89.1 8.1 %collective-permute-start.13 = (bf16[8,16,512]{2,1,0:T(8,128)(2,1)S(1)}, bf16[8,16,512]{2,1,0:T(8,128)(2,1)S(1)}, u32[]{:S(2)}, u32[]{:S(2)}) collective-permute-start(bf16[8,16,512]{2,1,0:T(8,128)(2,1)S(1)} %get-tuple-element.91), channel_id=1, source_target_pairs={{0,24},{8,0},{16,8},{24,16},{1,25},{9,1},{17,9},{25,17},{2,26},{10... | collective-permute-start | bytes 393224 | tf_op jit(solution)/shard_map/ppermute | solution.py:471
  97.9 12.5 %all-to-all-start.1 = ((bf16[8,16,512]{2,1,0:T(8,128)(2,1)}), bf16[8,16,512]{2,1,0:T(8,128)(2,1)S(1)}, u32[]{:S(2)}, u32[]{:S(2)}) async-start(bf16[8,16,512]{2,1,0:T(8,128)(2,1)} %line.1), calls=%async_computation.1 | async-start | bytes 262144 | tf_op jit(solution)/shard_map/all_to_all | solution.py:481
  (4 other events, 55.3 us)

commit v5 on v4

--- a/solution.py
+++ b/solution.py
@@ -160,30 +160,39 @@
     return (lane < HEAD) if h == 0 else (lane >= HEAD)
 
 
-def piece_of(step, table, spans, x, w, gain, wqkv, inp, tgt):
-    part = lax.rem(lax.axis_index("mp") + step, 4)
-    row = lax.broadcasted_iota(jnp.int32, (256, 128), 0)
-    frame = (row >> 5) * BLOCK + part * 32 + (row & 31)
-    lev = jnp.zeros((256, 128), F32)
-    for u, (begin, end, _, _) in enumerate(spans):
-        inside = (frame >= begin) & (frame < end)
-        lev = jnp.where(inside, table[0, 12 + u].astype(F32) / 64.0, lev)
-    noise, data = x[:, :128].astype(F32), x[:, 128:].astype(F32)
-    noisy = (1.0 - lev) * noise + lev * data
-    cond = jnp.where(masked_of(frame, spans), 0.0, data)
-    both = jnp.concatenate([noisy, cond], axis=1).astype(BF16)
-    inp[...] = both
-    tgt[...] = data - noise
-    h = dot(both, w[...])
-    scale = lax.rsqrt(jnp.mean(h * h, axis=1, keepdims=True) + EPS)
+def pieces_of(table, w, gain, wqkv, items):
+    spans = utterances(table)
+    made = []
+    for step, x, inp, tgt in items:
+        part = lax.rem(lax.axis_index("mp") + step, 4)
+        row = lax.broadcasted_iota(jnp.int32, (256, 128), 0)
+        frame = (row >> 5) * BLOCK + part * 32 + (row & 31)
+        lev = jnp.zeros((256, 128), F32)
+        for u, (begin, end, _, _) in enumerate(spans):
+            inside = (frame >= begin) & (frame < end)
+            lev = jnp.where(inside, table[0, 12 + u].astype(F32) / 64.0, lev)
+        noise, data = x[:, :128].astype(F32), x[:, 128:].astype(F32)
+        noisy = (1.0 - lev) * noise + lev * data
+        cond = jnp.where(masked_of(frame, spans), 0.0, data)
+        made.append(jnp.concatenate([noisy, cond], axis=1).astype(BF16))
+        inp[...] = made[-1]
+        tgt[...] = data - noise
+    hidden = [dot(both, w[...]) for both in made]
+    scales = [lax.rsqrt(jnp.mean(h * h, axis=1, keepdims=True) + EPS) for h in hidden]
     weights = jnp.concatenate([wqkv[0], wqkv[1], wqkv[2]], axis=1)
-    out = dot((h * scale * gain[...]).astype(BF16), weights)
-    query = (out[:, 0:128].astype(BF16).astype(F32) * HEAD ** (-0.5)).astype(BF16)
-    return query, out[:, 128:256].astype(BF16), out[:, 256:].astype(BF16)
+    outs = [dot((h * scale * gain[...]).astype(BF16), weights) for h, scale in zip(hidden, scales)]
+    return [
+        (
+            (out[:, 0:128].astype(BF16).astype(F32) * HEAD ** (-0.5)).astype(BF16),
+            out[:, 128:256].astype(BF16),
+            out[:, 256:].astype(BF16),
+        )
+        for out in outs
+    ]
 
 
 def piece_kernel(step, table, x, w, gain, wqkv, inp, tgt, qkv):
-    out = piece_of(step, table, utterances(table), x, w, gain, wqkv, inp, tgt)
+    (out,) = pieces_of(table, w, gain, wqkv, [(step, x, inp, tgt)])
     for j in range(3):
         qkv[:, j * 128 : (j + 1) * 128] = out[j]
 
@@ -194,11 +203,9 @@
 
 
 def front_kernel(
-    table, p0, p1, x2, x3, w, gain, wqkv, att, q, k, v, probs_out, i2, i3, t2, t3, vt, attt
+    table, p0, p1, x2, x3, w, gain, wqkv, att, attt, q, k, v, probs_out, i2, i3, t2, t3, vt
 ):
-    spans = utterances(table)
-    late = ((2, x2, i2, t2), (3, x3, i3, t3))
-    made = [piece_of(step, table, spans, x, w, gain, wqkv, i, t) for step, x, i, t in late]
+    made = pieces_of(table, w, gain, wqkv, [(2, x2, i2, t2), (3, x3, i3, t3)])
     early = [[p[:, j * 128 : (j + 1) * 128] for j in range(3)] for p in (p0, p1)]
     for step, piece in enumerate(early + made):
         for r, at in piece_rows(step):
@@ -208,22 +215,22 @@
 
     def one(first, rows):
         at = pl.ds(first, rows)
+        keys = [jnp.where(head_mask(rows, h), k[at, :], jnp.zeros((), BF16)) for h in range(2)]
+        scores = [dot(key, q[at, :], NT) for key in keys]
+        weights = [jnp.exp(s - jnp.max(s, axis=0, keepdims=True)) for s in scores]
+        inverse = [1.0 / jnp.sum(a, axis=0, keepdims=True) for a in weights]
+        probs = [a * b for a, b in zip(weights, inverse)]
+        parts = [dot(vt[h * HEAD : (h + 1) * HEAD, at], probs[h].astype(BF16)) for h in range(2)]
         for h in range(2):
-            keys = jnp.where(head_mask(rows, h), k[at, :], jnp.zeros((), BF16))
-            scores = dot(keys, q[at, :], NT)
-            top = jnp.max(scores, axis=0, keepdims=True)
-            weights = jnp.exp(scores - top)
-            inv = 1.0 / jnp.sum(weights, axis=0, keepdims=True)
-            probs = weights * inv
-            probs_out[h, at, 0:rows] = probs
-            part = dot(vt[h * HEAD : (h + 1) * HEAD, at], probs.astype(BF16))
-            attt[h * HEAD : (h + 1) * HEAD, at] = part.astype(BF16)
+            probs_out[h, at, 0:rows] = probs[h]
+            attt[h * HEAD : (h + 1) * HEAD, at] = parts[h].astype(BF16)
 
     each_utterance(table, one)
     att[...] = attt[...].T
 
 
-def mid_kernel(i0, i1, i2, i3, t0, t1, t2, t3, w, gain, hidden, normed, tgt):
+def mid_kernel(i0, i1, i2, i3, t0, t1, t2, t3, w, gain, k, hidden, normed, tgt, kt):
+    kt[...] = k[...].T
     for step, (inp, target) in enumerate(((i0, t0), (i1, t1), (i2, t2), (i3, t3))):
         h = dot(inp[...], w[...])
         scale = lax.rsqrt(jnp.mean(h * h, axis=1, keepdims=True) + EPS)
@@ -242,43 +249,53 @@
 
 
 def back_kernel(
-    table, a0, a1, a2, proj, hidden, normed, tgt, fgain, vel, q, k, v, probs,
-    keep, send, back1, dout, kt, dqt, dk, dv, lhs,
+    table, attt, a1, a2, proj, hidden, normed, tgt, fgain, vel, q, kt, v, probs,
+    keep, send, back1, dout, dqt, dk, dv, lhs,
 ):
     spans = utterances(table)
-    for i in range(4):
+    def first(i):
         rows = pl.ds(i * 256, 256)
         groups = jnp.concatenate([a1[rows, :], a2[rows, :]], axis=1)
         wide = (hidden[rows, :] + dot(groups, proj[128:384, :])).astype(BF16).astype(F32)
-        rscale = lax.rsqrt(jnp.mean(wide * wide, axis=1, keepdims=True) + EPS)
+        return wide, lax.rsqrt(jnp.mean(wide * wide, axis=1, keepdims=True) + EPS)
+
+    def second(i, wide, rscale):
+        rows = pl.ds(i * 256, 256)
         normalized = wide * rscale
-        final = (normalized * fgain[...]).astype(BF16)
-        velocity = dot(final, vel[...])
+        velocity = dot((normalized * fgain[...]).astype(BF16), vel[...])
         frame = i * 256 + lax.broadcasted_iota(jnp.int32, (256, 128), 0)
-        error = jnp.where(masked_of(frame, spans), 2.0 * (velocity - tgt[rows, :]), 0.0).astype(BF16)
+        error = jnp.where(masked_of(frame, spans), 2.0 * (velocity - tgt[rows, :]), 0.0)
+        return normalized, rscale, error.astype(BF16)
+
+    def third(i, normalized, rscale, error):
+        rows = pl.ds(i * 256, 256)
         scaled = dot(error, vel[...], NT) * fgain[...]
         middle = jnp.mean(scaled * normalized, axis=1, keepdims=True)
         b1 = (rscale * (scaled - normalized * middle)).astype(BF16)
         back1[rows, :] = b1
         dout[rows, :] = dot(b1, proj[0:128, :], NT).astype(BF16)
 
-    kt[...] = k[...].T
+    ones = [first(i) for i in range(4)]
+    twos = [second(i, *ones[i]) for i in range(4)]
+    for i in range(4):
+        third(i, *twos[i])
+
 
     def one(first, rows):
         at = pl.ds(first, rows)
         qs, vs, ds = q[at, :], v[at, :], dout[at, :]
-        dks, dvs = [], []
+        zero = jnp.zeros((), BF16)
+        ps = [probs[h, at, 0:rows] for h in range(2)]
+        dps = [
+            dot(jnp.where(head_mask(rows, h), vs, zero), ds, NT).astype(BF16).astype(F32) for h in range(2)
+        ]
+        dvs = [dot(p.astype(BF16), ds) for p in ps]
+        inner = [jnp.sum(p * dp, axis=0, keepdims=True) for p, dp in zip(ps, dps)]
+        dscores = [(p * (dp - s)).astype(BF16) for p, dp, s in zip(ps, dps, inner)]
+        dks = [dot(d, qs) for d in dscores]
         for h in range(2):
-            mask = head_mask(rows, h)
-            zero = jnp.zeros((), BF16)
-            p = probs[h, at, 0:rows]
-            dp = dot(jnp.where(mask, vs, zero), ds, NT).astype(BF16).astype(F32)
-            inner = jnp.sum(p * dp, axis=0, keepdims=True)
-            dscore = (p * (dp - inner)).astype(BF16)
-            dvs.append(dot(p.astype(BF16), ds))
-            dks.append(dot(dscore, qs))
             span = slice(h * HEAD, (h + 1) * HEAD)
-            dqt[span, at] = (dot(kt[span, at], dscore) * HEAD ** (-0.5)).astype(BF16)
+            dqt[span, at] = (dot(kt[span, at], dscores[h]) * HEAD ** (-0.5)).astype(BF16)
         mask = head_mask(rows, 0)
         dk[at, :] = jnp.where(mask, dks[0], dks[1]).astype(BF16)
         dv[at, :] = jnp.where(mask, dvs[0], dvs[1]).astype(BF16)
@@ -287,12 +304,11 @@
     lhs[0:128, :] = dqt[...]
     lhs[128:256, :] = dk[...].T
     lhs[256:384, :] = dv[...].T
-    lhs[384:512, :] = a0[...].T
     mine = lax.axis_index("c") == 0
     for j in range(4):
         cols = slice(j * 256, (j + 1) * 256)
         top = dot(lhs[0:384, :], normed[:, cols])
-        low = dot(lhs[384:512, :], back1[:, cols])
+        low = dot(attt[...], back1[:, cols])
         terms = jnp.concatenate([top.T, low.T], axis=1).reshape(8, 2, 16, 512)
         even, odd = terms[:, 0], terms[:, 1]
         keep[2 * j : 2 * j + 2] = jnp.where(mine, even, odd).reshape(2, 4, 16, 512)
@@ -391,7 +407,7 @@
     count = counts[0] * 32.0 + counts[1]
     pieces = [frames] + [turned(frames, by) for by in (1, 2, 3)]
 
-    half = jax.ShapeDtypeStruct((1024, 128), BF16)
+    half, turn = (jax.ShapeDtypeStruct(shape, BF16) for shape in ((1024, 128), (128, 1024)))
 
     def cost(flops, size):
         return pl.CostEstimate(flops=flops, bytes_accessed=size, transcendentals=0)
@@ -411,13 +427,13 @@
         )(table, frames, w, gain, wqkv)
 
     first = [piece(step, pieces[step]) for step in (0, 1)]
-    att, q, k, v, probs, *late = pl.pallas_call(
+    att, attt, q, k, v, probs, *late = pl.pallas_call(
         front_kernel,
-        out_shape=(half, half, half, half, jax.ShapeDtypeStruct((2, 1024, 512), F32))
+        out_shape=(half, turn, half, half, half, jax.ShapeDtypeStruct((2, 1024, 512), F32))
         + (jax.ShapeDtypeStruct((256, 256), BF16),) * 2 + (jax.ShapeDtypeStruct((256, 128), F32),) * 2,
         in_specs=[sm()] + [vm()] * 7,
-        out_specs=(vm(),) * 9,
-        scratch_shapes=[VMEM((128, 1024), BF16), VMEM((128, 1024), BF16)],
+        out_specs=(vm(),) * 10,
+        scratch_shapes=[VMEM((128, 1024), BF16)],
         compiler_params=params(20),
         name="front",
     )(table, first[0][2], first[1][2], pieces[2], pieces[3], w, gain, wqkv)
@@ -425,15 +441,15 @@
     tgt = (first[0][1], first[1][1], late[2], late[3])
     heads = [att] + [turned(att, by) for by in (1, 2, 3)]
     full = jax.ShapeDtypeStruct((1024, 1024), F32)
-    hidden, normed, target = pl.pallas_call(
+    hidden, normed, target, kt = pl.pallas_call(
         mid_kernel,
-        out_shape=(full, jax.ShapeDtypeStruct((1024, 1024), BF16), jax.ShapeDtypeStruct((1024, 128), F32)),
-        in_specs=[vm()] * 10,
-        out_specs=(vm(),) * 3,
+        out_shape=(full, jax.ShapeDtypeStruct((1024, 1024), BF16), jax.ShapeDtypeStruct((1024, 128), F32), turn),
+        in_specs=[vm()] * 11,
+        out_specs=(vm(),) * 4,
         compiler_params=params(14),
         cost_estimate=cost(1 << 29, 7 << 20),
         name="mid",
-    )(*inp, *tgt, w, gain)
+    )(*inp, *tgt, w, gain, k)
     hidden = pl.pallas_call(
         mix_kernel,
         out_shape=full,
@@ -451,12 +467,12 @@
         out_specs=(vm(), vm()),
         scratch_shapes=[
             VMEM((1024, 1024), BF16), VMEM((1024, 128), BF16),
-            VMEM((128, 1024), BF16), VMEM((128, 1024), BF16), VMEM((1024, 128), BF16),
-            VMEM((1024, 128), BF16), VMEM((512, 1024), BF16),
+            VMEM((128, 1024), BF16), VMEM((1024, 128), BF16), VMEM((1024, 128), BF16),
+            VMEM((384, 1024), BF16),
         ],
         compiler_params=params(28),
         name="back",
-    )(table, *heads[:3], proj, hidden, normed, target, fgain, vel, q, k, v, probs)
+    )(table, attt, *heads[1:3], proj, hidden, normed, target, fgain, vel, q, kt, v, probs)
     got = lax.ppermute(send, "c", swap)
     piece = jax.ShapeDtypeStruct((8, 16, 512), BF16)
     total, *sends = pl.pallas_call(

time: 111 us -> 108 us (0.973)
  Pallas kernels: 26 us -> 23.4 us
    pallas_call x1, Pallas kernels: 9.41 us -> 8.05 us  [shards(): pl.pallas_call(back_kernel, out_shape=tuple((jax.ShapeDtypeStruct((8, 4,...]
    pallas_call x1, Pallas kernels: 5.81 us -> 4.58 us  [shards(): pl.pallas_call(front_kernel, out_shape=(half, turn, half, half, half, jax...]
where the time goes in v5:
time: 108 us
  waiting for transfers between devices  42 us (39%)
  starting transfers between devices  36.1 us (33%)
  Pallas kernels  23.4 us (22%)
  other arithmetic  2.44 us (2%)
  between operations  2.27 us (2%)
  local copies, waits for them, and re-layouts  1.83 us (2%)
    ppermute x9, waiting for transfers between devices, turned(): return lax.ppermute(a, 'mp', [(i, (i - by) % 4) for i in range(4)])  18.6 us
    ppermute x9, starting transfers between devices, turned(): return lax.ppermute(a, 'mp', [(i, (i - by) % 4) for i in range(4)])  14.7 us
    all_to_all x1, starting transfers between devices, shards(): lax.all_to_all(packed, ('z', 'y'), 0, 0, tiled=True).reshape(64, SLOT, 128)  11.8 us
    all_to_all x1, waiting for transfers between devices, shards(): lax.all_to_all(packed, ('z', 'y'), 0, 0, tiled=True).reshape(64, SLOT, 128)  8.08 us
    pallas_call x1, Pallas kernels, shards(): pl.pallas_call(back_kernel, out_shape=tuple((jax.ShapeDtypeStruct((8, 4,...  8.05 us
    all_to_all x1, waiting for transfers between devices, shards(): parts = lax.all_to_all(line, 'z', 0, 0, tiled=True)  7.11 us
    ppermute x3, starting transfers between devices, shards(): lax.ppermute(a, 'y', [(i, (i + by) % 4) for i in range(4)])  5.93 us
    ppermute x3, waiting for transfers between devices, shards(): lax.ppermute(a, 'y', [(i, (i + by) % 4) for i in range(4)])  5.53 us
  transfers between devices with their start and end apart: 16, of which 14 were waited for; matrix products, arithmetic and copies ran while one was open for 3% of the time, Pallas kernels for 5%

profile of v5, /device:TPU:8, one launch (start us, length us, event | category | flops | bytes accessed | tf_op | source)
XLA Modules:
  0.0 108.1 jit_solution(14168255330690259138)
XLA Ops:
  0.7 1.6 %share.1.own = bf16[8,56,128]{2,1,0:T(8,128)(2,1)} custom-call(s32[1,4]{1,0:T(1,128)} %utt_hbm.1, s32[1,4]{1,0:T(1,128)} %start_hbm.1, s32[1,4]{1,0:T(1,128)} %size_hbm.1, bf16[8,12800]{1,0:T(8,128)(2,1)} %noise.1, bf16[8,12800]{1,0:T(8,128)(2,1)} %data.1), custom_call_target="tpu_custom_call" | custom-call | tf_op jit(solution)/shard_map/share/pallas_call | solution.py:349
  4.8 1.6 %pack.1 = bf16[32,2,56,128]{3,2,1,0:T(8,128)(2,1)} custom-call(s32[512]{0:T(512)S(1)} %add_select_fusion.bins, bf16[8,56,128]{2,1,0:T(8,128)(2,1)S(1)} %copy-done.1, bf16[8,56,128]{2,1,0:T(8,128)(2,1)S(1)} %collective-permute-done.other), custom_call_target="tpu_custom_call" | custom-call | tf_op jit(solution)/shard_map/pack/pallas_call | solution.py:361
  6.5 11.8 %all-to-all-start = ((bf16[32,2,56,128]{3,2,1,0:T(8,128)(2,1)}), bf16[32,2,56,128]{3,2,1,0:T(8,128)(2,1)S(1)}, u32[]{:S(2)}, u32[]{:S(2)}) async-start(bf16[32,2,56,128]{3,2,1,0:T(8,128)(2,1)} %pack.1), calls=%async_computation | async-start | bytes 1835008 | tf_op jit(solution)/shard_map/all_to_all | solution.py:385
  18.6 1.6 %collective-permute-start.3 = (bf16[128,1024]{1,0:T(8,128)(2,1)}, bf16[128,1024]{1,0:T(8,128)(2,1)}, u32[]{:S(2)}, u32[]{:S(2)}) collective-permute-start(bf16[128,1024]{1,0:T(8,128)(2,1)} %param.23), channel_id=1, source_target_pairs={{0,1},{1,2},{2,3},{3,0},{4,5},{5,6},{6,7},{7,4},{8,9},{9,10},{10,1... | collective-permute-start | bytes 786440 | tf_op jit(solution)/shard_map/ppermute | solution.py:346
  20.2 2.7 %collective-permute-start.2 = (bf16[128,1024]{1,0:T(8,128)(2,1)}, bf16[128,1024]{1,0:T(8,128)(2,1)}, u32[]{:S(2)}, u32[]{:S(2)}) collective-permute-start(bf16[128,1024]{1,0:T(8,128)(2,1)} %param.23), channel_id=1, source_target_pairs={{0,2},{1,3},{2,0},{3,1},{4,6},{5,7},{6,4},{7,5},{8,10},{9,11},{10,... | collective-permute-start | bytes 786440 | tf_op jit(solution)/shard_map/ppermute | solution.py:346
  22.9 1.4 %collective-permute-start.1 = (bf16[128,1024]{1,0:T(8,128)(2,1)}, bf16[128,1024]{1,0:T(8,128)(2,1)}, u32[]{:S(2)}, u32[]{:S(2)}) collective-permute-start(bf16[128,1024]{1,0:T(8,128)(2,1)} %param.23), channel_id=1, source_target_pairs={{0,3},{1,0},{2,1},{3,2},{4,7},{5,4},{6,5},{7,6},{8,11},{9,8},{10,9... | collective-permute-start | bytes 786440 | tf_op jit(solution)/shard_map/ppermute | solution.py:346
  25.0 3.5 %collective-permute-done.3 = bf16[128,1024]{1,0:T(8,128)(2,1)} collective-permute-done((bf16[128,1024]{1,0:T(8,128)(2,1)}, bf16[128,1024]{1,0:T(8,128)(2,1)}, u32[]{:S(2)}, u32[]{:S(2)}) %collective-permute-start.3) | collective-permute-done | bytes 262176 | tf_op jit(solution)/shard_map/ppermute | solution.py:346
  28.4 6.2 %collective-permute-done.2 = bf16[128,1024]{1,0:T(8,128)(2,1)} collective-permute-done((bf16[128,1024]{1,0:T(8,128)(2,1)}, bf16[128,1024]{1,0:T(8,128)(2,1)}, u32[]{:S(2)}, u32[]{:S(2)}) %collective-permute-start.2) | collective-permute-done | bytes 262176 | tf_op jit(solution)/shard_map/ppermute | solution.py:346
  35.9 8.1 %all-to-all-done = bf16[32,2,56,128]{3,2,1,0:T(8,128)(2,1)S(1)} async-done(((bf16[32,2,56,128]{3,2,1,0:T(8,128)(2,1)}), bf16[32,2,56,128]{3,2,1,0:T(8,128)(2,1)S(1)}, u32[]{:S(2)}, u32[]{:S(2)}) %all-to-all-start) | async-done | bytes 917536 | tf_op jit(solution)/shard_map/all_to_all | solution.py:385
  45.0 2.8 %collective-permute-start.4 = (bf16[256,256]{1,0:T(8,128)(2,1)S(1)}, bf16[256,256]{1,0:T(8,128)(2,1)S(1)}, u32[]{:S(2)}, u32[]{:S(2)}) collective-permute-start(bf16[256,256]{1,0:T(8,128)(2,1)S(1)} %unpack.1.x), channel_id=1, source_target_pairs={{0,3},{1,0},{2,1},{3,2},{4,7},{5,4},{6,5},{7,6},{8,11},{9,8},{10,9... | collective-permute-start | bytes 393224 | tf_op jit(solution)/shard_map/ppermute | solution.py:346
  47.8 2.3 %collective-permute-start.5 = (bf16[256,256]{1,0:T(8,128)(2,1)S(1)}, bf16[256,256]{1,0:T(8,128)(2,1)S(1)}, u32[]{:S(2)}, u32[]{:S(2)}) collective-permute-start(bf16[256,256]{1,0:T(8,128)(2,1)S(1)} %unpack.1.x), channel_id=1, source_target_pairs={{0,2},{1,3},{2,0},{3,1},{4,6},{5,7},{6,4},{7,5},{8,10},{9,11},{10,... | collective-permute-start | bytes 393224 | tf_op jit(solution)/shard_map/ppermute | solution.py:346
  53.2 2.2 %collective-permute-done.6.x3 = bf16[256,256]{1,0:T(8,128)(2,1)S(1)} collective-permute-done((bf16[256,256]{1,0:T(8,128)(2,1)S(1)}, bf16[256,256]{1,0:T(8,128)(2,1)S(1)}, u32[]{:S(2)}, u32[]{:S(2)}) %collective-permute-start.6) | collective-permute-done | bytes 131104 | tf_op jit(solution)/shard_map/ppermute | solution.py:346
  55.4 4.6 %front.1 = (bf16[1024,128]{1,0:T(8,128)(2,1)S(1)}, bf16[128,1024]{1,0:T(8,128)(2,1)S(1)}, bf16[1024,128]{1,0:T(8,128)(2,1)S(1)}, bf16[1024,128]{1,0:T(8,128)(2,1...) custom-call(s32[1,16]{1,0:T(1,128)S(1)} %pad_add_fusion.table, ...), custom_call_target="tpu_custom_call" | custom-call | tf_op jit(solution)/shard_map/front/pallas_call | solution.py:430
  60.1 3.6 %collective-permute-start.8 = (bf16[1024,128]{1,0:T(8,128)(2,1)S(1)}, bf16[1024,128]{1,0:T(8,128)(2,1)S(1)}, u32[]{:S(2)}, u32[]{:S(2)}) collective-permute-start(bf16[1024,128]{1,0:T(8,128)(2,1)S(1)} %get-tuple-element.70.a0), channel_id=1, source_target_pairs={{0,2},{1,3},{2,0},{3,1},{4,6},{5,7},{6,4},{7,5},{8,10},{9,11},{10,... | collective-permute-start | bytes 786440 | tf_op jit(solution)/shard_map/ppermute | solution.py:346
  65.1 4.2 %collective-permute-done.9.a3 = bf16[1024,128]{1,0:T(8,128)(2,1)S(1)} collective-permute-done((bf16[1024,128]{1,0:T(8,128)(2,1)S(1)}, bf16[1024,128]{1,0:T(8,128)(2,1)S(1)}, u32[]{:S(2)}, u32[]{:S(2)}) %collective-permute-start.9) | collective-permute-done | bytes 262176 | tf_op jit(solution)/shard_map/ppermute | solution.py:346
  70.3 1.9 %collective-permute-done.8.a2 = bf16[1024,128]{1,0:T(8,128)(2,1)S(1)} collective-permute-done((bf16[1024,128]{1,0:T(8,128)(2,1)S(1)}, bf16[1024,128]{1,0:T(8,128)(2,1)S(1)}, u32[]{:S(2)}, u32[]{:S(2)}) %collective-permute-start.8) | collective-permute-done | bytes 262176 | tf_op jit(solution)/shard_map/ppermute | solution.py:346
  72.6 8.0 %back.1 = (f32[8,4,16,512]{3,2,1,0:T(8,128)S(1)}, bf16[8,4,16,512]{3,2,1,0:T(8,128)(2,1)S(1)}) custom-call(s32[1,16]{1,0:T(1,128)S(1)} %pad_add_fusion.table, bf16[128,1024]{1,0:T(8,128)(2,1)S(1)} %get-tuple-element.69.attt, bf16[1024,128]{1,0:T(8,128)(2,1)S(1)} %collective-permute-done.7.a1, bf16[1024,128]{1,0:T(8,128)(2,1)S(1)} %collective-permute-done.8.a2, ...), custom_call_target="tpu_custom_call" | custom-call | tf_op jit(solution)/shard_map/back/pallas_call | solution.py:463
  80.8 1.9 %collective-permute-done.10.got = bf16[8,4,16,512]{3,2,1,0:T(8,128)(2,1)S(1)} collective-permute-done((bf16[8,4,16,512]{3,2,1,0:T(8,128)(2,1)S(1)}, bf16[8,4,16,512]{3,2,1,0:T(8,128)(2,1)S(1)}, u32[]{:S(2)}, u32[]{:S(2)}) %collective-permute-start.10) | collective-permute-done | bytes 524320 | tf_op jit(solution)/shard_map/ppermute | solution.py:476
  82.7 2.7 %collective-permute-start.11 = (bf16[8,16,512]{2,1,0:T(8,128)(2,1)S(1)}, bf16[8,16,512]{2,1,0:T(8,128)(2,1)S(1)}, u32[]{:S(2)}, u32[]{:S(2)}) collective-permute-start(bf16[8,16,512]{2,1,0:T(8,128)(2,1)S(1)} %get-tuple-element.93), channel_id=1, source_target_pairs={{0,8},{8,16},{16,24},{24,0},{1,9},{9,17},{17,25},{25,1},{2,10},{10... | collective-permute-start | bytes 393224 | tf_op jit(solution)/shard_map/ppermute | solution.py:487
  86.1 2.5 %collective-permute-start.13 = (bf16[8,16,512]{2,1,0:T(8,128)(2,1)S(1)}, bf16[8,16,512]{2,1,0:T(8,128)(2,1)S(1)}, u32[]{:S(2)}, u32[]{:S(2)}) collective-permute-start(bf16[8,16,512]{2,1,0:T(8,128)(2,1)S(1)} %get-tuple-element.95), channel_id=1, source_target_pairs={{0,24},{8,0},{16,8},{24,16},{1,25},{9,1},{17,9},{25,17},{2,26},{10... | collective-permute-start | bytes 393224 | tf_op jit(solution)/shard_map/ppermute | solution.py:487
  88.7 2.7 %collective-permute-done.11.r1 = bf16[8,16,512]{2,1,0:T(8,128)(2,1)S(1)} collective-permute-done((bf16[8,16,512]{2,1,0:T(8,128)(2,1)S(1)}, bf16[8,16,512]{2,1,0:T(8,128)(2,1)S(1)}, u32[]{:S(2)}, u32[]{:S(2)}) %collective-permute-start.11) | collective-permute-done | bytes 131104 | tf_op jit(solution)/shard_map/ppermute | solution.py:487
  91.4 2.0 %collective-permute-done.12.r2 = bf16[8,16,512]{2,1,0:T(8,128)(2,1)S(1)} collective-permute-done((bf16[8,16,512]{2,1,0:T(8,128)(2,1)S(1)}, bf16[8,16,512]{2,1,0:T(8,128)(2,1)S(1)}, u32[]{:S(2)}, u32[]{:S(2)}) %collective-permute-start.12) | collective-permute-done | bytes 131104 | tf_op jit(solution)/shard_map/ppermute | solution.py:487
  94.9 3.4 %all-to-all-start.1 = ((bf16[8,16,512]{2,1,0:T(8,128)(2,1)}), bf16[8,16,512]{2,1,0:T(8,128)(2,1)S(1)}, u32[]{:S(2)}, u32[]{:S(2)}) async-start(bf16[8,16,512]{2,1,0:T(8,128)(2,1)} %line.1), calls=%async_computation.1 | async-start | bytes 262144 | tf_op jit(solution)/shard_map/all_to_all | solution.py:497
  100.3 7.1 %all-to-all-done.1.parts = bf16[8,16,512]{2,1,0:T(8,128)(2,1)S(1)} async-done(((bf16[8,16,512]{2,1,0:T(8,128)(2,1)}), bf16[8,16,512]{2,1,0:T(8,128)(2,1)S(1)}, u32[]{:S(2)}, u32[]{:S(2)}) %all-to-all-start.1) | async-done | bytes 131104 | tf_op jit(solution)/shard_map/all_to_all | solution.py:497
  (59 shorter events, 15.4 us)
Async XLA Ops:
  0.6 23.7 %copy-start.10 = (pred[128]{0:T(512)(128)(4,1)S(1)}, pred[128]{0:T(512)(128)(4,1)}, u32[]{:S(2)}) copy-start(pred[128]{0:T(512)(128)(4,1)} %constant.46.clone.1) | copy-start | bytes 388
  0.7 23.7 %copy-start.2 = (bf16[200,1024]{1,0:T(8,128)(2,1)S(1)}, bf16[200,1024]{1,0:T(8,128)(2,1)}, u32[]{:S(2)}) copy-start(bf16[200,1024]{1,0:T(8,128)(2,1)} %param.20) | copy-start | bytes 1228804
  2.3 22.2 %copy-start.8 = (bf16[1024]{0:T(1024)(128)(2,1)S(1)}, bf16[1024]{0:T(1024)(128)(2,1)}, u32[]{:S(2)}) copy-start(bf16[1024]{0:T(1024)(128)(2,1)} %param.21) | copy-start | bytes 6148
  2.3 22.2 %copy-start.9 = (bf16[1024]{0:T(1024)(128)(2,1)S(1)}, bf16[1024]{0:T(1024)(128)(2,1)}, u32[]{:S(2)}) copy-start(bf16[1024]{0:T(1024)(128)(2,1)} %param.24) | copy-start | bytes 6148
  2.3 1.6 %collective-permute-start = (bf16[8,56,128]{2,1,0:T(8,128)(2,1)}, bf16[8,56,128]{2,1,0:T(8,128)(2,1)S(1)}, u32[]{:S(2)}, u32[]{:S(2)}) collective-permute-start(bf16[8,56,128]{2,1,0:T(8,128)(2,1)} %share.1.own), channel_id=1, source_target_pairs={{0,4},{4,0},{1,5},{5,1},{2,6},{6,2},{3,7},{7,3},{8,12},{12,8},{9,1... | collective-permute-start | bytes 344072 | tf_op jit(solution)/shard_map/ppermute | solution.py:359
  4.8 19.7 %copy-start.3 = (bf16[1024,100]{0,1:T(8,128)(2,1)S(1)}, bf16[1024,100]{0,1:T(8,128)(2,1)}, u32[]{:S(2)}) copy-start(bf16[1024,100]{0,1:T(8,128)(2,1)} %param.25) | copy-start | bytes 614404
  6.5 18.3 %copy-start.5 = (s32[1,4]{1,0:T(1,128)S(1)}, s32[1,4]{1,0:T(1,128)}, u32[]{:S(2)}) copy-start(s32[1,4]{1,0:T(1,128)} %utt_hbm.1) | copy-start | bytes 52
  6.5 18.3 %copy-start.6 = (s32[1,4]{1,0:T(1,128)S(1)}, s32[1,4]{1,0:T(1,128)}, u32[]{:S(2)}) copy-start(s32[1,4]{1,0:T(1,128)} %start_hbm.1) | copy-start | bytes 52
  6.5 37.4 %all-to-all-start = ((bf16[32,2,56,128]{3,2,1,0:T(8,128)(2,1)}), bf16[32,2,56,128]{3,2,1,0:T(8,128)(2,1)S(1)}, u32[]{:S(2)}, u32[]{:S(2)}) async-start(bf16[32,2,56,128]{3,2,1,0:T(8,128)(2,1)} %pack.1), calls=%async_computation | async-start | bytes 1835008 | tf_op jit(solution)/shard_map/all_to_all | solution.py:385
  18.6 9.8 %collective-permute-start.3 = (bf16[128,1024]{1,0:T(8,128)(2,1)}, bf16[128,1024]{1,0:T(8,128)(2,1)}, u32[]{:S(2)}, u32[]{:S(2)}) collective-permute-start(bf16[128,1024]{1,0:T(8,128)(2,1)} %param.23), channel_id=1, source_target_pairs={{0,1},{1,2},{2,3},{3,0},{4,5},{5,6},{6,7},{7,4},{8,9},{9,10},{10,1... | collective-permute-start | bytes 786440 | tf_op jit(solution)/shard_map/ppermute | solution.py:346
  20.2 14.4 %collective-permute-start.2 = (bf16[128,1024]{1,0:T(8,128)(2,1)}, bf16[128,1024]{1,0:T(8,128)(2,1)}, u32[]{:S(2)}, u32[]{:S(2)}) collective-permute-start(bf16[128,1024]{1,0:T(8,128)(2,1)} %param.23), channel_id=1, source_target_pairs={{0,2},{1,3},{2,0},{3,1},{4,6},{5,7},{6,4},{7,5},{8,10},{9,11},{10,... | collective-permute-start | bytes 786440 | tf_op jit(solution)/shard_map/ppermute | solution.py:346
  22.9 11.7 %collective-permute-start.1 = (bf16[128,1024]{1,0:T(8,128)(2,1)}, bf16[128,1024]{1,0:T(8,128)(2,1)}, u32[]{:S(2)}, u32[]{:S(2)}) collective-permute-start(bf16[128,1024]{1,0:T(8,128)(2,1)} %param.23), channel_id=1, source_target_pairs={{0,3},{1,0},{2,1},{3,2},{4,7},{5,4},{6,5},{7,6},{8,11},{9,8},{10,9... | collective-permute-start | bytes 786440 | tf_op jit(solution)/shard_map/ppermute | solution.py:346
  24.8 25.3 %copy-start = (bf16[1024,3,128]{2,0,1:T(8,128)(2,1)S(1)}, bf16[1024,3,128]{2,0,1:T(8,128)(2,1)}, u32[]{:S(2)}) copy-start(bf16[1024,3,128]{2,0,1:T(8,128)(2,1)} %param.22) | copy-start | bytes 2359300
  45.0 6.8 %collective-permute-start.4 = (bf16[256,256]{1,0:T(8,128)(2,1)S(1)}, bf16[256,256]{1,0:T(8,128)(2,1)S(1)}, u32[]{:S(2)}, u32[]{:S(2)}) collective-permute-start(bf16[256,256]{1,0:T(8,128)(2,1)S(1)} %unpack.1.x), channel_id=1, source_target_pairs={{0,3},{1,0},{2,1},{3,2},{4,7},{5,4},{6,5},{7,6},{8,11},{9,8},{10,9... | collective-permute-start | bytes 393224 | tf_op jit(solution)/shard_map/ppermute | solution.py:346
  47.8 7.6 %collective-permute-start.6 = (bf16[256,256]{1,0:T(8,128)(2,1)S(1)}, bf16[256,256]{1,0:T(8,128)(2,1)S(1)}, u32[]{:S(2)}, u32[]{:S(2)}) collective-permute-start(bf16[256,256]{1,0:T(8,128)(2,1)S(1)} %unpack.1.x), channel_id=1, source_target_pairs={{0,1},{1,2},{2,3},{3,0},{4,5},{5,6},{6,7},{7,4},{8,9},{9,10},{10,1... | collective-permute-start | bytes 393224 | tf_op jit(solution)/shard_map/ppermute | solution.py:346
  47.8 7.6 %collective-permute-start.5 = (bf16[256,256]{1,0:T(8,128)(2,1)S(1)}, bf16[256,256]{1,0:T(8,128)(2,1)S(1)}, u32[]{:S(2)}, u32[]{:S(2)}) collective-permute-start(bf16[256,256]{1,0:T(8,128)(2,1)S(1)} %unpack.1.x), channel_id=1, source_target_pairs={{0,2},{1,3},{2,0},{3,1},{4,6},{5,7},{6,4},{7,5},{8,10},{9,11},{10,... | collective-permute-start | bytes 393224 | tf_op jit(solution)/shard_map/ppermute | solution.py:346
  60.0 9.3 %collective-permute-start.9 = (bf16[1024,128]{1,0:T(8,128)(2,1)S(1)}, bf16[1024,128]{1,0:T(8,128)(2,1)S(1)}, u32[]{:S(2)}, u32[]{:S(2)}) collective-permute-start(bf16[1024,128]{1,0:T(8,128)(2,1)S(1)} %get-tuple-element.70.a0), channel_id=1, source_target_pairs={{0,1},{1,2},{2,3},{3,0},{4,5},{5,6},{6,7},{7,4},{8,9},{9,10},{10,1... | collective-permute-start | bytes 786440 | tf_op jit(solution)/shard_map/ppermute | solution.py:346
  60.1 12.0 %collective-permute-start.8 = (bf16[1024,128]{1,0:T(8,128)(2,1)S(1)}, bf16[1024,128]{1,0:T(8,128)(2,1)S(1)}, u32[]{:S(2)}, u32[]{:S(2)}) collective-permute-start(bf16[1024,128]{1,0:T(8,128)(2,1)S(1)} %get-tuple-element.70.a0), channel_id=1, source_target_pairs={{0,2},{1,3},{2,0},{3,1},{4,6},{5,7},{6,4},{7,5},{8,10},{9,11},{10,... | collective-permute-start | bytes 786440 | tf_op jit(solution)/shard_map/ppermute | solution.py:346
  63.7 8.9 %collective-permute-start.7 = (bf16[1024,128]{1,0:T(8,128)(2,1)S(1)}, bf16[1024,128]{1,0:T(8,128)(2,1)S(1)}, u32[]{:S(2)}, u32[]{:S(2)}) collective-permute-start(bf16[1024,128]{1,0:T(8,128)(2,1)S(1)} %get-tuple-element.70.a0), channel_id=1, source_target_pairs={{0,3},{1,0},{2,1},{3,2},{4,7},{5,4},{6,5},{7,6},{8,11},{9,8},{10,9... | collective-permute-start | bytes 786440 | tf_op jit(solution)/shard_map/ppermute | solution.py:346
  80.7 2.0 %collective-permute-start.10 = (bf16[8,4,16,512]{3,2,1,0:T(8,128)(2,1)S(1)}, bf16[8,4,16,512]{3,2,1,0:T(8,128)(2,1)S(1)}, u32[]{:S(2)}, u32[]{:S(2)}) collective-permute-start(bf16[8,4,16,512]{3,2,1,0:T(8,128)(2,1)S(1)} %get-tuple-element.91), channel_id=1, source_target_pairs={{0,4},{4,0},{1,5},{5,1},{2,6},{6,2},{3,7},{7,3},{8,12},{12,8},{9,1... | collective-permute-start | bytes 1572872 | tf_op jit(solution)/shard_map/ppermute | solution.py:476
  82.7 8.6 %collective-permute-start.11 = (bf16[8,16,512]{2,1,0:T(8,128)(2,1)S(1)}, bf16[8,16,512]{2,1,0:T(8,128)(2,1)S(1)}, u32[]{:S(2)}, u32[]{:S(2)}) collective-permute-start(bf16[8,16,512]{2,1,0:T(8,128)(2,1)S(1)} %get-tuple-element.93), channel_id=1, source_target_pairs={{0,8},{8,16},{16,24},{24,0},{1,9},{9,17},{17,25},{25,1},{2,10},{10... | collective-permute-start | bytes 393224 | tf_op jit(solution)/shard_map/ppermute | solution.py:487
  85.5 7.9 %collective-permute-start.12 = (bf16[8,16,512]{2,1,0:T(8,128)(2,1)S(1)}, bf16[8,16,512]{2,1,0:T(8,128)(2,1)S(1)}, u32[]{:S(2)}, u32[]{:S(2)}) collective-permute-start(bf16[8,16,512]{2,1,0:T(8,128)(2,1)S(1)} %get-tuple-element.94), channel_id=1, source_target_pairs={{0,16},{8,24},{16,0},{24,8},{1,17},{9,25},{17,1},{25,9},{2,18},{10... | collective-permute-start | bytes 393224 | tf_op jit(solution)/shard_map/ppermute | solution.py:487
  86.1 8.1 %collective-permute-start.13 = (bf16[8,16,512]{2,1,0:T(8,128)(2,1)S(1)}, bf16[8,16,512]{2,1,0:T(8,128)(2,1)S(1)}, u32[]{:S(2)}, u32[]{:S(2)}) collective-permute-start(bf16[8,16,512]{2,1,0:T(8,128)(2,1)S(1)} %get-tuple-element.95), channel_id=1, source_target_pairs={{0,24},{8,0},{16,8},{24,16},{1,25},{9,1},{17,9},{25,17},{2,26},{10... | collective-permute-start | bytes 393224 | tf_op jit(solution)/shard_map/ppermute | solution.py:487
  94.9 12.5 %all-to-all-start.1 = ((bf16[8,16,512]{2,1,0:T(8,128)(2,1)}), bf16[8,16,512]{2,1,0:T(8,128)(2,1)S(1)}, u32[]{:S(2)}, u32[]{:S(2)}) async-start(bf16[8,16,512]{2,1,0:T(8,128)(2,1)} %line.1), calls=%async_computation.1 | async-start | bytes 262144 | tf_op jit(solution)/shard_map/all_to_all | solution.py:497
  (4 other events, 55.3 us)

commit v6 on v5

--- a/solution.py
+++ b/solution.py
@@ -12,6 +12,7 @@
 BLOCK = 128
 MEL = 100
 SLOT = 56
+PAIR = 104
 ALL = 60
 EPS = 1e-06
 VMEM, SMEM = pltpu.VMEM, pltpu.SMEM
@@ -70,43 +71,54 @@
     count = jnp.int32(0)
     for u in range(4):
         count += 2 * utt[0, u] * (jnp.minimum(start[0, u] + size[0, u], 64) - start[0, u])
-    lane = lax.broadcasted_iota(jnp.int32, (SLOT - 50, 128), 1)
+    lane = lax.broadcasted_iota(jnp.int32, (SLOT - 52, 128), 1)
     tail = jnp.where(lane == 0, count >> 5, jnp.where(lane == 1, count & 31, 0)).astype(F32)
     for b in range(8):
-        buf[b * SLOT + 50 : (b + 1) * SLOT, :] = tail
+        buf[b * SLOT + 50 : b * SLOT + 52, :] = buf[b * SLOT + 48 : b * SLOT + 50, :]
+        buf[b * SLOT + 52 : (b + 1) * SLOT, :] = tail
         out[b] = buf[b * SLOT : (b + 1) * SLOT, :].astype(BF16)
 
 
-def pack_kernel(bins, own, other, out, ends, tails, sem, sems):
+def pack_kernel(bins, own, other, out, ends, wide, tails, sem, sems):
     here = device()
     fetch([(ref.at[:, 48:SLOT, :], ends.at[half]) for half, ref in ((0, own), (1, other))], sem)()
-    for half in range(2):
-        tails[:, half] = jnp.broadcast_to(ends[half, 0][None], (out.shape[0], SLOT - 48, 128))
+    row = lax.broadcasted_iota(jnp.int32, (8, 128), 0)
+    counts = jnp.where(row == 4, ends[0, 0].astype(F32), ends[1, 0].astype(F32))
+    wide[...] = jnp.broadcast_to(counts[None], wide.shape)
     sends = []
     for half, ref in ((0, own), (1, other)):
         for i in range(8):
             b = bins[(here ^ half) * 8 + i]
             copy = pltpu.make_async_copy(
-                ref.at[i, 0:48, :], out.at[b >> 1, half, 0:48, :], sems.at[half * 8 + i]
+                ref.at[i, 0:48, :], out.at[b >> 1, half * 48 : half * 48 + 48, :], sems.at[half * 8 + i]
             )
             sends.append(((b & 1) == (here & 1), copy))
 
             @pl.when(sends[-1][0])
             def _():
                 copy.start()
-                tails[b >> 1, half] = ends[half, i]
-
-    last = pltpu.make_async_copy(tails, out.at[:, :, 48:SLOT, :], sems.at[16])
+                mine = (row >> 1) == half
+                wide[b >> 1] = jnp.where(mine, ends[half, i].astype(F32), wide[b >> 1])
+
+    tails[...] = wide[...].astype(BF16)
+    last = pltpu.make_async_copy(tails, out.at[:, 96:PAIR, :], sems.at[16])
     last.start()
     for chosen, copy in sends:
         pl.when(chosen)(copy.wait)
     last.wait()
 
 
-def unpack_kernel(source, arrived, out, slots, wide, rows, sems):
-    fetch([(arrived.at[source[j]], slots.at[j]) for j in range(8)], sems)()
+def unpack_kernel(source, arrived, out, slots, ends, wide, rows, sems):
+    pairs = []
     for j in range(8):
-        wide[j * SLOT : (j + 1) * SLOT, :] = slots[j].astype(F32)
+        chip, half = source[j] >> 1, source[j] & 1
+        body = arrived.at[chip, pl.ds(pl.multiple_of(half * 48, 16), 48), :]
+        pairs += [(body, slots.at[j, 0:48, :]), (arrived.at[chip, 96:PAIR, :], ends.at[j])]
+    fetch(pairs, sems)()
+    for j in range(8):
+        wide[j * SLOT : j * SLOT + 48, :] = slots[j].astype(F32)
+        end = ends[j].astype(F32)
+        wide[j * SLOT + 48 : j * SLOT + 50, :] = jnp.where((source[j] & 1) == 0, end[0:2], end[2:4])
     lane = lax.broadcasted_iota(jnp.int32, (8, 128), 1)
     for a in range(2):
         lines = [wide[pl.ds(a * 25 + r, 8, stride=SLOT), :] for r in range(25)]
@@ -360,11 +372,11 @@
     bins = destination // 8
     packed = pl.pallas_call(
         pack_kernel,
-        out_shape=jax.ShapeDtypeStruct((32, 2, SLOT, 128), BF16),
+        out_shape=jax.ShapeDtypeStruct((32, PAIR, 128), BF16),
         in_specs=[sm(), hb(), hb()],
         out_specs=hb(),
         scratch_shapes=[
-            VMEM((2, 8, SLOT - 48, 128), BF16), VMEM((32, 2, SLOT - 48, 128), BF16),
+            VMEM((2, 8, 8, 128), BF16), VMEM((32, 8, 128), F32), VMEM((32, 8, 128), BF16),
             pltpu.SemaphoreType.DMA((2,)), pltpu.SemaphoreType.DMA((17,)),
         ],
         compiler_params=params(8),
@@ -382,7 +394,7 @@
     wqkv = qkv_weight.transpose(1, 0, 2)
     vel = jnp.pad(vel_weight, ((0, 0), (0, 28)))
     proj = jnp.concatenate([out_proj] + [turned(out_proj, by) for by in (1, 2, 3)], axis=0)
-    arrived = lax.all_to_all(packed, ("z", "y"), 0, 0, tiled=True).reshape(64, SLOT, 128)
+    arrived = lax.all_to_all(packed, ("z", "y"), 0, 0, tiled=True)
     wanted = here * 8 + jnp.arange(8, dtype=jnp.int32)
     row = jnp.sum(
         jnp.where(destination[None, :] == wanted[:, None], jnp.arange(512, dtype=jnp.int32)[None, :], 0), axis=1
@@ -397,13 +409,13 @@
         in_specs=[sm(), hb()],
         out_specs=vm(),
         scratch_shapes=[
-            VMEM((8, SLOT, 128), BF16), VMEM((8 * SLOT, 128), F32), VMEM((256, 128), F32),
-            pltpu.SemaphoreType.DMA((8,)),
+            VMEM((8, 48, 128), BF16), VMEM((8, 8, 128), BF16), VMEM((8 * SLOT, 128), F32),
+            VMEM((256, 128), F32), pltpu.SemaphoreType.DMA((16,)),
         ],
         compiler_params=params(8),
         name="unpack",
     )(source, arrived)
-    counts = jnp.sum(arrived[:, 50, 0:2].astype(F32), axis=0)
+    counts = jnp.sum(arrived[:, 100:102, 0:2].astype(F32), axis=(0, 1))
     count = counts[0] * 32.0 + counts[1]
     pieces = [frames] + [turned(frames, by) for by in (1, 2, 3)]
 

time: 108 us -> 107 us (level)
  waiting for transfers between devices: 42 us -> 40.8 us
    all_to_all x1, waiting for transfers between devices: 8.08 us -> 6.67 us  [shards(): arrived = lax.all_to_all(packed, ('z', 'y'), 0, 0, tiled=True)]
where the time goes in v6:
time: 107 us
  waiting for transfers between devices  40.8 us (38%)
  starting transfers between devices  36.1 us (34%)
  Pallas kernels  23.5 us (22%)
  other arithmetic  2.41 us (2%)
  between operations  2.27 us (2%)
  local copies, waits for them, and re-layouts  1.83 us (2%)
    ppermute x9, waiting for transfers between devices, turned(): return lax.ppermute(a, 'mp', [(i, (i - by) % 4) for i in range(4)])  18.7 us
    ppermute x9, starting transfers between devices, turned(): return lax.ppermute(a, 'mp', [(i, (i - by) % 4) for i in range(4)])  14.9 us
    all_to_all x1, starting transfers between devices, shards(): arrived = lax.all_to_all(packed, ('z', 'y'), 0, 0, tiled=True)  11.8 us
    pallas_call x1, Pallas kernels, shards(): pl.pallas_call(back_kernel, out_shape=tuple((jax.ShapeDtypeStruct((8, 4,...  8.07 us
    all_to_all x1, waiting for transfers between devices, shards(): parts = lax.all_to_all(line, 'z', 0, 0, tiled=True)  7.14 us
    all_to_all x1, waiting for transfers between devices, shards(): arrived = lax.all_to_all(packed, ('z', 'y'), 0, 0, tiled=True)  6.67 us
    ppermute x3, starting transfers between devices, shards(): lax.ppermute(a, 'y', [(i, (i + by) % 4) for i in range(4)])  5.78 us
    ppermute x3, waiting for transfers between devices, shards(): lax.ppermute(a, 'y', [(i, (i + by) % 4) for i in range(4)])  5.53 us
  transfers between devices with their start and end apart: 16, of which 14 were waited for; matrix products, arithmetic and copies ran while one was open for 3% of the time, Pallas kernels for 5%

profile of v6, /device:TPU:8, one launch (start us, length us, event | category | flops | bytes accessed | tf_op | source)
XLA Modules:
  0.0 107.0 jit_solution(15507686951718684966)
XLA Ops:
  0.7 1.6 %share.1.own = bf16[8,56,128]{2,1,0:T(8,128)(2,1)} custom-call(s32[1,4]{1,0:T(1,128)} %utt_hbm.1, s32[1,4]{1,0:T(1,128)} %start_hbm.1, s32[1,4]{1,0:T(1,128)} %size_hbm.1, bf16[8,12800]{1,0:T(8,128)(2,1)} %noise.1, bf16[8,12800]{1,0:T(8,128)(2,1)} %data.1), custom_call_target="tpu_custom_call" | custom-call | tf_op jit(solution)/shard_map/share/pallas_call | solution.py:361
  4.9 1.6 %pack.1 = bf16[32,104,128]{2,1,0:T(8,128)(2,1)} custom-call(s32[512]{0:T(512)S(1)} %add_select_fusion.bins, bf16[8,56,128]{2,1,0:T(8,128)(2,1)S(1)} %copy-done.1, bf16[8,56,128]{2,1,0:T(8,128)(2,1)S(1)} %collective-permute-done.other), custom_call_target="tpu_custom_call" | custom-call | tf_op jit(solution)/shard_map/pack/pallas_call | solution.py:373
  6.5 11.8 %all-to-all-start = ((bf16[32,104,128]{2,1,0:T(8,128)(2,1)}), bf16[32,104,128]{2,1,0:T(8,128)(2,1)S(1)}, u32[]{:S(2)}, u32[]{:S(2)}) async-start(bf16[32,104,128]{2,1,0:T(8,128)(2,1)} %pack.1), calls=%async_computation | async-start | bytes 1703936 | tf_op jit(solution)/shard_map/all_to_all | solution.py:397
  18.5 1.6 %collective-permute-start.3 = (bf16[128,1024]{1,0:T(8,128)(2,1)}, bf16[128,1024]{1,0:T(8,128)(2,1)}, u32[]{:S(2)}, u32[]{:S(2)}) collective-permute-start(bf16[128,1024]{1,0:T(8,128)(2,1)} %param.23), channel_id=1, source_target_pairs={{0,1},{1,2},{2,3},{3,0},{4,5},{5,6},{6,7},{7,4},{8,9},{9,10},{10,1... | collective-permute-start | bytes 786440 | tf_op jit(solution)/shard_map/ppermute | solution.py:358
  20.1 2.7 %collective-permute-start.2 = (bf16[128,1024]{1,0:T(8,128)(2,1)}, bf16[128,1024]{1,0:T(8,128)(2,1)}, u32[]{:S(2)}, u32[]{:S(2)}) collective-permute-start(bf16[128,1024]{1,0:T(8,128)(2,1)} %param.23), channel_id=1, source_target_pairs={{0,2},{1,3},{2,0},{3,1},{4,6},{5,7},{6,4},{7,5},{8,10},{9,11},{10,... | collective-permute-start | bytes 786440 | tf_op jit(solution)/shard_map/ppermute | solution.py:358
  22.8 1.4 %collective-permute-start.1 = (bf16[128,1024]{1,0:T(8,128)(2,1)}, bf16[128,1024]{1,0:T(8,128)(2,1)}, u32[]{:S(2)}, u32[]{:S(2)}) collective-permute-start(bf16[128,1024]{1,0:T(8,128)(2,1)} %param.23), channel_id=1, source_target_pairs={{0,3},{1,0},{2,1},{3,2},{4,7},{5,4},{6,5},{7,6},{8,11},{9,8},{10,9... | collective-permute-start | bytes 786440 | tf_op jit(solution)/shard_map/ppermute | solution.py:358
  24.9 3.5 %collective-permute-done.3 = bf16[128,1024]{1,0:T(8,128)(2,1)} collective-permute-done((bf16[128,1024]{1,0:T(8,128)(2,1)}, bf16[128,1024]{1,0:T(8,128)(2,1)}, u32[]{:S(2)}, u32[]{:S(2)}) %collective-permute-start.3) | collective-permute-done | bytes 262176 | tf_op jit(solution)/shard_map/ppermute | solution.py:358
  28.4 6.2 %collective-permute-done.2 = bf16[128,1024]{1,0:T(8,128)(2,1)} collective-permute-done((bf16[128,1024]{1,0:T(8,128)(2,1)}, bf16[128,1024]{1,0:T(8,128)(2,1)}, u32[]{:S(2)}, u32[]{:S(2)}) %collective-permute-start.2) | collective-permute-done | bytes 262176 | tf_op jit(solution)/shard_map/ppermute | solution.py:358
  35.8 6.7 %all-to-all-done.arrived = bf16[32,104,128]{2,1,0:T(8,128)(2,1)S(1)} async-done(((bf16[32,104,128]{2,1,0:T(8,128)(2,1)}), bf16[32,104,128]{2,1,0:T(8,128)(2,1)S(1)}, u32[]{:S(2)}, u32[]{:S(2)}) %all-to-all-start) | async-done | bytes 852000 | tf_op jit(solution)/shard_map/all_to_all | solution.py:397
  43.7 2.8 %collective-permute-start.4 = (bf16[256,256]{1,0:T(8,128)(2,1)S(1)}, bf16[256,256]{1,0:T(8,128)(2,1)S(1)}, u32[]{:S(2)}, u32[]{:S(2)}) collective-permute-start(bf16[256,256]{1,0:T(8,128)(2,1)S(1)} %unpack.1.x), channel_id=1, source_target_pairs={{0,3},{1,0},{2,1},{3,2},{4,7},{5,4},{6,5},{7,6},{8,11},{9,8},{10,9... | collective-permute-start | bytes 393224 | tf_op jit(solution)/shard_map/ppermute | solution.py:358
  46.5 2.3 %collective-permute-start.5 = (bf16[256,256]{1,0:T(8,128)(2,1)S(1)}, bf16[256,256]{1,0:T(8,128)(2,1)S(1)}, u32[]{:S(2)}, u32[]{:S(2)}) collective-permute-start(bf16[256,256]{1,0:T(8,128)(2,1)S(1)} %unpack.1.x), channel_id=1, source_target_pairs={{0,2},{1,3},{2,0},{3,1},{4,6},{5,7},{6,4},{7,5},{8,10},{9,11},{10,... | collective-permute-start | bytes 393224 | tf_op jit(solution)/shard_map/ppermute | solution.py:358
  51.8 2.2 %collective-permute-done.6.x3 = bf16[256,256]{1,0:T(8,128)(2,1)S(1)} collective-permute-done((bf16[256,256]{1,0:T(8,128)(2,1)S(1)}, bf16[256,256]{1,0:T(8,128)(2,1)S(1)}, u32[]{:S(2)}, u32[]{:S(2)}) %collective-permute-start.6) | collective-permute-done | bytes 131104 | tf_op jit(solution)/shard_map/ppermute | solution.py:358
  54.1 4.6 %front.1 = (bf16[1024,128]{1,0:T(8,128)(2,1)S(1)}, bf16[128,1024]{1,0:T(8,128)(2,1)S(1)}, bf16[1024,128]{1,0:T(8,128)(2,1)S(1)}, bf16[1024,128]{1,0:T(8,128)(2,1...) custom-call(s32[1,16]{1,0:T(1,128)S(1)} %pad_add_fusion.table, ...), custom_call_target="tpu_custom_call" | custom-call | tf_op jit(solution)/shard_map/front/pallas_call | solution.py:442
  58.9 3.6 %collective-permute-start.8 = (bf16[1024,128]{1,0:T(8,128)(2,1)S(1)}, bf16[1024,128]{1,0:T(8,128)(2,1)S(1)}, u32[]{:S(2)}, u32[]{:S(2)}) collective-permute-start(bf16[1024,128]{1,0:T(8,128)(2,1)S(1)} %get-tuple-element.70.a0), channel_id=1, source_target_pairs={{0,2},{1,3},{2,0},{3,1},{4,6},{5,7},{6,4},{7,5},{8,10},{9,11},{10,... | collective-permute-start | bytes 786440 | tf_op jit(solution)/shard_map/ppermute | solution.py:358
  64.0 4.3 %collective-permute-done.9.a3 = bf16[1024,128]{1,0:T(8,128)(2,1)S(1)} collective-permute-done((bf16[1024,128]{1,0:T(8,128)(2,1)S(1)}, bf16[1024,128]{1,0:T(8,128)(2,1)S(1)}, u32[]{:S(2)}, u32[]{:S(2)}) %collective-permute-start.9) | collective-permute-done | bytes 262176 | tf_op jit(solution)/shard_map/ppermute | solution.py:358
  69.2 1.9 %collective-permute-done.8.a2 = bf16[1024,128]{1,0:T(8,128)(2,1)S(1)} collective-permute-done((bf16[1024,128]{1,0:T(8,128)(2,1)S(1)}, bf16[1024,128]{1,0:T(8,128)(2,1)S(1)}, u32[]{:S(2)}, u32[]{:S(2)}) %collective-permute-start.8) | collective-permute-done | bytes 262176 | tf_op jit(solution)/shard_map/ppermute | solution.py:358
  71.6 8.1 %back.1 = (f32[8,4,16,512]{3,2,1,0:T(8,128)S(1)}, bf16[8,4,16,512]{3,2,1,0:T(8,128)(2,1)S(1)}) custom-call(s32[1,16]{1,0:T(1,128)S(1)} %pad_add_fusion.table, bf16[128,1024]{1,0:T(8,128)(2,1)S(1)} %get-tuple-element.69.attt, bf16[1024,128]{1,0:T(8,128)(2,1)S(1)} %collective-permute-done.7.a1, bf16[1024,128]{1,0:T(8,128)(2,1)S(1)} %collective-permute-done.8.a2, ...), custom_call_target="tpu_custom_call" | custom-call | tf_op jit(solution)/shard_map/back/pallas_call | solution.py:475
  79.8 1.9 %collective-permute-done.10.got = bf16[8,4,16,512]{3,2,1,0:T(8,128)(2,1)S(1)} collective-permute-done((bf16[8,4,16,512]{3,2,1,0:T(8,128)(2,1)S(1)}, bf16[8,4,16,512]{3,2,1,0:T(8,128)(2,1)S(1)}, u32[]{:S(2)}, u32[]{:S(2)}) %collective-permute-start.10) | collective-permute-done | bytes 524320 | tf_op jit(solution)/shard_map/ppermute | solution.py:488
  81.7 2.6 %collective-permute-start.11 = (bf16[8,16,512]{2,1,0:T(8,128)(2,1)S(1)}, bf16[8,16,512]{2,1,0:T(8,128)(2,1)S(1)}, u32[]{:S(2)}, u32[]{:S(2)}) collective-permute-start(bf16[8,16,512]{2,1,0:T(8,128)(2,1)S(1)} %get-tuple-element.93), channel_id=1, source_target_pairs={{0,8},{8,16},{16,24},{24,0},{1,9},{9,17},{17,25},{25,1},{2,10},{10... | collective-permute-start | bytes 393224 | tf_op jit(solution)/shard_map/ppermute | solution.py:499
  85.0 2.5 %collective-permute-start.13 = (bf16[8,16,512]{2,1,0:T(8,128)(2,1)S(1)}, bf16[8,16,512]{2,1,0:T(8,128)(2,1)S(1)}, u32[]{:S(2)}, u32[]{:S(2)}) collective-permute-start(bf16[8,16,512]{2,1,0:T(8,128)(2,1)S(1)} %get-tuple-element.95), channel_id=1, source_target_pairs={{0,24},{8,0},{16,8},{24,16},{1,25},{9,1},{17,9},{25,17},{2,26},{10... | collective-permute-start | bytes 393224 | tf_op jit(solution)/shard_map/ppermute | solution.py:499
  87.5 2.7 %collective-permute-done.11.r1 = bf16[8,16,512]{2,1,0:T(8,128)(2,1)S(1)} collective-permute-done((bf16[8,16,512]{2,1,0:T(8,128)(2,1)S(1)}, bf16[8,16,512]{2,1,0:T(8,128)(2,1)S(1)}, u32[]{:S(2)}, u32[]{:S(2)}) %collective-permute-start.11) | collective-permute-done | bytes 131104 | tf_op jit(solution)/shard_map/ppermute | solution.py:499
  90.2 2.0 %collective-permute-done.12.r2 = bf16[8,16,512]{2,1,0:T(8,128)(2,1)S(1)} collective-permute-done((bf16[8,16,512]{2,1,0:T(8,128)(2,1)S(1)}, bf16[8,16,512]{2,1,0:T(8,128)(2,1)S(1)}, u32[]{:S(2)}, u32[]{:S(2)}) %collective-permute-start.12) | collective-permute-done | bytes 131104 | tf_op jit(solution)/shard_map/ppermute | solution.py:499
  93.8 3.4 %all-to-all-start.1 = ((bf16[8,16,512]{2,1,0:T(8,128)(2,1)}), bf16[8,16,512]{2,1,0:T(8,128)(2,1)S(1)}, u32[]{:S(2)}, u32[]{:S(2)}) async-start(bf16[8,16,512]{2,1,0:T(8,128)(2,1)} %line.1), calls=%async_computation.1 | async-start | bytes 262144 | tf_op jit(solution)/shard_map/all_to_all | solution.py:509
  99.1 7.1 %all-to-all-done.1.parts = bf16[8,16,512]{2,1,0:T(8,128)(2,1)S(1)} async-done(((bf16[8,16,512]{2,1,0:T(8,128)(2,1)}), bf16[8,16,512]{2,1,0:T(8,128)(2,1)S(1)}, u32[]{:S(2)}, u32[]{:S(2)}) %all-to-all-start.1) | async-done | bytes 131104 | tf_op jit(solution)/shard_map/all_to_all | solution.py:509
  (59 shorter events, 15.6 us)
Async XLA Ops:
  0.6 23.7 %copy-start.10 = (pred[128]{0:T(512)(128)(4,1)S(1)}, pred[128]{0:T(512)(128)(4,1)}, u32[]{:S(2)}) copy-start(pred[128]{0:T(512)(128)(4,1)} %constant.46.clone.1) | copy-start | bytes 388
  0.7 23.8 %copy-start.9 = (bf16[1024]{0:T(1024)(128)(2,1)S(1)}, bf16[1024]{0:T(1024)(128)(2,1)}, u32[]{:S(2)}) copy-start(bf16[1024]{0:T(1024)(128)(2,1)} %param.24) | copy-start | bytes 6148
  0.7 23.8 %copy-start.8 = (bf16[1024]{0:T(1024)(128)(2,1)S(1)}, bf16[1024]{0:T(1024)(128)(2,1)}, u32[]{:S(2)}) copy-start(bf16[1024]{0:T(1024)(128)(2,1)} %param.21) | copy-start | bytes 6148
  0.7 23.6 %copy-start.2 = (bf16[200,1024]{1,0:T(8,128)(2,1)S(1)}, bf16[200,1024]{1,0:T(8,128)(2,1)}, u32[]{:S(2)}) copy-start(bf16[200,1024]{1,0:T(8,128)(2,1)} %param.20) | copy-start | bytes 1228804
  2.3 1.6 %collective-permute-start = (bf16[8,56,128]{2,1,0:T(8,128)(2,1)}, bf16[8,56,128]{2,1,0:T(8,128)(2,1)S(1)}, u32[]{:S(2)}, u32[]{:S(2)}) collective-permute-start(bf16[8,56,128]{2,1,0:T(8,128)(2,1)} %share.1.own), channel_id=1, source_target_pairs={{0,4},{4,0},{1,5},{5,1},{2,6},{6,2},{3,7},{7,3},{8,12},{12,8},{9,1... | collective-permute-start | bytes 344072 | tf_op jit(solution)/shard_map/ppermute | solution.py:371
  4.8 19.6 %copy-start.3 = (bf16[1024,100]{0,1:T(8,128)(2,1)S(1)}, bf16[1024,100]{0,1:T(8,128)(2,1)}, u32[]{:S(2)}) copy-start(bf16[1024,100]{0,1:T(8,128)(2,1)} %param.25) | copy-start | bytes 614404
  6.4 18.3 %copy-start.5 = (s32[1,4]{1,0:T(1,128)S(1)}, s32[1,4]{1,0:T(1,128)}, u32[]{:S(2)}) copy-start(s32[1,4]{1,0:T(1,128)} %utt_hbm.1) | copy-start | bytes 52
  6.4 18.3 %copy-start.6 = (s32[1,4]{1,0:T(1,128)S(1)}, s32[1,4]{1,0:T(1,128)}, u32[]{:S(2)}) copy-start(s32[1,4]{1,0:T(1,128)} %start_hbm.1) | copy-start | bytes 52
  6.5 36.0 %all-to-all-start = ((bf16[32,104,128]{2,1,0:T(8,128)(2,1)}), bf16[32,104,128]{2,1,0:T(8,128)(2,1)S(1)}, u32[]{:S(2)}, u32[]{:S(2)}) async-start(bf16[32,104,128]{2,1,0:T(8,128)(2,1)} %pack.1), calls=%async_computation | async-start | bytes 1703936 | tf_op jit(solution)/shard_map/all_to_all | solution.py:397
  18.5 9.8 %collective-permute-start.3 = (bf16[128,1024]{1,0:T(8,128)(2,1)}, bf16[128,1024]{1,0:T(8,128)(2,1)}, u32[]{:S(2)}, u32[]{:S(2)}) collective-permute-start(bf16[128,1024]{1,0:T(8,128)(2,1)} %param.23), channel_id=1, source_target_pairs={{0,1},{1,2},{2,3},{3,0},{4,5},{5,6},{6,7},{7,4},{8,9},{9,10},{10,1... | collective-permute-start | bytes 786440 | tf_op jit(solution)/shard_map/ppermute | solution.py:358
  20.1 14.4 %collective-permute-start.2 = (bf16[128,1024]{1,0:T(8,128)(2,1)}, bf16[128,1024]{1,0:T(8,128)(2,1)}, u32[]{:S(2)}, u32[]{:S(2)}) collective-permute-start(bf16[128,1024]{1,0:T(8,128)(2,1)} %param.23), channel_id=1, source_target_pairs={{0,2},{1,3},{2,0},{3,1},{4,6},{5,7},{6,4},{7,5},{8,10},{9,11},{10,... | collective-permute-start | bytes 786440 | tf_op jit(solution)/shard_map/ppermute | solution.py:358
  22.8 11.7 %collective-permute-start.1 = (bf16[128,1024]{1,0:T(8,128)(2,1)}, bf16[128,1024]{1,0:T(8,128)(2,1)}, u32[]{:S(2)}, u32[]{:S(2)}) collective-permute-start(bf16[128,1024]{1,0:T(8,128)(2,1)} %param.23), channel_id=1, source_target_pairs={{0,3},{1,0},{2,1},{3,2},{4,7},{5,4},{6,5},{7,6},{8,11},{9,8},{10,9... | collective-permute-start | bytes 786440 | tf_op jit(solution)/shard_map/ppermute | solution.py:358
  24.8 24.0 %copy-start = (bf16[1024,3,128]{2,0,1:T(8,128)(2,1)S(1)}, bf16[1024,3,128]{2,0,1:T(8,128)(2,1)}, u32[]{:S(2)}) copy-start(bf16[1024,3,128]{2,0,1:T(8,128)(2,1)} %param.22) | copy-start | bytes 2359300
  43.7 6.8 %collective-permute-start.4 = (bf16[256,256]{1,0:T(8,128)(2,1)S(1)}, bf16[256,256]{1,0:T(8,128)(2,1)S(1)}, u32[]{:S(2)}, u32[]{:S(2)}) collective-permute-start(bf16[256,256]{1,0:T(8,128)(2,1)S(1)} %unpack.1.x), channel_id=1, source_target_pairs={{0,3},{1,0},{2,1},{3,2},{4,7},{5,4},{6,5},{7,6},{8,11},{9,8},{10,9... | collective-permute-start | bytes 393224 | tf_op jit(solution)/shard_map/ppermute | solution.py:358
  46.5 7.6 %collective-permute-start.6 = (bf16[256,256]{1,0:T(8,128)(2,1)S(1)}, bf16[256,256]{1,0:T(8,128)(2,1)S(1)}, u32[]{:S(2)}, u32[]{:S(2)}) collective-permute-start(bf16[256,256]{1,0:T(8,128)(2,1)S(1)} %unpack.1.x), channel_id=1, source_target_pairs={{0,1},{1,2},{2,3},{3,0},{4,5},{5,6},{6,7},{7,4},{8,9},{9,10},{10,1... | collective-permute-start | bytes 393224 | tf_op jit(solution)/shard_map/ppermute | solution.py:358
  46.5 7.6 %collective-permute-start.5 = (bf16[256,256]{1,0:T(8,128)(2,1)S(1)}, bf16[256,256]{1,0:T(8,128)(2,1)S(1)}, u32[]{:S(2)}, u32[]{:S(2)}) collective-permute-start(bf16[256,256]{1,0:T(8,128)(2,1)S(1)} %unpack.1.x), channel_id=1, source_target_pairs={{0,2},{1,3},{2,0},{3,1},{4,6},{5,7},{6,4},{7,5},{8,10},{9,11},{10,... | collective-permute-start | bytes 393224 | tf_op jit(solution)/shard_map/ppermute | solution.py:358
  58.7 9.6 %collective-permute-start.9 = (bf16[1024,128]{1,0:T(8,128)(2,1)S(1)}, bf16[1024,128]{1,0:T(8,128)(2,1)S(1)}, u32[]{:S(2)}, u32[]{:S(2)}) collective-permute-start(bf16[1024,128]{1,0:T(8,128)(2,1)S(1)} %get-tuple-element.70.a0), channel_id=1, source_target_pairs={{0,1},{1,2},{2,3},{3,0},{4,5},{5,6},{6,7},{7,4},{8,9},{9,10},{10,1... | collective-permute-start | bytes 786440 | tf_op jit(solution)/shard_map/ppermute | solution.py:358
  58.9 12.2 %collective-permute-start.8 = (bf16[1024,128]{1,0:T(8,128)(2,1)S(1)}, bf16[1024,128]{1,0:T(8,128)(2,1)S(1)}, u32[]{:S(2)}, u32[]{:S(2)}) collective-permute-start(bf16[1024,128]{1,0:T(8,128)(2,1)S(1)} %get-tuple-element.70.a0), channel_id=1, source_target_pairs={{0,2},{1,3},{2,0},{3,1},{4,6},{5,7},{6,4},{7,5},{8,10},{9,11},{10,... | collective-permute-start | bytes 786440 | tf_op jit(solution)/shard_map/ppermute | solution.py:358
  62.5 9.1 %collective-permute-start.7 = (bf16[1024,128]{1,0:T(8,128)(2,1)S(1)}, bf16[1024,128]{1,0:T(8,128)(2,1)S(1)}, u32[]{:S(2)}, u32[]{:S(2)}) collective-permute-start(bf16[1024,128]{1,0:T(8,128)(2,1)S(1)} %get-tuple-element.70.a0), channel_id=1, source_target_pairs={{0,3},{1,0},{2,1},{3,2},{4,7},{5,4},{6,5},{7,6},{8,11},{9,8},{10,9... | collective-permute-start | bytes 786440 | tf_op jit(solution)/shard_map/ppermute | solution.py:358
  79.7 2.0 %collective-permute-start.10 = (bf16[8,4,16,512]{3,2,1,0:T(8,128)(2,1)S(1)}, bf16[8,4,16,512]{3,2,1,0:T(8,128)(2,1)S(1)}, u32[]{:S(2)}, u32[]{:S(2)}) collective-permute-start(bf16[8,4,16,512]{3,2,1,0:T(8,128)(2,1)S(1)} %get-tuple-element.91), channel_id=1, source_target_pairs={{0,4},{4,0},{1,5},{5,1},{2,6},{6,2},{3,7},{7,3},{8,12},{12,8},{9,1... | collective-permute-start | bytes 1572872 | tf_op jit(solution)/shard_map/ppermute | solution.py:488
  81.7 8.5 %collective-permute-start.11 = (bf16[8,16,512]{2,1,0:T(8,128)(2,1)S(1)}, bf16[8,16,512]{2,1,0:T(8,128)(2,1)S(1)}, u32[]{:S(2)}, u32[]{:S(2)}) collective-permute-start(bf16[8,16,512]{2,1,0:T(8,128)(2,1)S(1)} %get-tuple-element.93), channel_id=1, source_target_pairs={{0,8},{8,16},{16,24},{24,0},{1,9},{9,17},{17,25},{25,1},{2,10},{10... | collective-permute-start | bytes 393224 | tf_op jit(solution)/shard_map/ppermute | solution.py:499
  84.3 7.9 %collective-permute-start.12 = (bf16[8,16,512]{2,1,0:T(8,128)(2,1)S(1)}, bf16[8,16,512]{2,1,0:T(8,128)(2,1)S(1)}, u32[]{:S(2)}, u32[]{:S(2)}) collective-permute-start(bf16[8,16,512]{2,1,0:T(8,128)(2,1)S(1)} %get-tuple-element.94), channel_id=1, source_target_pairs={{0,16},{8,24},{16,0},{24,8},{1,17},{9,25},{17,1},{25,9},{2,18},{10... | collective-permute-start | bytes 393224 | tf_op jit(solution)/shard_map/ppermute | solution.py:499
  85.0 8.1 %collective-permute-start.13 = (bf16[8,16,512]{2,1,0:T(8,128)(2,1)S(1)}, bf16[8,16,512]{2,1,0:T(8,128)(2,1)S(1)}, u32[]{:S(2)}, u32[]{:S(2)}) collective-permute-start(bf16[8,16,512]{2,1,0:T(8,128)(2,1)S(1)} %get-tuple-element.95), channel_id=1, source_target_pairs={{0,24},{8,0},{16,8},{24,16},{1,25},{9,1},{17,9},{25,17},{2,26},{10... | collective-permute-start | bytes 393224 | tf_op jit(solution)/shard_map/ppermute | solution.py:499
  93.8 12.5 %all-to-all-start.1 = ((bf16[8,16,512]{2,1,0:T(8,128)(2,1)}), bf16[8,16,512]{2,1,0:T(8,128)(2,1)S(1)}, u32[]{:S(2)}, u32[]{:S(2)}) async-start(bf16[8,16,512]{2,1,0:T(8,128)(2,1)} %line.1), calls=%async_computation.1 | async-start | bytes 262144 | tf_op jit(solution)/shard_map/all_to_all | solution.py:509
  (4 other events, 55.2 us)
